TPU v7x, 32 devices: a whole 2x2x4 slice. The times are simulated.
32 devices in a mesh: dp: 2 (over y), row: 4 (over x, core), col: 4 (over z).
Axes of the slice: x: 2, y: 2, z: 4, core: 2. Of those that a mesh axis runs over, the one named last changes fastest.
Arguments:
- tokens: bfloat16 [8192, 1024], P(('dp', 'col'), 'row'), may hold values from -6 to 6
- encoder: bfloat16 [8192, 1024], P(('dp', 'col'), 'row'), may hold values from -6 to 6
- cotangent: bfloat16 [8192, 1024], P(('dp', 'col'), 'row'), may hold values from -6 to 6
- prefixes: int32 [2], P('dp'), may hold values from 409 to 2048
- selfqkv: bfloat16 [1024, 3, 1024], P('row', None, 'col'), may hold values from -0.1875 to 0.1875
- selfbias: float32 [2, 1024], P(None, 'col'), may hold values from -0.3 to 0.3
- selfproj: bfloat16 [1024, 1024], P('col', 'row'), may hold values from -3 to 3
- selfshift: float32 [1024], P('row'), may hold values from -3 to 3
- crossquery: bfloat16 [1024, 1024], P('row', 'col'), may hold values from -0.1875 to 0.1875
- crosskv: bfloat16 [1024, 2, 1024], P('row', None, 'col'), may hold values from -0.1875 to 0.1875
- crossbias: float32 [2, 1024], P(None, 'col'), may hold values from -0.3 to 0.3
- crossproj: bfloat16 [1024, 1024], P('col', 'row'), may hold values from -4 to 4
- crossshift: float32 [1024], P('row'), may hold values from -3 to 3
- upweight: bfloat16 [1024, 4096], P('row', 'col'), may hold values from -0.1875 to 0.1875
- upbias: float32 [4096], P('col'), may hold values from -6 to 6
- downweight: bfloat16 [4096, 1024], P('col', 'row'), may hold values from -0.09375 to 0.09375
- downbias: float32 [1024], P('row'), may hold values from -3 to 3
- normgain: float32 [3, 1024], P(None, 'row'), may hold values from 0.5 to 1.5
- normshift: float32 [3, 1024], P(None, 'row'), may hold values from -3 to 3
Outputs:
- layer_out: bfloat16 [8192, 1024], P(('dp', 'col'), 'row')
- tokens_grad: float32 [8192, 1024], P(('dp', 'col'), 'row')
- encoder_grad: float32 [8192, 1024], P(('dp', 'col'), 'row')
- selfqkv_grad: float32 [1024, 3, 1024], P('row', None, 'col')
- selfbias_grad: float32 [2, 1024], P(None, 'col')
- selfproj_grad: float32 [1024, 1024], P('col', 'row')
- selfshift_grad: float32 [1024], P('row')
- crossquery_grad: float32 [1024, 1024], P('row', 'col')
- crosskv_grad: float32 [1024, 2, 1024], P('row', None, 'col')
- crossbias_grad: float32 [2, 1024], P(None, 'col')
- crossproj_grad: float32 [1024, 1024], P('col', 'row')
- crossshift_grad: float32 [1024], P('row')
- upweight_grad: float32 [1024, 4096], P('row', 'col')
- upbias_grad: float32 [4096], P('col')
- downweight_grad: float32 [4096, 1024], P('col', 'row')
- downbias_grad: float32 [1024], P('row')
- normgain_grad: float32 [3, 1024], P(None, 'row')
- normshift_grad: float32 [3, 1024], P(None, 'row')
Inputs may be any that keep to these rules, and one draw needn't show every extreme that they name: prefixes counts each sequence's leading tokens that see one another both ways.
All inputs are finite; a program needn't handle non-finite values.
Results may differ from a plain program's by a relative error of at most 0.018.
Values may be sent and summed in bfloat16 or wider, within the bound.
No kernel may reach another device: no remote copies, remote signals or barrier semaphores. Data moves between devices by JAX's collectives and lax.ppermute only.
A program may use at most 384 MiB of HBM per device.

v0:
```python
import jax
import jax.numpy as jnp
from jax import lax
from jax.sharding import PartitionSpec as P

HD = 64
SEQ_LEN = 4096
ENC_LEN = 4096


EPSILON = 1e-05
NEGATIVE = -1e30


def gather_cols(operand):
    return lax.all_gather(operand, "col", axis=0, tiled=True)


def gather_rows(operand):
    return lax.all_gather(operand, "row", axis=0, tiled=True)


def contract_with(gathered, weight, contract):
    return lax.dot_general(
        gathered, weight, (((1,), (contract,)), ((), ())), preferred_element_type=jnp.float32
    )


def total_rows(gathered, weight, contract):
    return lax.psum_scatter(
        contract_with(gathered, weight, contract), "row", scatter_dimension=0, tiled=True
    )


def total_cols(gathered, weight, contract):
    return lax.psum_scatter(
        contract_with(gathered, weight, contract), "col", scatter_dimension=0, tiled=True
    )


def over_tokens(left_side, right_side):
    return lax.dot_general(
        left_side, right_side, (((0,), (0,)), ((), ())), preferred_element_type=jnp.float32
    )


def exact_gelu(inputs):
    return jax.nn.gelu(inputs, approximate=False)


def norm_forward(hidden, gain_row, shift_row):
    moments = lax.psum((jnp.sum(hidden, axis=1), jnp.sum(hidden * hidden, axis=1)), "row")
    full_width = hidden.shape[1] * lax.axis_size("row")
    average = moments[0] / full_width
    inverse = lax.rsqrt(moments[1] / full_width - average * average + EPSILON)
    normed = (hidden - average[:, None]) * inverse[:, None]
    return (normed * gain_row + shift_row, normed, inverse)


def norm_backward(upstream, normed, inverse, gain_row):
    scaled = upstream * gain_row
    moments = lax.psum((jnp.sum(scaled, axis=1), jnp.sum(scaled * normed, axis=1)), "row")
    full_width = upstream.shape[1] * lax.axis_size("row")
    grad_in = inverse[:, None] * (
        scaled - (moments[0] / full_width)[:, None] - normed * (moments[1] / full_width)[:, None]
    )
    return (grad_in, jnp.sum(upstream * normed, axis=0), jnp.sum(upstream, axis=0))


def block_scores(query_block, key_block, limit_len, first_pos, masked):
    scores = jnp.einsum("qhd,khd->hqk", query_block, key_block, preferred_element_type=jnp.float32)
    if masked:
        query_pos = first_pos + jnp.arange(query_block.shape[0], dtype=jnp.int32)
        key_pos = jnp.arange(key_block.shape[0], dtype=jnp.int32)
        allowed = (key_pos[None, :] < limit_len) | (key_pos[None, :] <= query_pos[:, None])
        scores = jnp.where(allowed[None], scores, NEGATIVE)
    return scores


def block_inputs(queries, pairs_all, key_len, block_rows, block_index):
    full_width = queries.shape[1]
    heads_here = full_width // HD
    first_row = lax.axis_index("row") * queries.shape[0] + block_index * block_rows
    sequence = first_row // SEQ_LEN
    query_block = lax.dynamic_slice_in_dim(
        queries, block_index * block_rows, block_rows, 0
    ).reshape(block_rows, heads_here, HD)
    pair_block = lax.dynamic_slice_in_dim(pairs_all, sequence * key_len, key_len, 0)
    key_block = pair_block[:, 0].reshape(key_len, heads_here, HD)
    value_block = pair_block[:, 1].reshape(key_len, heads_here, HD)
    return (query_block, key_block, value_block, sequence, first_row - sequence * SEQ_LEN)


def attention_forward(queries, pairs_all, key_len, limits, masked):
    query_rows = queries.shape[0]
    full_width = queries.shape[1]
    block_rows = min(512, query_rows)

    def one_block(block_index):
        query_block, key_block, value_block, sequence, first_pos = block_inputs(
            queries, pairs_all, key_len, block_rows, block_index
        )
        scores = block_scores(query_block, key_block, limits[sequence], first_pos, masked)
        row_peak = jnp.max(scores, axis=2, keepdims=True)
        exponent = jnp.exp(scores - row_peak)
        denominator = jnp.sum(exponent, axis=2, keepdims=True)
        probability = (exponent / denominator).astype(jnp.bfloat16)
        output = jnp.einsum(
            "hqk,khd->qhd", probability, value_block, preferred_element_type=jnp.float32
        )
        return (
            output.reshape(block_rows, full_width),
            row_peak[:, :, 0] + jnp.log(denominator[:, :, 0]),
        )

    outputs, logsums = lax.map(one_block, jnp.arange(query_rows // block_rows))
    return (outputs.reshape(query_rows, full_width), logsums)


def share_pairs(pair_grads):
    return lax.psum_scatter(pair_grads, "row", scatter_dimension=0, tiled=True)


def attention_backward(queries, pairs_all, grads_low, logsums, key_len, limits, masked):
    query_rows = queries.shape[0]
    full_width = queries.shape[1]
    heads_here = full_width // HD
    block_rows = min(512, query_rows)

    def one_block(accumulated, block_index):
        query_block, key_block, value_block, sequence, first_pos = block_inputs(
            queries, pairs_all, key_len, block_rows, block_index
        )
        scores = block_scores(query_block, key_block, limits[sequence], first_pos, masked)
        probability = jnp.exp(scores - logsums[block_index][:, :, None])
        grad_block = lax.dynamic_slice_in_dim(
            grads_low, block_index * block_rows, block_rows, 0
        ).reshape(block_rows, heads_here, HD)
        grad_probs = jnp.einsum(
            "qhd,khd->hqk", grad_block, value_block, preferred_element_type=jnp.float32
        )
        grad_scores = (
            probability * (grad_probs - jnp.sum(probability * grad_probs, axis=2, keepdims=True))
        ).astype(jnp.bfloat16)
        grad_query = jnp.einsum(
            "hqk,khd->qhd", grad_scores, key_block, preferred_element_type=jnp.float32
        )
        grad_keys = jnp.einsum(
            "hqk,qhd->khd", grad_scores, query_block, preferred_element_type=jnp.float32
        )
        grad_values = jnp.einsum(
            "hqk,qhd->khd",
            probability.astype(jnp.bfloat16),
            grad_block,
            preferred_element_type=jnp.float32,
        )
        update = jnp.stack(
            [grad_keys.reshape(key_len, full_width), grad_values.reshape(key_len, full_width)],
            axis=1,
        )
        start_row = sequence * key_len
        current = lax.dynamic_slice_in_dim(accumulated, start_row, key_len, 0)
        accumulated = lax.dynamic_update_slice_in_dim(accumulated, current + update, start_row, 0)
        return (accumulated, grad_query.reshape(block_rows, full_width))

    zeros_init = jnp.zeros((pairs_all.shape[0], 2, full_width), jnp.float32)
    pair_grads, query_grads = lax.scan(one_block, zeros_init, jnp.arange(query_rows // block_rows))
    return (query_grads.reshape(query_rows, full_width), share_pairs(pair_grads))


def shards(
    tokens,
    encoder,
    cotangent,
    prefixes,
    selfqkv,
    selfbias,
    selfproj,
    selfshift,
    crossquery,
    crosskv,
    crossbias,
    crossproj,
    crossshift,
    upweight,
    upbias,
    downweight,
    downbias,
    normgain,
    normshift,
):
    in_width = tokens.shape[1]
    head_width = selfqkv.shape[2]
    query_scale = HD ** (-0.5)
    qkv_weight = selfqkv.reshape(in_width, 3 * head_width)
    pair_weight = crosskv.reshape(in_width, 2 * head_width)
    value_only = jnp.stack([jnp.zeros_like(selfbias[1]), selfbias[1]])
    cross_value_only = jnp.stack([jnp.zeros_like(crossbias[1]), crossbias[1]])
    tokens_all = gather_cols(tokens)
    encoder_all = gather_cols(encoder)
    mixed_qkv = total_rows(tokens_all, qkv_weight, 0).reshape(-1, 3, head_width)
    self_query = ((mixed_qkv[:, 0] + selfbias[0]) * query_scale).astype(jnp.bfloat16)
    self_pairs = (mixed_qkv[:, 1:] + value_only).astype(jnp.bfloat16)
    cross_mixed = total_rows(encoder_all, pair_weight, 0).reshape(-1, 2, head_width)
    cross_pairs = (cross_mixed + cross_value_only).astype(jnp.bfloat16)
    pairs_all = gather_rows(self_pairs)
    cross_all = gather_rows(cross_pairs)
    attended, self_logsum = attention_forward(self_query, pairs_all, SEQ_LEN, prefixes, True)
    attended = attended.astype(jnp.bfloat16)
    attended_all = gather_rows(attended)
    first_sum = tokens.astype(jnp.float32) + (total_cols(attended_all, selfproj, 0) + selfshift)
    first_out, first_normed, first_inverse = norm_forward(first_sum, normgain[0], normshift[0])
    first_low = first_out.astype(jnp.bfloat16)
    first_all = gather_cols(first_low)
    cross_query = ((total_rows(first_all, crossquery, 0) + crossbias[0]) * query_scale).astype(
        jnp.bfloat16
    )
    crossed, cross_logsum = attention_forward(cross_query, cross_all, ENC_LEN, prefixes, False)
    crossed = crossed.astype(jnp.bfloat16)
    crossed_all = gather_rows(crossed)
    second_sum = first_out + (total_cols(crossed_all, crossproj, 0) + crossshift)
    second_out, second_normed, second_inverse = norm_forward(second_sum, normgain[1], normshift[1])
    second_low = second_out.astype(jnp.bfloat16)
    second_all = gather_cols(second_low)
    hidden_pre = total_rows(second_all, upweight, 0) + upbias
    hidden_act = exact_gelu(hidden_pre).astype(jnp.bfloat16)
    hidden_all = gather_rows(hidden_act)
    third_sum = second_out + (total_cols(hidden_all, downweight, 0) + downbias)
    third_out, third_normed, third_inverse = norm_forward(third_sum, normgain[2], normshift[2])
    layer_out = third_out.astype(jnp.bfloat16)
    third_grad, third_gain, third_shift = norm_backward(
        cotangent.astype(jnp.float32), third_normed, third_inverse, normgain[2]
    )
    down_all = gather_cols(third_grad.astype(jnp.bfloat16))
    downweight_grad = over_tokens(hidden_all, down_all)
    downbias_grad = jnp.sum(down_all, axis=0, dtype=jnp.float32)
    act_grad = total_rows(down_all, downweight, 1)
    gelu_back = jax.vjp(exact_gelu, hidden_pre)[1]
    pre_low = gelu_back(act_grad)[0].astype(jnp.bfloat16)
    pre_all = gather_rows(pre_low)
    upweight_grad = over_tokens(second_all, pre_all)
    upbias_grad = jnp.sum(pre_all, axis=0, dtype=jnp.float32)
    second_grad = third_grad + total_cols(pre_all, upweight, 1)
    mid_grad, second_gain, second_shift = norm_backward(
        second_grad, second_normed, second_inverse, normgain[1]
    )
    cross_from = gather_cols(mid_grad.astype(jnp.bfloat16))
    crossproj_grad = over_tokens(crossed_all, cross_from)
    crossshift_grad = jnp.sum(cross_from, axis=0, dtype=jnp.float32)
    crossed_grad = total_rows(cross_from, crossproj, 1).astype(jnp.bfloat16)
    cross_query_grad, cross_pair_share = attention_backward(
        cross_query, cross_all, crossed_grad, cross_logsum, ENC_LEN, prefixes, False
    )
    cross_query_all = gather_rows(cross_query_grad.astype(jnp.bfloat16) * query_scale)
    cross_pair_all = gather_rows(cross_pair_share.astype(jnp.bfloat16)).reshape(-1, 2 * head_width)
    crossquery_grad = over_tokens(first_all, cross_query_all)
    crosskv_grad = over_tokens(encoder_all, cross_pair_all).reshape(in_width, 2, head_width)
    crossbias_grad = jnp.stack(
        [
            jnp.sum(cross_query_all, axis=0, dtype=jnp.float32),
            jnp.sum(cross_pair_all[:, head_width:], axis=0, dtype=jnp.float32),
        ]
    )
    encoder_grad = total_cols(cross_pair_all, pair_weight, 1)
    first_grad = mid_grad + total_cols(cross_query_all, crossquery, 1)
    low_grad, first_gain, first_shift = norm_backward(
        first_grad, first_normed, first_inverse, normgain[0]
    )
    self_from = gather_cols(low_grad.astype(jnp.bfloat16))
    selfproj_grad = over_tokens(attended_all, self_from)
    selfshift_grad = jnp.sum(self_from, axis=0, dtype=jnp.float32)
    attended_grad = total_rows(self_from, selfproj, 1).astype(jnp.bfloat16)
    self_query_grad, self_pair_share = attention_backward(
        self_query, pairs_all, attended_grad, self_logsum, SEQ_LEN, prefixes, True
    )
    combined = jnp.concatenate(
        [
            (self_query_grad.astype(jnp.bfloat16) * query_scale)[:, None],
            self_pair_share.astype(jnp.bfloat16),
        ],
        axis=1,
    )
    combined_all = gather_rows(combined).reshape(-1, 3 * head_width)
    selfqkv_grad = over_tokens(tokens_all, combined_all).reshape(in_width, 3, head_width)
    selfbias_grad = jnp.stack(
        [
            jnp.sum(combined_all[:, :head_width], axis=0, dtype=jnp.float32),
            jnp.sum(combined_all[:, 2 * head_width :], axis=0, dtype=jnp.float32),
        ]
    )
    tokens_grad = low_grad + total_cols(combined_all, qkv_weight, 1)
    norm_sums = lax.psum(
        (
            jnp.stack([first_gain, second_gain, third_gain]),
            jnp.stack([first_shift, second_shift, third_shift]),
        ),
        ("dp", "col"),
    )
    weight_sums = lax.psum(
        (
            selfqkv_grad,
            selfbias_grad,
            selfproj_grad,
            selfshift_grad,
            crossquery_grad,
            crosskv_grad,
            crossbias_grad,
            crossproj_grad,
            crossshift_grad,
            upweight_grad,
            upbias_grad,
            downweight_grad,
            downbias_grad,
        ),
        "dp",
    )
    return (
        layer_out,
        tokens_grad,
        encoder_grad,
        weight_sums[0],
        weight_sums[1],
        weight_sums[2],
        weight_sums[3],
        weight_sums[4],
        weight_sums[5],
        weight_sums[6],
        weight_sums[7],
        weight_sums[8],
        weight_sums[9],
        weight_sums[10],
        weight_sums[11],
        weight_sums[12],
        norm_sums[0],
        norm_sums[1],
    )


def solution(mesh):
    in_specs = (
        P(("dp", "col"), "row"),
        P(("dp", "col"), "row"),
        P(("dp", "col"), "row"),
        P("dp"),
        P("row", None, "col"),
        P(None, "col"),
        P("col", "row"),
        P("row"),
        P("row", "col"),
        P("row", None, "col"),
        P(None, "col"),
        P("col", "row"),
        P("row"),
        P("row", "col"),
        P("col"),
        P("col", "row"),
        P("row"),
        P(None, "row"),
        P(None, "row"),
    )
    out_specs = (
        P(("dp", "col"), "row"),
        P(("dp", "col"), "row"),
        P(("dp", "col"), "row"),
        P("row", None, "col"),
        P(None, "col"),
        P("col", "row"),
        P("row"),
        P("row", "col"),
        P("row", None, "col"),
        P(None, "col"),
        P("col", "row"),
        P("row"),
        P("row", "col"),
        P("col"),
        P("col", "row"),
        P("row"),
        P(None, "row"),
        P(None, "row"),
    )
    return jax.shard_map(shards, mesh=mesh, in_specs=in_specs, out_specs=out_specs, check_vma=False)
```

profile of v0, /device:TPU:0, one launch (start us, length us, event | category | flops | bytes accessed | tf_op | source)
XLA Modules:
  0.0 2853.1 jit_solution(15353358920252729811)
XLA Ops:
  9.2 48.8 %all-gather.17.cloned.1.call-done = bf16[4096,256]{1,0:T(8,128)(2,1)} async-done(((bf16[1024,256]{1,0:T(8,128)(2,1)}), bf16[4096,256]{1,0:T(8,128)(2,1)}) %all-gather.17.cloned.1.call-update) | async-done | bytes 2097168 | tf_op jit(solution)/shard_map/all_gather | solution.py:16
  66.7 98.1 %reduce-scatter.17.cloned.1.call-done = f32[1024,768]{1,0:T(8,128)} async-done(((f32[4096,768]{1,0:T(8,128)}), f32[1024,768]{1,0:T(8,128)}) %reduce-scatter.17.cloned.1.call-update) | async-done | bytes 3145744 | tf_op jit(solution)/shard_map/reduce_scatter | solution.py:30
  173.4 32.3 %all-gather.19.cloned.1.call-done = bf16[4096,2,256]{0,2,1:T(8,128)(2,1)} async-done(((bf16[1024,2,256]{0,2,1:T(8,128)(2,1)}), bf16[4096,2,256]{0,2,1:T(8,128)(2,1)}) %all-gather.19.cloned.1.call-update) | async-done | bytes 4194320 | tf_op jit(solution)/shard_map/all_gather | solution.py:20
  207.6 106.4 %while.54 = (s32[]{:T(128)}, bf16[2,512,256]{2,1,0:T(8,128)(2,1)}, f32[2,4,512]{2,1,0:T(4,128)}, s32[1]{0:T(128)}, s32[2]{0:T(128)}, /*index=5*/bf16[1024,256]{0...) while((s32[]{:T(128)}, bf16[2,512,256]{2,1,0:T(8,128)(2,1)}, ...), condition=%wide.region_4.5_spmd, body=%wide.region_1.4_spmd.sunk | while | flops 2227177984 | bytes 123810256 | solution.py:116
  216.2 13.4 select_reduce_fusion.2
  229.6 14.6 fusion.195
  244.2 15.1 fusion.196
  269.4 13.4 select_reduce_fusion.2
  282.7 14.6 fusion.195
  297.4 15.1 fusion.196
  314.1 22.7 all-gather.21.cloned.1.call-done
  343.4 74.6 %reduce-scatter.19.cloned.1.call-done = f32[1024,256]{1,0:T(8,128)} async-done(((f32[4096,256]{1,0:T(8,128)}), f32[1024,256]{1,0:T(8,128)}) %reduce-scatter.19.cloned.1.call-update) | async-done | bytes 1048592 | tf_op jit(solution)/shard_map/reduce_scatter | solution.py:36
  427.3 38.3 %all-gather.25.cloned.1.call-done = bf16[4096,256]{1,0:T(8,128)(2,1)} async-done(((bf16[1024,256]{1,0:T(8,128)(2,1)}), bf16[4096,256]{1,0:T(8,128)(2,1)}) %all-gather.25.cloned.1.call-update) | async-done | bytes 2097168 | tf_op jit(solution)/shard_map/all_gather | solution.py:16
  471.9 40.4 %all-gather.23.cloned.1.call-done = bf16[4096,256]{1,0:T(8,128)(2,1)} async-done(((bf16[1024,256]{1,0:T(8,128)(2,1)}), bf16[4096,256]{1,0:T(8,128)(2,1)}) %all-gather.23.cloned.1.call-update) | async-done | bytes 2097168 | tf_op jit(solution)/shard_map/all_gather | solution.py:16
  517.3 67.8 %reduce-scatter.23.cloned.1.call-done = f32[1024,512]{1,0:T(8,128)} async-done(((f32[4096,512]{1,0:T(8,128)}), f32[1024,512]{1,0:T(8,128)}) %reduce-scatter.23.cloned.1.call-update) | async-done | bytes 2097168 | tf_op jit(solution)/shard_map/reduce_scatter | solution.py:30
  588.2 44.0 %reduce-scatter.21.cloned.1.call-done = f32[1024,256]{1,0:T(8,128)} async-done(((f32[4096,256]{1,0:T(8,128)}), f32[1024,256]{1,0:T(8,128)}) %reduce-scatter.21.cloned.1.call-update) | async-done | bytes 1048592 | tf_op jit(solution)/shard_map/reduce_scatter | solution.py:30
  633.8 35.0 %all-gather.27.cloned.1.call-done = bf16[4096,2,256]{0,2,1:T(8,128)(2,1)} async-done(((bf16[1024,2,256]{0,2,1:T(8,128)(2,1)}), bf16[4096,2,256]{0,2,1:T(8,128)(2,1)}) %all-gather.27.cloned.1.call-update) | async-done | bytes 4194320 | tf_op jit(solution)/shard_map/all_gather | solution.py:20
  670.7 92.6 %while.55 = (s32[]{:T(128)}, bf16[2,512,256]{2,1,0:T(8,128)(2,1)}, f32[2,4,512]{2,1,0:T(4,128)}, s32[2]{0:T(128)}, bf16[1024,256]{0,1:T(8,128)(2,1)S(1)}, /*inde...) while((s32[]{:T(128)}, bf16[2,512,256]{2,1,0:T(8,128)(2,1)}, ...), condition=%wide.region_15.16_spmd, body=%wide.region_12.15_spmd.sunk | while | flops 2197813248 | bytes 115409064 | solution.py:116
  675.1 13.2 fusion.201
  688.3 13.6 fusion.202
  701.9 13.7 fusion.203
  721.4 13.2 fusion.201
  734.6 13.6 fusion.202
  748.2 13.7 fusion.203
  763.4 22.7 all-gather.29.cloned.1.call-done
  790.5 76.9 %reduce-scatter.25.cloned.1.call-done = f32[1024,256]{1,0:T(8,128)} async-done(((f32[4096,256]{1,0:T(8,128)}), f32[1024,256]{1,0:T(8,128)}) %reduce-scatter.25.cloned.1.call-update) | async-done | bytes 1048592 | tf_op jit(solution)/shard_map/reduce_scatter | solution.py:36
  877.1 45.8 %all-gather.31.cloned.1.call-done = bf16[4096,256]{1,0:T(8,128)(2,1)} async-done(((bf16[1024,256]{1,0:T(8,128)(2,1)}), bf16[4096,256]{1,0:T(8,128)(2,1)}) %all-gather.31.cloned.1.call-update) | async-done | bytes 2097168 | tf_op jit(solution)/shard_map/all_gather | solution.py:16
  932.7 123.9 %reduce-scatter.27.cloned.1.call-done = f32[1024,1024]{1,0:T(8,128)} async-done(((f32[4096,1024]{1,0:T(8,128)}), f32[1024,1024]{1,0:T(8,128)}) %reduce-scatter.27.cloned.1.call-update) | async-done | bytes 4194320 | tf_op jit(solution)/shard_map/reduce_scatter | solution.py:30
  1068.5 58.4 %all-gather.33.cloned.1.call-done = bf16[4096,1024]{1,0:T(8,128)(2,1)} async-done(((bf16[1024,1024]{1,0:T(8,128)(2,1)}), bf16[4096,1024]{1,0:T(8,128)(2,1)}) %all-gather.33.cloned.1.call-update) | async-done | bytes 8388624 | tf_op jit(solution)/shard_map/all_gather | solution.py:20
  1134.7 76.9 %reduce-scatter.29.cloned.1.call-done = f32[1024,256]{1,0:T(8,128)} async-done(((f32[4096,256]{1,0:T(8,128)}), f32[1024,256]{1,0:T(8,128)}) %reduce-scatter.29.cloned.1.call-update) | async-done | bytes 1048592 | tf_op jit(solution)/shard_map/reduce_scatter | solution.py:36
  1230.8 46.0 %all-gather.35.cloned.1.call-done = bf16[4096,256]{1,0:T(8,128)(2,1)} async-done(((bf16[1024,256]{1,0:T(8,128)(2,1)}), bf16[4096,256]{1,0:T(8,128)(2,1)}) %all-gather.35.cloned.1.call-update) | async-done | bytes 2097168 | tf_op jit(solution)/shard_map/all_gather | solution.py:16
  1286.6 123.9 %reduce-scatter.31.cloned.1.call-done = f32[1024,1024]{1,0:T(8,128)} async-done(((f32[4096,1024]{1,0:T(8,128)}), f32[1024,1024]{1,0:T(8,128)}) %reduce-scatter.31.cloned.1.call-update) | async-done | bytes 4194320 | tf_op jit(solution)/shard_map/reduce_scatter | solution.py:30
  1417.3 58.4 %all-gather.37.cloned.1.call-done = bf16[4096,1024]{1,0:T(8,128)(2,1)} async-done(((bf16[1024,1024]{1,0:T(8,128)(2,1)}), bf16[4096,1024]{1,0:T(8,128)(2,1)}) %all-gather.37.cloned.1.call-update) | async-done | bytes 8388624 | tf_op jit(solution)/shard_map/all_gather | solution.py:20
  1483.5 76.9 %reduce-scatter.33.cloned.1.call-done = f32[1024,256]{1,0:T(8,128)} async-done(((f32[4096,256]{1,0:T(8,128)}), f32[1024,256]{1,0:T(8,128)}) %reduce-scatter.33.cloned.1.call-update) | async-done | bytes 1048592 | tf_op jit(solution)/shard_map/reduce_scatter | solution.py:36
  1573.4 46.0 %all-gather.39.cloned.1.call-done = bf16[4096,256]{1,0:T(8,128)(2,1)} async-done(((bf16[1024,256]{1,0:T(8,128)(2,1)}), bf16[4096,256]{1,0:T(8,128)(2,1)}) %all-gather.39.cloned.1.call-update) | async-done | bytes 2097168 | tf_op jit(solution)/shard_map/all_gather | solution.py:16
  1623.8 43.5 %reduce-scatter.35.cloned.1.call-done = f32[1024,256]{1,0:T(8,128)} async-done(((f32[4096,256]{1,0:T(8,128)}), f32[1024,256]{1,0:T(8,128)}) %reduce-scatter.35.cloned.1.call-update) | async-done | bytes 1048592 | tf_op jit(solution)/shard_map/reduce_scatter | solution.py:30
  1670.2 209.3 %while.56 = (s32[]{:T(128)}, f32[4096,2,256]{0,2,1:T(8,128)}, bf16[2,512,256]{2,1,0:T(8,128)(2,1)}, s32[2]{0:T(128)S(1)}, bf16[1024,256]{0,1:T(8,128)(2,1)S(1)},...) while((s32[]{:T(128)}, f32[4096,2,256]{0,2,1:T(8,128)}, ...), condition=%wide.region_40.41_spmd.clone, body=%wide.region_38.40_spmd.clone.sunk | while | flops 5450496000 | bytes 396157344 | solution.py:167
  1677.7 13.1 fusion.215
  1690.8 15.3 fusion.216
  1706.1 21.8 multiply_reduce_fusion.13
  1727.9 27.4 multiply_convert_fusion.6
  1781.0 13.1 fusion.215
  1794.1 15.3 fusion.216
  1809.4 21.8 multiply_reduce_fusion.13
  1831.2 27.4 multiply_convert_fusion.6
  1881.4 22.6 all-gather.41.cloned.1.call-done
  1908.5 76.9 %reduce-scatter.37.cloned.1.call-done = f32[1024,256]{1,0:T(8,128)} async-done(((f32[4096,256]{1,0:T(8,128)}), f32[1024,256]{1,0:T(8,128)}) %reduce-scatter.37.cloned.1.call-update) | async-done | bytes 1048592 | tf_op jit(solution)/shard_map/reduce_scatter | solution.py:36
  1997.8 46.0 %all-gather.43.cloned.1.call-done = bf16[4096,256]{1,0:T(8,128)(2,1)} async-done(((bf16[1024,256]{1,0:T(8,128)(2,1)}), bf16[4096,256]{1,0:T(8,128)(2,1)}) %all-gather.43.cloned.1.call-update) | async-done | bytes 2097168 | tf_op jit(solution)/shard_map/all_gather | solution.py:16
  2048.2 43.5 %reduce-scatter.39.cloned.1.call-done = f32[1024,256]{1,0:T(8,128)} async-done(((f32[4096,256]{1,0:T(8,128)}), f32[1024,256]{1,0:T(8,128)}) %reduce-scatter.39.cloned.1.call-update) | async-done | bytes 1048592 | tf_op jit(solution)/shard_map/reduce_scatter | solution.py:30
  2093.8 229.1 %while.57 = (s32[]{:T(128)}, f32[4096,2,256]{0,2,1:T(8,128)}, bf16[2,512,256]{2,1,0:T(8,128)(2,1)}, s32[2]{0:T(128)S(1)}, bf16[1024,256]{0,1:T(8,128)(2,1)S(1)},...) while((s32[]{:T(128)}, f32[4096,2,256]{0,2,1:T(8,128)}, ...), condition=%wide.region_49.50_spmd.clone, body=%wide.region_47.49_spmd.clone.sunk | while | flops 5479860736 | bytes 412947168 | solution.py:167
  2118.4 16.7 fusion.232
  2135.1 25.1 multiply_reduce_fusion.14
  2160.2 27.7 multiply_convert_fusion.7
  2218.4 13.1 fusion.230
  2231.5 16.7 fusion.232
  2248.2 25.1 multiply_reduce_fusion.14
  2273.4 27.7 multiply_convert_fusion.7
  2342.3 61.0 %reduce-scatter.41.cloned.1.call-done = f32[1024,2,256]{2,0,1:T(8,128)} async-done(((f32[4096,2,256]{2,0,1:T(8,128)}), f32[1024,2,256]{2,0,1:T(8,128)}) %reduce-scatter.41.cloned.1.call-update) | async-done | bytes 2097168 | tf_op jit(solution)/shard_map/reduce_scatter | solution.py:121
  2406.4 71.0 %reduce-scatter.45.cloned.1.call-done = f32[1024,2,256]{2,0,1:T(8,128)} async-done(((f32[4096,2,256]{2,0,1:T(8,128)}), f32[1024,2,256]{2,0,1:T(8,128)}) %reduce-scatter.45.cloned.1.call-update) | async-done | bytes 2097168 | tf_op jit(solution)/shard_map/reduce_scatter | solution.py:121
  2480.1 45.2 %all-gather.45.cloned.1.call-done = bf16[4096,3,256]{2,0,1:T(8,128)(2,1)} async-done(((bf16[1024,3,256]{2,0,1:T(8,128)(2,1)}), bf16[4096,3,256]{2,0,1:T(8,128)(2,1)}) %all-gather.45.cloned.1.call-update) | async-done | bytes 6291472 | tf_op jit(solution)/shard_map/all_gather | solution.py:20
  2532.0 29.8 %all-gather.47.cloned.1.call-done = bf16[4096,2,256]{2,0,1:T(8,128)(2,1)} async-done(((bf16[1024,2,256]{2,0,1:T(8,128)(2,1)}), bf16[4096,2,256]{2,0,1:T(8,128)(2,1)}) %all-gather.47.cloned.1.call-update) | async-done | bytes 4194320 | tf_op jit(solution)/shard_map/all_gather | solution.py:20
  2621.7 23.7 all-reduce.2
  2661.0 61.4 %reduce-scatter.47.cloned.1.call-done = f32[1024,256]{1,0:T(8,128)} async-done(((f32[4096,256]{1,0:T(8,128)}), f32[1024,256]{1,0:T(8,128)}) %reduce-scatter.47.cloned.1.call-update) | async-done | bytes 1048592 | tf_op jit(solution)/shard_map/reduce_scatter | solution.py:36
  2722.4 112.5 %all-reduce.13.cloned.1.call-done = (f32[256,3,256]{2,0,1:T(8,128)}, f32[256,256]{1,0:T(8,128)}, f32[256,256]{1,0:T(8,128)}, f32[256,2,256]{2,1,0:T(2,128)}, f32...) async-done(((f32[256,3,256]{2,0,1:T(8,128)}, f32[256,256]{1,0:T(8,128)}, f32[256,256]{1,0:T(8,128)}, f32[256,2,256]{2,1,0:T(2,128)}, f32[256,256]{1,0:T(8,128)}, ...) | async-done | bytes 4194320 | tf_op jit(solution)/shard_map/psum | solution.py:299
  (439 shorter events, 453.5 us)
Async XLA Ops:
  7.2 1119.7 %copy-start = (bf16[1024,256]{1,0:T(8,128)(2,1)S(1)}, bf16[1024,256]{1,0:T(8,128)(2,1)}, u32[]{:S(2)}) copy-start(bf16[1024,256]{1,0:T(8,128)(2,1)} %param.42) | copy-start | bytes 1572868
  7.2 50.8 %all-gather.17.cloned.1.call-start = ((), (), s32[]{:S(2)}) async-start(), calls=%async_computation.16 | async-start | bytes 2621440 | tf_op jit(solution)/shard_map/all_gather | solution.py:16
  7.9 156.8 %reduce-scatter.17.cloned.1.call-start = ((), (), s32[]{:S(2)}) async-start(), calls=%async_computation.17 | async-start | bytes 15728640 | tf_op jit(solution)/shard_map/reduce_scatter | solution.py:30
  66.0 139.7 %all-gather.19.cloned.1.call-start = ((), (), s32[]{:S(2)}) async-start(), calls=%async_computation.18 | async-start | bytes 5242880 | tf_op jit(solution)/shard_map/all_gather | solution.py:20
  171.0 165.7 %all-gather.21.cloned.1.call-start = ((), (), s32[]{:S(2)}) async-start(), calls=%async_computation.19 | async-start | bytes 2621440 | tf_op jit(solution)/shard_map/all_gather | solution.py:20
  207.6 129.1 %copy-start.43 = (bf16[256,256]{1,0:T(8,128)(2,1)S(1)}, bf16[256,256]{1,0:T(8,128)(2,1)}, u32[]{:S(2)}) copy-start(bf16[256,256]{1,0:T(8,128)(2,1)} %param.33) | copy-start | bytes 393220
  314.0 104.0 %reduce-scatter.19.cloned.1.call-start = ((), (), s32[]{:S(2)}) async-start(), calls=%async_computation.20 | async-start | bytes 5242880 | tf_op jit(solution)/shard_map/reduce_scatter | solution.py:36
  341.0 77.0 %copy-start.30 = (bf16[1024,256]{1,0:T(8,128)(2,1)S(1)}, bf16[1024,256]{1,0:T(8,128)(2,1)}, u32[]{:S(2)}) copy-start(bf16[1024,256]{1,0:T(8,128)(2,1)} %param.27) | copy-start | bytes 1572868
  341.0 77.0 %copy-start.76 = (f32[256]{0:T(256)S(1)}, f32[256]{0:T(256)}, u32[]{:S(2)}) copy-start(f32[256]{0:T(256)} %param.34) | copy-start | bytes 3076
  341.0 86.2 %copy-start.37 = (bf16[256,2,256]{2,1,0:T(2,128)(2,1)S(1)}, bf16[256,2,256]{2,1,0:T(2,128)(2,1)}, u32[]{:S(2)}) copy-start(bf16[256,2,256]{2,1,0:T(2,128)(2,1)} %param.36) | copy-start | bytes 786436
  341.1 124.6 %all-gather.25.cloned.1.call-start = ((), (), s32[]{:S(2)}) async-start(), calls=%async_computation.23 | async-start | bytes 2621440 | tf_op jit(solution)/shard_map/all_gather | solution.py:16
  341.7 170.6 %all-gather.23.cloned.1.call-start = ((), (), s32[]{:S(2)}) async-start(), calls=%async_computation.21 | async-start | bytes 2621440 | tf_op jit(solution)/shard_map/all_gather | solution.py:16
  342.9 128.9 %copy-start.54 = (f32[1,256]{1,0:T(1,128)}, f32[1,256]{1,0:T(1,128)S(1)}, u32[]{:S(2)}) copy-start(f32[1,256]{1,0:T(1,128)S(1)} %get-tuple-element.563) | copy-start | bytes 3076
  343.4 128.3 %copy-start.61 = (f32[1,256]{1,0:T(1,128)}, f32[1,256]{1,0:T(1,128)S(1)}, u32[]{:S(2)}) copy-start(f32[1,256]{1,0:T(1,128)S(1)} %get-tuple-element.566) | copy-start | bytes 3076
  419.6 52.2 %copy-start.7 = (f32[1024,256]{1,0:T(8,128)}, f32[1024,256]{1,0:T(8,128)S(1)}, u32[]{:S(2)}) copy-start(f32[1024,256]{1,0:T(8,128)S(1)} %get-tuple-element.542) | copy-start | bytes 3145732
  427.2 157.9 %reduce-scatter.23.cloned.1.call-start = ((), (), s32[]{:S(2)}) async-start(), calls=%async_computation.24 | async-start | bytes 10485760 | tf_op jit(solution)/shard_map/reduce_scatter | solution.py:30
  471.8 160.4 %reduce-scatter.21.cloned.1.call-start = ((), (), s32[]{:S(2)}) async-start(), calls=%async_computation.22 | async-start | bytes 5242880 | tf_op jit(solution)/shard_map/reduce_scatter | solution.py:30
  516.6 152.1 %all-gather.27.cloned.1.call-start = ((), (), s32[]{:S(2)}) async-start(), calls=%async_computation.25 | async-start | bytes 5242880 | tf_op jit(solution)/shard_map/all_gather | solution.py:20
  588.2 197.9 %all-gather.29.cloned.1.call-start = ((), (), s32[]{:S(2)}) async-start(), calls=%async_computation.26 | async-start | bytes 2621440 | tf_op jit(solution)/shard_map/all_gather | solution.py:20
  670.7 115.4 %copy-start.41 = (bf16[256,256]{1,0:T(8,128)(2,1)S(1)}, bf16[256,256]{1,0:T(8,128)(2,1)}, u32[]{:S(2)}) copy-start(bf16[256,256]{1,0:T(8,128)(2,1)} %param.38) | copy-start | bytes 393220
  763.3 104.0 %reduce-scatter.25.cloned.1.call-start = ((), (), s32[]{:S(2)}) async-start(), calls=%async_computation.27 | async-start | bytes 5242880 | tf_op jit(solution)/shard_map/reduce_scatter | solution.py:36
  790.3 77.0 %copy-start.8 = (f32[1024,256]{1,0:T(8,128)S(1)}, f32[1024,256]{1,0:T(8,128)}, u32[]{:S(2)}) copy-start(f32[1024,256]{1,0:T(8,128)} %copy-done.7) | copy-start | bytes 3145732
  790.3 77.0 %copy-start.49 = (f32[1024]{0:T(1024)S(1)}, f32[1024]{0:T(1024)}, u32[]{:S(2)}) copy-start(f32[1024]{0:T(1024)} %copy-done.48) | copy-start | bytes 12292
  790.3 77.0 %copy-start.52 = (f32[1024]{0:T(1024)S(1)}, f32[1024]{0:T(1024)}, u32[]{:S(2)}) copy-start(f32[1024]{0:T(1024)} %copy-done.51) | copy-start | bytes 12292
  790.3 77.0 %copy-start.55 = (f32[1,256]{1,0:T(1,128)S(1)}, f32[1,256]{1,0:T(1,128)}, u32[]{:S(2)}) copy-start(f32[1,256]{1,0:T(1,128)} %copy-done.54) | copy-start | bytes 3076
  790.3 77.0 %copy-start.62 = (f32[1,256]{1,0:T(1,128)S(1)}, f32[1,256]{1,0:T(1,128)}, u32[]{:S(2)}) copy-start(f32[1,256]{1,0:T(1,128)} %copy-done.61) | copy-start | bytes 3076
  790.3 77.0 %copy-start.74 = (f32[256]{0:T(256)S(1)}, f32[256]{0:T(256)}, u32[]{:S(2)}) copy-start(f32[256]{0:T(256)} %param.39) | copy-start | bytes 3076
  790.4 85.3 %copy-start.57 = (f32[1,256]{1,0:T(1,128)S(1)}, f32[1,256]{1,0:T(1,128)}, u32[]{:S(2)}) copy-start(f32[1,256]{1,0:T(1,128)} %get-tuple-element.564) | copy-start | bytes 3076
  790.4 85.3 %copy-start.60 = (f32[1,256]{1,0:T(1,128)S(1)}, f32[1,256]{1,0:T(1,128)}, u32[]{:S(2)}) copy-start(f32[1,256]{1,0:T(1,128)} %get-tuple-element.567) | copy-start | bytes 3076
  790.4 132.5 %all-gather.31.cloned.1.call-start = ((), (), s32[]{:S(2)}) async-start(), calls=%async_computation.28 | async-start | bytes 2621440 | tf_op jit(solution)/shard_map/all_gather | solution.py:16
  876.9 179.8 %reduce-scatter.27.cloned.1.call-start = ((), (), s32[]{:S(2)}) async-start(), calls=%async_computation.29 | async-start | bytes 20971520 | tf_op jit(solution)/shard_map/reduce_scatter | solution.py:30
  932.7 124.0 %copy-start.59 = (f32[1024]{0:T(1024)S(1)}, f32[1024]{0:T(1024)}, u32[]{:S(2)}) copy-start(f32[1024]{0:T(1024)} %param.41) | copy-start | bytes 12292
  932.7 194.2 %all-gather.33.cloned.1.call-start = ((), (), s32[]{:S(2)}) async-start(), calls=%async_computation.30 | async-start | bytes 10485760 | tf_op jit(solution)/shard_map/all_gather | solution.py:20
  1068.4 143.2 %reduce-scatter.29.cloned.1.call-start = ((), (), s32[]{:S(2)}) async-start(), calls=%async_computation.31 | async-start | bytes 5242880 | tf_op jit(solution)/shard_map/reduce_scatter | solution.py:36
  1134.7 77.0 %copy-start.75 = (f32[256]{0:T(256)S(1)}, f32[256]{0:T(256)}, u32[]{:S(2)}) copy-start(f32[256]{0:T(256)} %param.43) | copy-start | bytes 3076
  1134.7 85.2 %copy-start.58 = (f32[1,256]{1,0:T(1,128)S(1)}, f32[1,256]{1,0:T(1,128)}, u32[]{:S(2)}) copy-start(f32[1,256]{1,0:T(1,128)} %get-tuple-element.562) | copy-start | bytes 3076
  1134.7 142.1 %all-gather.35.cloned.1.call-start = ((), (), s32[]{:S(2)}) async-start(), calls=%async_computation.32 | async-start | bytes 2621440 | tf_op jit(solution)/shard_map/all_gather | solution.py:16
  1230.8 179.7 %reduce-scatter.31.cloned.1.call-start = ((), (), s32[]{:S(2)}) async-start(), calls=%async_computation.33 | async-start | bytes 20971520 | tf_op jit(solution)/shard_map/reduce_scatter | solution.py:30
  1286.5 189.1 %all-gather.37.cloned.1.call-start = ((), (), s32[]{:S(2)}) async-start(), calls=%async_computation.34 | async-start | bytes 10485760 | tf_op jit(solution)/shard_map/all_gather | solution.py:20
  1410.5 65.2 %copy-start.45 = (bf16[256,1024]{1,0:T(8,128)(2,1)S(1)}, bf16[256,1024]{1,0:T(8,128)(2,1)}, u32[]{:S(2)}) copy-start(bf16[256,1024]{1,0:T(8,128)(2,1)} %param.40) | copy-start | bytes 1572868
  1417.3 143.2 %reduce-scatter.33.cloned.1.call-start = ((), (), s32[]{:S(2)}) async-start(), calls=%async_computation.35 | async-start | bytes 5242880 | tf_op jit(solution)/shard_map/reduce_scatter | solution.py:36
  1483.4 77.0 %copy-start.27 = (bf16[1024,256]{1,0:T(8,128)(2,1)S(1)}, bf16[1024,256]{1,0:T(8,128)(2,1)}, u32[]{:S(2)}) copy-start(bf16[1024,256]{1,0:T(8,128)(2,1)} %param.29) | copy-start | bytes 1572868
  1483.4 77.0 %copy-start.67 = (f32[1,256]{1,0:T(1,128)S(1)}, f32[1,256]{1,0:T(1,128)}, u32[]{:S(2)}) copy-start(f32[1,256]{1,0:T(1,128)} %get-tuple-element.565) | copy-start | bytes 3076
  1483.5 135.9 %all-gather.39.cloned.1.call-start = ((), (), s32[]{:S(2)}) async-start(), calls=%async_computation.36 | async-start | bytes 2621440 | tf_op jit(solution)/shard_map/all_gather | solution.py:16
  1573.4 93.9 %reduce-scatter.35.cloned.1.call-start = ((), (), s32[]{:S(2)}) async-start(), calls=%async_computation.37 | async-start | bytes 5242880 | tf_op jit(solution)/shard_map/reduce_scatter | solution.py:30
  1623.7 46.5 %copy-start.47 = (f32[2,4,512]{2,1,0:T(4,128)S(1)}, f32[2,4,512]{2,1,0:T(4,128)}, u32[]{:S(2)}) copy-start(f32[2,4,512]{2,1,0:T(4,128)} %get-tuple-element.881) | copy-start | bytes 49156
  1623.7 280.3 %all-gather.41.cloned.1.call-start = ((), (), s32[]{:S(2)}) async-start(), calls=%async_computation.38 | async-start | bytes 2621440 | tf_op jit(solution)/shard_map/all_gather | solution.py:20
  1881.4 104.0 %reduce-scatter.37.cloned.1.call-start = ((), (), s32[]{:S(2)}) async-start(), calls=%async_computation.39 | async-start | bytes 5242880 | tf_op jit(solution)/shard_map/reduce_scatter | solution.py:36
  1908.4 77.0 %copy-start.9 = (f32[1024,256]{1,0:T(8,128)S(1)}, f32[1024,256]{1,0:T(8,128)}, u32[]{:S(2)}) copy-start(f32[1024,256]{1,0:T(8,128)} %copy-done.7) | copy-start | bytes 3145732
  1908.4 77.0 %copy-start.29 = (f32[1024,256]{1,0:T(8,128)S(1)}, f32[1024,256]{1,0:T(8,128)}, u32[]{:S(2)}) copy-start(f32[1024,256]{1,0:T(8,128)} %get-tuple-element.536) | copy-start | bytes 3145732
  1908.4 77.0 %copy-start.50 = (f32[1024]{0:T(1024)S(1)}, f32[1024]{0:T(1024)}, u32[]{:S(2)}) copy-start(f32[1024]{0:T(1024)} %copy-done.48) | copy-start | bytes 12292
  1908.4 77.0 %copy-start.53 = (f32[1024]{0:T(1024)S(1)}, f32[1024]{0:T(1024)}, u32[]{:S(2)}) copy-start(f32[1024]{0:T(1024)} %copy-done.51) | copy-start | bytes 12292
  1908.4 77.0 %copy-start.56 = (f32[1,256]{1,0:T(1,128)S(1)}, f32[1,256]{1,0:T(1,128)}, u32[]{:S(2)}) copy-start(f32[1,256]{1,0:T(1,128)} %copy-done.54) | copy-start | bytes 3076
  1908.4 135.4 %all-gather.43.cloned.1.call-start = ((), (), s32[]{:S(2)}) async-start(), calls=%async_computation.40 | async-start | bytes 2621440 | tf_op jit(solution)/shard_map/all_gather | solution.py:16
  1985.4 58.4 %copy-start.44 = (bf16[256,256]{1,0:T(8,128)(2,1)S(1)}, bf16[256,256]{1,0:T(8,128)(2,1)}, u32[]{:S(2)}) copy-start(bf16[256,256]{1,0:T(8,128)(2,1)} %param.33) | copy-start | bytes 393220
  1997.8 93.9 %reduce-scatter.39.cloned.1.call-start = ((), (), s32[]{:S(2)}) async-start(), calls=%async_computation.41 | async-start | bytes 5242880 | tf_op jit(solution)/shard_map/reduce_scatter | solution.py:30
  2048.1 355.2 %reduce-scatter.41.cloned.1.call-start = ((), (), s32[]{:S(2)}) async-start(), calls=%async_computation.42 | async-start | bytes 10485760 | tf_op jit(solution)/shard_map/reduce_scatter | solution.py:121
  2331.8 145.6 %reduce-scatter.45.cloned.1.call-start = ((), (), s32[]{:S(2)}) async-start(), calls=%async_computation.45 | async-start | bytes 10485760 | tf_op jit(solution)/shard_map/reduce_scatter | solution.py:121
  2341.1 184.2 %all-gather.45.cloned.1.call-start = ((), (), s32[]{:S(2)}) async-start(), calls=%async_computation.43 | async-start | bytes 7864320 | tf_op jit(solution)/shard_map/all_gather | solution.py:20
  2405.0 120.3 %copy-start.36 = (bf16[256,3,256]{2,0,1:T(8,128)(2,1)S(1)}, bf16[256,3,256]{2,0,1:T(8,128)(2,1)}, u32[]{:S(2)}) copy-start(bf16[256,3,256]{2,0,1:T(8,128)(2,1)} %param.31) | copy-start | bytes 1179652
  2406.3 155.4 %all-gather.47.cloned.1.call-start = ((), (), s32[]{:S(2)}) async-start(), calls=%async_computation.46 | async-start | bytes 5242880 | tf_op jit(solution)/shard_map/all_gather | solution.py:20
  2480.0 178.6 %reduce-scatter.43.cloned.1.call-start = ((), (), s32[]{:S(2)}) async-start(), calls=%async_computation.44 | async-start | bytes 5242880 | tf_op jit(solution)/shard_map/reduce_scatter | solution.py:36
  2531.9 190.4 %reduce-scatter.47.cloned.1.call-start = ((), (), s32[]{:S(2)}) async-start(), calls=%async_computation.47 | async-start | bytes 5242880 | tf_op jit(solution)/shard_map/reduce_scatter | solution.py:36
  2567.3 267.5 %all-reduce.13.cloned.1.call-start = ((), (), s32[]{:S(2)}) async-start(), calls=%async_computation.48 | async-start | bytes 8388608 | tf_op jit(solution)/shard_map/psum | solution.py:299
  (59 other events, 446.6 us)
Sparse Core Ops, SparseCore 0:
  9.6 48.3 all-gather.16
  66.1 98.5 reduce-scatter.16
  171.2 34.4 all-gather.18
  314.1 22.5 all-gather.20
  341.2 76.7 reduce-scatter.18
  419.5 46.1 all-gather.24
  467.8 44.4 all-gather.22
  514.9 70.1 reduce-scatter.22
  587.6 44.5 reduce-scatter.20
  634.2 34.4 all-gather.26
  763.5 22.5 all-gather.28
  790.5 76.7 reduce-scatter.24
  877.0 45.8 all-gather.30
  932.8 123.8 reduce-scatter.26
  1068.6 58.2 all-gather.32
  1134.8 76.7 reduce-scatter.28
  1230.9 45.8 all-gather.34
  1286.7 123.8 reduce-scatter.30
  1417.4 58.2 all-gather.36
  1483.6 76.7 reduce-scatter.32
  1573.5 45.8 all-gather.38
  1623.9 43.3 reduce-scatter.34
  1881.5 22.5 all-gather.40
  1908.5 76.7 reduce-scatter.36
  1997.9 45.8 all-gather.42
  2048.2 43.3 reduce-scatter.38
  2331.9 71.3 reduce-scatter.40
  2405.9 71.4 reduce-scatter.44
  2478.9 46.3 all-gather.44
  2527.3 34.4 all-gather.46
  2564.1 77.8 reduce-scatter.42
  2644.8 77.4 reduce-scatter.46
  2726.4 108.4 all-reduce.12
where the time goes:
time: 2860 us; the launch traced here: 2850 us
  waiting for transfers between devices  1870 us (65%)
  matrix products  485 us (17%)
  other arithmetic  273 us (10%)
  local copies, waits for them, and re-layouts  120 us (4%)
  blocking collectives  69.3 us (2%)
    reduce_scatter x7, waiting for transfers between devices, total_rows(): lax.psum_scatter(contract_with(gathered, weight, contract), 'row', scatte...  545 us
    reduce_scatter x7, waiting for transfers between devices, total_cols(): lax.psum_scatter(contract_with(gathered, weight, contract), 'col', scatte...  444 us
    all_gather x9, waiting for transfers between devices, gather_rows(): return lax.all_gather(operand, 'row', axis=0, tiled=True)  327 us
    all_gather x7, waiting for transfers between devices, gather_cols(): return lax.all_gather(operand, 'col', axis=0, tiled=True)  311 us
    reduce_scatter x2, waiting for transfers between devices, share_pairs(): return lax.psum_scatter(pair_grads, 'row', scatter_dimension=0, tiled=True)  132 us
    psum x1, waiting for transfers between devices, shards(): lax.psum((selfqkv_grad, selfbias_grad, selfproj_grad, selfshift_grad, cro...  113 us
    convert_element_type x4, other arithmetic, one_block(): grad_scores = (probability * (grad_probs - jnp.sum(probability * grad_pro...  110 us
    dot_general x8, matrix products, block_scores(): jnp.einsum('qhd,khd->hqk', query_block, key_block, preferred_element_type...  106 us
  transfers between devices with their start and end apart: 33, of which 32 were waited for; matrix products, arithmetic and copies ran while one was open for 4% of the time, Pallas kernels for 0%

commit v1 on v0

v1 whole, which is shorter than its diff:
```python
import functools
import jax
import jax.numpy as jnp
from jax import lax
from jax.experimental import pallas as pl
from jax.experimental.pallas import tpu as pltpu
from jax.sharding import Mesh
from jax.sharding import PartitionSpec as P

HD = 64
NEGATIVE = -1e30
F32 = jnp.float32
BF16 = jnp.bfloat16


def dot_nn(a, b):
    return lax.dot_general(a, b, (((1,), (0,)), ((), ())), preferred_element_type=F32)


def allowed_mask(first_key, first_query, prefix, shape):
    key_pos = first_key + lax.broadcasted_iota(jnp.int32, shape, 0)
    query_pos = first_query + lax.broadcasted_iota(jnp.int32, shape, 1)
    return (key_pos < prefix) | (key_pos <= query_pos)


def forward_kernel(masked, bq, bk, prefix_ref, q_ref, k_ref, v_ref, o_ref, low_ref, lse_ref, keys, values, acc, peak):
    chunks, _, chunk = k_ref.shape
    per = chunk // bk
    blocks = chunks * per
    step = pl.program_id(0)
    prefix = prefix_ref[0]

    @pl.when(step == 0)
    def _():
        for c in range(chunks):
            for b in range(per):
                i = c * per + b
                keys[i] = k_ref[c, :, b * bk:(b + 1) * bk].T
                values[i, :HD, :] = v_ref[c, :, b * bk:(b + 1) * bk]
                rows = lax.broadcasted_iota(jnp.int32, (16, bk), 0)
                values[i, HD:, :] = jnp.where(rows == 0, 1.0, 0.0).astype(BF16)

    first_query = step * bq
    query = q_ref[0]
    peak[...] = jnp.full(peak.shape, NEGATIVE, F32)
    acc[...] = jnp.zeros(acc.shape, F32)

    def visit(i, use_mask):
        scores = dot_nn(keys[i], query)
        if use_mask:
            scores = jnp.where(allowed_mask(i * bk, first_query, prefix, scores.shape), scores, NEGATIVE)
        old = peak[...]
        new = jnp.maximum(old, jnp.max(scores, axis=0, keepdims=True))
        weight = jnp.exp(scores - new).astype(BF16)
        acc[...] = acc[...] * jnp.exp(old - new) + dot_nn(values[i], weight)
        peak[...] = new

    if masked:
        full = jnp.maximum(prefix, first_query + 1) // bk
        stop = (jnp.maximum(prefix, first_query + bq) + bk - 1) // bk
        lax.fori_loop(0, full, lambda i, c: (visit(i, False), c)[1], 0)
        lax.fori_loop(full, stop, lambda i, c: (visit(i, True), c)[1], 0)
    else:
        lax.fori_loop(0, blocks, lambda i, c: (visit(i, False), c)[1], 0)
    total = acc[HD:HD + 1, :]
    out = acc[:HD, :] / total
    o_ref[0] = out
    low_ref[0] = out.astype(BF16)
    lse_ref[0] = peak[...] + jnp.log(total)


def flash_forward(prefix, queries, q_part, pairs, k_part, v_part, masked, bq=1024, bk=1024):
    chunks, _, chunk = queries.shape
    length = chunks * chunk
    per = chunk // bq
    whole = lambda part: pl.BlockSpec((chunks, HD, chunk), lambda i, p: (0, part, 0))
    mine = lambda rows: pl.BlockSpec((1, rows, bq), lambda i, p: (i // per, 0, i % per))
    return pl.pallas_call(
        functools.partial(forward_kernel, masked, bq, bk),
        out_shape=(
            jax.ShapeDtypeStruct((chunks, HD, chunk), F32),
            jax.ShapeDtypeStruct((chunks, HD, chunk), BF16),
            jax.ShapeDtypeStruct((chunks, 1, chunk), F32),
        ),
        grid_spec=pltpu.PrefetchScalarGridSpec(
            num_scalar_prefetch=1,
            grid=(length // bq,),
            in_specs=[
                pl.BlockSpec((1, HD, bq), lambda i, p: (i // per, q_part, i % per)),
                whole(k_part),
                whole(v_part),
            ],
            out_specs=[mine(HD), mine(HD), mine(1)],
            scratch_shapes=[
                pltpu.VMEM((length // bk, bk, HD), BF16),
                pltpu.VMEM((length // bk, HD + 16, bk), BF16),
                pltpu.VMEM((HD + 16, bq), F32),
                pltpu.VMEM((1, bq), F32),
            ],
        ),
        cost_estimate=pl.CostEstimate(
            flops=4 * HD * length * length, transcendentals=length * length, bytes_accessed=14 * HD * length
        ),
        name="attend_self" if masked else "attend_cross",
    )(prefix, queries, pairs, pairs)


def backward_kernel(masked, bq, bk, prefix_ref, q_ref, g_ref, o_ref, lse_ref, k_ref, v_ref,
                    dq_ref, dk_ref, dv_ref, rows_q, rows_g, delta, dq_acc, dk_acc, dv_acc):
    chunks, _, chunk = q_ref.shape
    per = chunk // bq
    blocks = chunks * per
    step = pl.program_id(0)
    prefix = prefix_ref[0]

    @pl.when(step == 0)
    def _():
        for c in range(chunks):
            for b in range(per):
                i = c * per + b
                at = slice(b * bq, (b + 1) * bq)
                grad = g_ref[c, :, at]
                rows_q[i] = q_ref[c, :, at].T
                rows_g[i] = grad.T
                delta[i] = jnp.sum(grad.astype(F32) * o_ref[c, :, at], axis=0, keepdims=True)
        dq_acc[...] = jnp.zeros(dq_acc.shape, F32)

    first_key = step * bk
    key_cols = k_ref[0]
    key_rows = key_cols.T
    value_rows = v_ref[0].T
    dk_acc[...] = jnp.zeros(dk_acc.shape, F32)
    dv_acc[...] = jnp.zeros(dv_acc.shape, F32)

    def visit(i, use_mask):
        c, at = i // per, pl.ds(pl.multiple_of((i % per) * bq, bq), bq)
        scores = dot_nn(key_rows, q_ref[c, :, at])
        if use_mask:
            scores = jnp.where(allowed_mask(first_key, i * bq, prefix, scores.shape), scores, NEGATIVE)
        probs = jnp.exp(scores - lse_ref[c, :, at])
        dprobs = dot_nn(value_rows, g_ref[c, :, at])
        dscore = (probs * (dprobs - delta[i])).astype(BF16)
        dv_acc[...] += dot_nn(probs.astype(BF16), rows_g[i])
        dk_acc[...] += dot_nn(dscore, rows_q[i])
        dq_acc[i] += dot_nn(key_cols, dscore)

    if masked:
        inside = first_key + bk <= prefix
        start = jnp.where(first_key < prefix, 0, first_key // bq)
        free = jnp.where(inside, 0, jnp.minimum((first_key + bk - 1 + bq - 1) // bq, blocks))
        lax.fori_loop(start, free, lambda i, c: (visit(i, True), c)[1], 0)
        lax.fori_loop(jnp.maximum(start, free), blocks, lambda i, c: (visit(i, False), c)[1], 0)
    else:
        lax.fori_loop(0, blocks, lambda i, c: (visit(i, False), c)[1], 0)
    dk_ref[0] = dk_acc[...].T.astype(BF16)
    dv_ref[0] = dv_acc[...].T.astype(BF16)

    @pl.when(step == pl.num_programs(0) - 1)
    def _():
        for c in range(chunks):
            for b in range(per):
                low = dq_acc[c * per + b].astype(BF16)
                dq_ref[c, :, b * bq:(b + 1) * bq] = low * jnp.asarray(HD ** -0.5, BF16)


def flash_backward(prefix, queries, q_part, pairs, k_part, v_part, grads, outputs, lse, masked, bq=1024, bk=1024):
    chunks, _, chunk = queries.shape
    length = chunks * chunk
    per = chunk // bk
    whole = lambda part, rows=HD: pl.BlockSpec((chunks, rows, chunk), lambda i, p: (0, part, 0))
    mine = lambda part: pl.BlockSpec((1, HD, bk), lambda i, p: (i // per, part, i % per))
    shape = jax.ShapeDtypeStruct((chunks, HD, chunk), BF16)
    return pl.pallas_call(
        functools.partial(backward_kernel, masked, bq, bk),
        out_shape=(shape, shape, shape),
        grid_spec=pltpu.PrefetchScalarGridSpec(
            num_scalar_prefetch=1,
            grid=(length // bk,),
            in_specs=[whole(q_part), whole(0), whole(0), whole(0, 1), mine(k_part), mine(v_part)],
            out_specs=[whole(0), mine(0), mine(0)],
            scratch_shapes=[
                pltpu.VMEM((length // bq, bq, HD), BF16),
                pltpu.VMEM((length // bq, bq, HD), BF16),
                pltpu.VMEM((length // bq, 1, bq), F32),
                pltpu.VMEM((length // bq, HD, bq), F32),
                pltpu.VMEM((bk, HD), F32),
                pltpu.VMEM((bk, HD), F32),
            ],
        ),
        cost_estimate=pl.CostEstimate(
            flops=10 * HD * length * length, transcendentals=length * length, bytes_accessed=20 * HD * length
        ),
        name="attend_self_back" if masked else "attend_cross_back",
    )(prefix, queries, grads, outputs, lse, pairs, pairs)


EPSILON = 1e-05
SCALE = HD ** -0.5


def contract(left, right, left_dim, right_dim):
    return lax.dot_general(
        left, right, (((left_dim,), (right_dim,)), ((), ())), preferred_element_type=F32
    )


class Layout:
    def __init__(self, sizes):
        self.sizes = sizes
        keep = lambda names: tuple(n for n in names if sizes[n] > 1) or names[-1:]
        self.team = ("rx", "rc")
        self.cols = keep(("sq", "cs"))
        self.ring = keep(("rb", "cs"))
        self.every = ("dp", "rb", "rx", "rc", "sq", "cs")

    def count(self, names):
        total = 1
        for name in names:
            total *= self.sizes[name]
        return total

    def me(self):
        return lax.axis_index("rx") * 2 + lax.axis_index("rc")

    def swap(self, value, bits):
        if bits == 1:
            return lax.ppermute(value, "rc", [(0, 1), (1, 0)])
        if bits == 2:
            return lax.ppermute(value, "rx", [(0, 1), (1, 0)])
        return lax.ppermute(value, self.team, [(i, i ^ 3) for i in range(4)])

    def place(self, parts, spots):
        out = jnp.zeros((len(parts),) + parts[0].shape, parts[0].dtype)
        for part, spot in zip(parts, spots):
            out = lax.dynamic_update_index_in_dim(out, part, spot, 0)
        return out

    def team_gather(self, value):
        me = self.me()
        core, across = self.swap(value, 1), self.swap(value, 2)
        diagonal = self.swap(across, 1)
        return self.place([value, core, across, diagonal], [me, me ^ 1, me ^ 2, me ^ 3])

    def team_exchange(self, blocks):
        me = self.me()
        pick = lambda bits: lax.dynamic_index_in_dim(blocks, me ^ bits, 0, keepdims=False)
        parts = [pick(0)] + [self.swap(pick(bits), bits) for bits in (1, 2, 3)]
        return self.place(parts, [me, me ^ 1, me ^ 2, me ^ 3])

    def team_reduce(self, blocks):
        rx, rc = lax.axis_index("rx"), lax.axis_index("rc")
        grid = blocks.reshape((2, 2) + blocks.shape[1:])
        away = lax.dynamic_index_in_dim(grid, 1 - rc, 1, keepdims=False).astype(BF16)
        home = lax.dynamic_index_in_dim(grid, rc, 1, keepdims=False) + self.swap(away, 1).astype(F32)
        away = lax.dynamic_index_in_dim(home, 1 - rx, 0, keepdims=False).astype(BF16)
        return lax.dynamic_index_in_dim(home, rx, 0, keepdims=False) + self.swap(away, 2).astype(F32)

    def ring_index(self):
        return lax.axis_index("cs") * self.sizes["rb"] + lax.axis_index("rb")

    def flip(self, blocks, first, second):
        first, second = self.sizes[first], self.sizes[second]
        if first == 1 or second == 1:
            return blocks
        return blocks.reshape((first, second) + blocks.shape[1:]).swapaxes(0, 1).reshape(blocks.shape)

    def ring_exchange(self, blocks):
        blocks = lax.all_to_all(self.flip(blocks, "cs", "rb"), self.ring, 0, 0, tiled=True)
        return self.flip(blocks, "rb", "cs")

    def ring_trickle(self, blocks):
        size = self.count(self.ring)
        me = lax.axis_index(self.ring)
        blocks = self.flip(blocks, "cs", "rb")
        pick = lambda step: lax.dynamic_index_in_dim(blocks, (me + step) % size, 0, keepdims=False)
        parts, spots = [pick(0)], [me]
        for step in range(1, size):
            parts.append(lax.ppermute(pick(step), self.ring, [(i, (i + step) % size) for i in range(size)]))
            spots.append((me + size - step) % size)
        return self.flip(self.place(parts, spots), "rb", "cs")

    def block_sum(self, value):
        return lax.psum_scatter(value, self.cols, scatter_dimension=0, tiled=True)

    def halves(self, value):
        if self.sizes["rb"] == 1:
            return value
        return lax.all_to_all(value, "rb", 0, 1, tiled=True)

    def unhalves(self, value):
        if self.sizes["rb"] == 1:
            return value
        return lax.all_to_all(value, "rb", 1, 0, tiled=True)

    def feature_blocks(self, value):
        rb = self.sizes["rb"]
        parts = value.reshape(value.shape[0], rb, 4, -1).transpose(2, 0, 1, 3)
        return parts.reshape(4, value.shape[0], -1)

    def join_features(self, blocks):
        rb = self.sizes["rb"]
        count = blocks.shape[1]
        return blocks.reshape(4, count, rb, -1).transpose(1, 2, 0, 3).reshape(count, -1)

    def weight(self, blocks):
        mine = self.team_exchange(blocks).transpose(1, 0, 2)
        mine = mine.reshape(mine.shape[0], -1)
        if self.sizes["rb"] > 1:
            mine = lax.all_gather(mine, "rb", axis=1, tiled=True)
        return lax.all_gather(mine, self.cols, axis=0, tiled=True)

    def weight_grad(self, partial):
        total = self.block_sum(partial.astype(BF16))
        if self.sizes["rb"] > 1:
            total = lax.psum_scatter(total, "rb", scatter_dimension=1, tiled=True)
        blocks = total.reshape(total.shape[0], 4, -1).transpose(1, 0, 2)
        low = self.team_exchange(blocks)
        if self.sizes["dp"] == 2:
            return low.astype(F32) + lax.ppermute(low, "dp", [(0, 1), (1, 0)]).astype(F32)
        return lax.psum(low.astype(F32), "dp")


def norm_forward(hidden, gain_row, shift_row):
    average = jnp.mean(hidden, axis=1, keepdims=True)
    square = jnp.mean(hidden * hidden, axis=1, keepdims=True)
    inverse = lax.rsqrt(square - average * average + EPSILON)
    normed = (hidden - average) * inverse
    return normed * gain_row + shift_row, normed, inverse


def norm_backward(upstream, normed, inverse, gain_row):
    scaled = upstream * gain_row
    first = jnp.mean(scaled, axis=1, keepdims=True)
    second = jnp.mean(scaled * normed, axis=1, keepdims=True)
    grad = inverse * (scaled - first - normed * second)
    return grad, jnp.sum(upstream * normed, axis=0), jnp.sum(upstream, axis=0)


def exact_gelu(inputs):
    return jax.nn.gelu(inputs, approximate=False)


def column_rows(weight):
    features, parts, width = weight.shape
    blocks = weight.reshape(features, parts, 4, width // 4).transpose(2, 1, 3, 0)
    return blocks.reshape(4, -1, features)


def column_rows_back(blocks, parts):
    features = blocks.shape[2]
    return blocks.reshape(4, parts, -1, features).transpose(3, 1, 0, 2).reshape(features, parts, -1)


def shards(
    layout, tokens, encoder, cotangent, prefixes, selfqkv, selfbias, selfproj, selfshift, crossquery,
    crosskv, crossbias, crossproj, crossshift, upweight, upbias, downweight, downbias, normgain, normshift,
):
    me = layout.me()
    split_rows = lambda weight: weight.reshape(4, -1, weight.shape[1])
    qkv_w = layout.weight(column_rows(selfqkv))
    tokens_all = layout.join_features(layout.team_gather(layout.halves(tokens)))
    width = tokens_all.shape[1]
    group = tokens_all.shape[0]
    own_rows = group // 4
    columns = layout.count(layout.cols)
    heads = columns

    by_col = jnp.concatenate([selfbias.reshape(-1), crossbias.reshape(-1), upbias])
    by_col = lax.all_gather(by_col, layout.cols, axis=0, tiled=False).reshape(columns, -1)
    block = selfbias.shape[1]
    head_biases = lax.dynamic_index_in_dim(
        by_col[:, : 4 * block].reshape(columns, 4, 4, HD), me, 2, keepdims=False
    )
    up_bias = lax.dynamic_index_in_dim(
        by_col[:, 4 * block:].reshape(columns, 4, -1), me, 1, keepdims=False
    ).reshape(1, -1)
    by_row = jnp.concatenate([selfshift[None], crossshift[None], downbias[None], normgain, normshift])
    by_row = lax.all_gather(by_row, ("rb", "rx", "rc"), axis=1, tiled=True)
    self_shift, cross_shift, down_bias = by_row[0], by_row[1], by_row[2]
    gains, shifts = by_row[3:6], by_row[6:9]

    def gather_tokens(own):
        return layout.team_gather(own).reshape(group, width)

    def reduce_tokens(partial):
        return layout.team_reduce(partial.reshape(4, own_rows, width))

    sequence_prefix = prefixes
    if layout.sizes["sq"] > 1:
        sequence_prefix = lax.dynamic_slice_in_dim(prefixes, lax.axis_index("sq"), 1, 0)

    qkv = contract(qkv_w, tokens_all, 1, 1).reshape(heads, 3, HD, group)
    qkv_bias = jnp.stack([head_biases[:, 0], jnp.zeros_like(head_biases[:, 0]), head_biases[:, 1]], axis=1)
    factor = jnp.array([SCALE, 1.0, 1.0], F32)[None, :, None, None]
    qkv = ((qkv + qkv_bias[..., None]) * factor).astype(BF16).reshape(heads, 3 * HD, group)
    self_set = layout.ring_exchange(qkv)
    self_out, self_low, self_lse = flash_forward(sequence_prefix, self_set, 0, self_set, 1, 2, True)
    attended = layout.ring_exchange(self_low).reshape(heads * HD, group)

    self_w = layout.weight(split_rows(selfproj))
    encoder_all = layout.join_features(layout.team_gather(layout.halves(encoder)))
    kv_w = layout.weight(column_rows(crosskv))
    query_w = layout.weight(column_rows(crossquery[:, None]))
    cross_w = layout.weight(split_rows(crossproj))
    up_w = layout.weight(column_rows(upweight[:, None]))
    down_w = layout.weight(split_rows(downweight))
    pair = contract(kv_w, encoder_all, 1, 1).reshape(heads, 2, HD, group)
    pair_bias = jnp.stack([jnp.zeros_like(head_biases[:, 3]), head_biases[:, 3]], axis=1)
    pair = (pair + pair_bias[..., None]).astype(BF16).reshape(heads, 2 * HD, group)
    cross_set = layout.ring_trickle(pair)
    upstream = layout.join_features(
        layout.team_exchange(layout.halves(cotangent).reshape(4, own_rows, -1))
    ).astype(F32)

    own_tokens = lax.dynamic_slice_in_dim(tokens_all, me * own_rows, own_rows, 0).astype(F32)
    first_sum = own_tokens + (reduce_tokens(contract(attended, self_w, 0, 0)) + self_shift)
    first_out, first_normed, first_inverse = norm_forward(first_sum, gains[0], shifts[0])
    first_all = gather_tokens(first_out.astype(BF16))

    query = contract(query_w, first_all, 1, 1).reshape(heads, HD, group)
    query = ((query + head_biases[:, 2][..., None]) * SCALE).astype(BF16)
    cross_query = layout.ring_exchange(query)
    cross_out, cross_low, cross_lse = flash_forward(sequence_prefix, cross_query, 0, cross_set, 0, 1, False)
    crossed = layout.ring_exchange(cross_low).reshape(heads * HD, group)
    second_sum = first_out + (reduce_tokens(contract(crossed, cross_w, 0, 0)) + cross_shift)
    second_out, second_normed, second_inverse = norm_forward(second_sum, gains[1], shifts[1])
    second_all = gather_tokens(second_out.astype(BF16))

    hidden_pre = contract(second_all, up_w, 1, 1) + up_bias
    hidden_act = exact_gelu(hidden_pre).astype(BF16)
    third_sum = second_out + (reduce_tokens(contract(hidden_act, down_w, 1, 0)) + down_bias)
    third_out, third_normed, third_inverse = norm_forward(third_sum, gains[2], shifts[2])
    layer_out = third_out.astype(BF16)
    layer_out = layout.team_exchange(layout.feature_blocks(layer_out))
    layer_out = layout.unhalves(layer_out.reshape(group, -1))

    third_grad, third_gain, third_shift = norm_backward(upstream, third_normed, third_inverse, gains[2])
    down_own = third_grad.astype(BF16)
    down_all = gather_tokens(down_own)
    act_grad = contract(down_all, down_w, 1, 1)
    pre_low = jax.vjp(exact_gelu, hidden_pre)[1](act_grad)[0].astype(BF16)
    second_grad = third_grad + reduce_tokens(contract(pre_low, up_w, 1, 0))
    downweight_grad = layout.weight_grad(contract(hidden_act, down_all, 0, 0))
    upweight_grad = layout.weight_grad(contract(pre_low, second_all, 0, 0))
    mid_grad, second_gain, second_shift = norm_backward(second_grad, second_normed, second_inverse, gains[1])
    cross_own = mid_grad.astype(BF16)
    cross_all = gather_tokens(cross_own)
    crossed_grad = contract(cross_w, cross_all, 1, 1).astype(BF16).reshape(heads, HD, group)
    crossed_grad = layout.ring_exchange(crossed_grad)
    crossproj_grad = layout.weight_grad(contract(crossed, cross_all, 1, 0))
    dquery, dkeys, dvalues = flash_backward(
        sequence_prefix, cross_query, 0, cross_set, 0, 1, crossed_grad, cross_out, cross_lse, False
    )
    cross_bias_sums = (jnp.sum(dquery.astype(F32), axis=(0, 2)), jnp.sum(dvalues.astype(F32), axis=(0, 2)))
    dquery = layout.ring_exchange(dquery).reshape(heads * HD, group)
    first_grad = mid_grad + reduce_tokens(contract(dquery, query_w, 0, 0))
    dpair = layout.ring_trickle(jnp.concatenate([dkeys, dvalues], axis=1)).reshape(heads * 2 * HD, group)
    crossquery_grad = layout.weight_grad(contract(dquery, first_all, 1, 0))
    crosskv_grad = layout.weight_grad(contract(dpair, encoder_all, 1, 0))
    encoder_grad = layout.team_reduce(layout.feature_blocks(contract(dpair, kv_w, 0, 0)))
    encoder_grad = layout.unhalves(encoder_grad)
    low_grad, first_gain, first_shift = norm_backward(first_grad, first_normed, first_inverse, gains[0])
    self_own = low_grad.astype(BF16)
    self_all = gather_tokens(self_own)
    attended_grad = contract(self_w, self_all, 1, 1).astype(BF16).reshape(heads, HD, group)
    attended_grad = layout.ring_exchange(attended_grad)
    selfproj_grad = layout.weight_grad(contract(attended, self_all, 1, 0))
    dq, dk, dv = flash_backward(
        sequence_prefix, self_set, 0, self_set, 1, 2, attended_grad, self_out, self_lse, True
    )
    self_bias_sums = (jnp.sum(dq.astype(F32), axis=(0, 2)), jnp.sum(dv.astype(F32), axis=(0, 2)))
    dqkv = layout.ring_exchange(jnp.concatenate([dq, dk, dv], axis=1)).reshape(heads * 3 * HD, group)
    selfqkv_grad = layout.weight_grad(contract(dqkv, tokens_all, 1, 0))
    tokens_part = contract(dqkv, qkv_w, 0, 0)
    mine = lax.dynamic_slice_in_dim(tokens_part, me * own_rows, own_rows, 0) + low_grad
    tokens_part = lax.dynamic_update_slice_in_dim(tokens_part, mine, me * own_rows, 0)
    tokens_grad = layout.unhalves(layout.team_reduce(layout.feature_blocks(tokens_part)))

    def at_head(sums):
        spot = (layout.ring_index() * 4 + me) * HD
        return lax.dynamic_update_slice_in_dim(jnp.zeros((width,), F32), sums, spot, 0)

    up_sums = jnp.zeros((columns, 4, pre_low.shape[1] // columns), F32)
    up_sums = lax.dynamic_update_index_in_dim(
        up_sums, jnp.sum(pre_low.astype(F32), axis=0).reshape(columns, -1), me, 1
    )
    column_sum = lambda low: jnp.sum(low.astype(F32), axis=0)
    rows = jnp.stack([
        first_gain, second_gain, third_gain, first_shift, second_shift, third_shift,
        column_sum(self_own), column_sum(cross_own), column_sum(down_own),
        at_head(cross_bias_sums[0]), at_head(cross_bias_sums[1]),
    ])
    rows, up_sums = lax.psum((rows, up_sums), layout.every)
    late = lax.psum(jnp.stack([at_head(self_bias_sums[0]), at_head(self_bias_sums[1])]), layout.every)
    row_at = (lax.axis_index("rb") * 4 + me) * normgain.shape[1]
    col_at = lax.axis_index(layout.cols)
    by_row = lax.dynamic_slice_in_dim(rows[:9], row_at, normgain.shape[1], 1)
    crossbias_grad = lax.dynamic_slice_in_dim(rows[9:], col_at * block, block, 1)
    selfbias_grad = lax.dynamic_slice_in_dim(late, col_at * block, block, 1)
    upbias_grad = lax.dynamic_index_in_dim(up_sums, col_at, 0, keepdims=False).reshape(-1)
    join_rows = lambda blocks: blocks.reshape(-1, blocks.shape[2])
    return (
        layer_out,
        tokens_grad,
        encoder_grad,
        column_rows_back(selfqkv_grad, 3),
        selfbias_grad,
        join_rows(selfproj_grad),
        by_row[6],
        column_rows_back(crossquery_grad, 1)[:, 0],
        column_rows_back(crosskv_grad, 2),
        crossbias_grad,
        join_rows(crossproj_grad),
        by_row[7],
        column_rows_back(upweight_grad, 1)[:, 0],
        upbias_grad,
        join_rows(downweight_grad),
        by_row[8],
        by_row[:3],
        by_row[3:6],
    )


def solution(mesh):
    def run(*arrays):
        dp, row, col = (mesh.shape[name] for name in ("dp", "row", "col"))
        per_col = arrays[4].shape[2] // HD // col
        seqs = arrays[3].shape[0] // dp
        assert per_col == 4 and row % 4 == 0 and col % seqs == 0
        assert (row // 4) * (col // seqs) == col
        sizes = {"dp": dp, "rb": row // 4, "rx": 2, "rc": 2, "sq": seqs, "cs": col // seqs}
        grid = Mesh(mesh.devices.reshape(tuple(sizes.values())), tuple(sizes))
        rows, cols, tokens = ("rb", "rx", "rc"), ("sq", "cs"), ("dp", "sq", "cs")
        specs = {
            "tokens": P(tokens, rows), "rc": P(rows, cols), "cr": P(cols, rows), "r3c": P(rows, None, cols),
            "c": P(cols), "r": P(rows), "2c": P(None, cols), "2r": P(None, rows),
        }
        ins = (
            "tokens", "tokens", "tokens", "dp", "r3c", "2c", "cr", "r", "rc", "r3c", "2c", "cr", "r", "rc", "c", "cr", "r", "2r", "2r",
        )
        outs = (
            "tokens", "tokens", "tokens", "r3c", "2c", "cr", "r", "rc", "r3c", "2c", "cr", "r", "rc", "c", "cr", "r", "2r", "2r",
        )
        specs["dp"] = P("dp")
        body = functools.partial(shards, Layout(sizes))
        return jax.shard_map(
            body, mesh=grid, in_specs=tuple(specs[s] for s in ins), out_specs=tuple(specs[s] for s in outs),
            check_vma=False,
        )(*arrays)

    return run
```

time: 2860 us -> 1210 us (0.42)
  waiting for transfers between devices: 1870 us -> 399 us
  matrix products: 485 us -> 70.8 us
  other arithmetic: 273 us -> 42.5 us
  local copies, waits for them, and re-layouts: 120 us -> 331 us
  Pallas kernels: 0 us -> 133 us
  starting transfers between devices: 2.43 us -> 115 us
    reduce_scatter x16 -> x7, waiting for transfers between devices: 1120 us -> 28.6 us  [block_sum(): return lax.psum_scatter(value, self.cols, scatter_dimension=0, tiled=True)]
    all_gather x16 -> x4, waiting for transfers between devices: 638 us -> 35.9 us  [weight(): return lax.all_gather(mine, self.cols, axis=0, tiled=True)]
    dot_general x49 -> x21, matrix products: 485 us -> 70.8 us  [contract(): lax.dot_general(left, right, (((left_dim,), (right_dim,)), ((), ())), pre...]
    dynamic_update_slice x16 -> x100, local copies, waits for them, and re-layouts: 4.05 us -> 182 us  [the longest x94 180 us: place(): out = lax.dynamic_update_index_in_dim(out, part, spot, 0)]
    ppermute x0 -> x96, waiting for transfers between devices: none -> 154 us  [the longest x30 105 us: swap(): return lax.ppermute(value, 'rx', [(0, 1), (1, 0)])]
    convert_element_type x19 -> x1, other arithmetic: 152 us -> 0.14 us  [shards(): upstream = layout.join_features(layout.team_exchange(layout.halves(cotang...]
    pallas_call x0 -> x4, Pallas kernels: none -> 133 us  [the longest x2 81.5 us: flash_backward(): pl.pallas_call(functools.partial(backward_kernel, masked, bq, bk), out_sh...]
    all_gather x0 -> x5, blocking collectives: none -> 84.4 us  [the longest x3 65.8 us: weight(): return lax.all_gather(mine, self.cols, axis=0, tiled=True)]
  transfers between devices with their start and end apart: 33 -> 116, of which waited for: 32 -> 35; matrix products, arithmetic and copies ran while one was open for 4% -> 32% of each run, Pallas kernels for 0% -> 11%
where the time goes in v1:
time: 1210 us; the launch traced here: 1190 us
  waiting for transfers between devices  399 us (33%)
  local copies, waits for them, and re-layouts  331 us (27%)
  Pallas kernels  133 us (11%)
  starting transfers between devices  115 us (10%)
  blocking collectives  84.4 us (7%)
  matrix products  70.8 us (6%)
  other arithmetic  42.5 us (4%)
  between operations  17.9 us (1%)
    dynamic_update_slice x94, local copies, waits for them, and re-layouts, place(): out = lax.dynamic_update_index_in_dim(out, part, spot, 0)  180 us
    ppermute x30, waiting for transfers between devices, swap(): return lax.ppermute(value, 'rx', [(0, 1), (1, 0)])  105 us
    psum x1, waiting for transfers between devices, shards(): lax.psum(jnp.stack([at_head(self_bias_sums[0]), at_head(self_bias_sums[1]...  99.3 us
    pallas_call x2, Pallas kernels, flash_backward(): pl.pallas_call(functools.partial(backward_kernel, masked, bq, bk), out_sh...  81.5 us
    all_to_all x8, waiting for transfers between devices, ring_exchange(): lax.all_to_all(self.flip(blocks, 'cs', 'rb'), self.ring, 0, 0, tiled=True)  81.2 us
    dot_general x21, matrix products, contract(): lax.dot_general(left, right, (((left_dim,), (right_dim,)), ((), ())), pre...  70.8 us
    all_gather x3, blocking collectives, weight(): return lax.all_gather(mine, self.cols, axis=0, tiled=True)  65.8 us
    pallas_call x2, Pallas kernels, flash_forward(): pl.pallas_call(functools.partial(forward_kernel, masked, bq, bk), out_sha...  51 us
  transfers between devices with their start and end apart: 116, of which 35 were waited for; matrix products, arithmetic and copies ran while one was open for 32% of the time, Pallas kernels for 11%

profile of v1, /device:TPU:0, one launch (start us, length us, event | category | flops | bytes accessed | tf_op | source)
XLA Modules:
  0.0 1193.2 jit_solution(13930981332135533742)
XLA Ops:
  11.8 3.6 collective-permute-done.4
  19.4 13.4 %all-gather = f32[8192]{0:T(1024)S(1)} all-gather(f32[2048]{0:T(1024)S(1)} %pad_maximum_fusion.1), channel_id=2, replica_groups=mesh['dp'=2,'rb'=1,'rx'=2,'rc'=2,'sq'=1,'cs'=4] {'cs'}, dimensions={0}, use_global_device_ids=true | all-gather | bytes 40960 | tf_op jit(solution)/shard_map/all_gather | solution.py:369
  36.0 13.4 %dynamic_update_slice.342 = bf16[4,1024,1,256]{3,0,1,2:T(4,128)(2,1)S(1)} dynamic-update-slice(bf16[4,1024,1,256]{3,0,1,2:T(4,128)(2,1)S(1)} %reshape.486.clone, bf16[1,1024,1,256]{3,0,1,2:T(2,128)(2,1)S(1)} %copy.256, s32[]{:T(128)S(6)} %select_n.305, s32[]{:T(128)} %constant.617.clone.1, s32[]{:T(128)} %constant.617.clone.1, s32[]{:T(128)} %constant.617.clone.1) | dynamic-update-slice | bytes 1048580 | tf_op jit(solution)/shard_map/jit(dynamic_update_index_in_dim)/dynamic_update_slice | solution.py:235
  54.8 13.3 %dynamic_update_slice.343 = bf16[4,1024,1,256]{3,0,1,2:T(4,128)(2,1)S(1)} dynamic-update-slice(bf16[4,1024,1,256]{3,0,1,2:T(4,128)(2,1)S(1)} %dynamic_update_slice.342, bf16[1,1024,1,256]{3,0,1,2:T(2,128)(2,1)S(1)} %copy.257, s32[]{:T(128)S(6)} %select_n.306, s32[]{:T(128)} %constant.617.clone.1, s32[]{:T(128)} %constant.617.clone.1, s32[]{:T(128)} %constant.617.clone.1) | dynamic-update-slice | bytes 1048580 | tf_op jit(solution)/shard_map/jit(dynamic_update_index_in_dim)/dynamic_update_slice | solution.py:235
  68.2 19.0 %dynamic_update_slice.344 = bf16[4,1024,1,256]{3,0,1,2:T(4,128)(2,1)S(1)} dynamic-update-slice(bf16[4,1024,1,256]{3,0,1,2:T(4,128)(2,1)S(1)} %dynamic_update_slice.343, bf16[1,1024,1,256]{3,0,1,2:T(2,128)(2,1)} %copy.258, s32[]{:T(128)S(6)} %select_n.307, s32[]{:T(128)} %constant.617.clone.1, s32[]{:T(128)} %constant.617.clone.1, s32[]{:T(128)} %constant.617.clone.1) | dynamic-update-slice | bytes 1048580 | tf_op jit(solution)/shard_map/jit(dynamic_update_index_in_dim)/dynamic_update_slice | solution.py:235
  89.0 13.4 %dynamic_update_slice.345 = bf16[4,1024,1,256]{3,0,1,2:T(4,128)(2,1)S(1)} dynamic-update-slice(bf16[4,1024,1,256]{3,0,1,2:T(4,128)(2,1)S(1)} %dynamic_update_slice.344, bf16[1,1024,1,256]{3,0,1,2:T(2,128)(2,1)S(1)} %copy.259, s32[]{:T(128)S(6)} %select_n.308, s32[]{:T(128)} %constant.617.clone.1, s32[]{:T(128)} %constant.617.clone.1, s32[]{:T(128)} %constant.617.clone.1) | dynamic-update-slice | bytes 1048580 | tf_op jit(solution)/shard_map/jit(dynamic_update_index_in_dim)/dynamic_update_slice | solution.py:235
  105.1 5.1 multiply_convert_fusion.1
  110.2 5.2 all-to-all-start
  118.8 34.3 %all-to-all-done.q_ref.k_ref.v_ref = bf16[4,192,1024]{2,1,0:T(8,128)(2,1)} async-done(((bf16[4,192,1024]{2,1,0:T(8,128)(2,1)}), bf16[4,192,1024]{2,1,0:T(8,128)(2,1)}, u32[]{:S(2)}, u32[]{:S(2)}) %all-to-all-start) | async-done | bytes 1572896 | tf_op jit(solution)/shard_map/all_to_all | solution.py:268
  153.1 20.7 %attend_self.1 = (f32[4,64,1024]{2,1,0:T(8,128)}, bf16[4,64,1024]{2,1,0:T(8,128)(2,1)}, f32[4,1,1024]{2,1,0:T(1,128)}) custom-call(s32[1]{0:T(128)S(6)} %copy.589.prefix_ref, bf16[4,192,1024]{2,1,0:T(8,128)(2,1)} %all-to-all-done.q_ref.k_ref.v_ref, bf16[4,192,1024]{2,1,0:T(8,128)(2,1)} %all-to-all-done.q_ref.k_ref.v_ref, ...), custom_call_target="tpu_custom_call" | custom-call | flops 4294967296 | bytes 3670016 | tf_op jit(solution)/shard_map/attend_self/pallas_call | solution.py:78
  173.8 3.5 all-to-all-start.1
  177.5 24.5 %all_gather.33 = bf16[256,1024]{1,0:T(8,128)(2,1)S(1)} all-gather(bf16[64,1024]{1,0:T(8,128)(2,1)S(1)} %bitcast.701), channel_id=1, replica_groups=mesh['dp'=2,'rb'=1,'rx'=2,'rc'=2,'sq'=1,'cs'=4] {'cs'}, dimensions={0}, use_global_device_ids=true | all-gather | bytes 655360 | tf_op jit(solution)/shard_map/all_gather | solution.py:310
  218.9 21.3 %dynamic_update_slice.366 = bf16[4,1024,1,256]{3,0,1,2:T(4,128)(2,1)} dynamic-update-slice(bf16[4,1024,1,256]{3,0,1,2:T(4,128)(2,1)} %reshape.486.clone.1, bf16[1,1024,1,256]{3,0,1,2:T(2,128)(2,1)S(1)} %copy.274, s32[]{:T(128)S(6)} %select_n.305, s32[]{:T(128)} %constant.617.clone.1, s32[]{:T(128)} %constant.617.clone.1, s32[]{:T(128)} %constant.617.clone.1) | dynamic-update-slice | bytes 1048580 | tf_op jit(solution)/shard_map/jit(dynamic_update_index_in_dim)/dynamic_update_slice | solution.py:235
  240.9 5.2 all_gather.34
  260.1 5.5 collective-permute-done.12
  267.0 10.3 collective-permute-done.10
  280.8 18.1 %all_gather.35 = bf16[256,1024]{1,0:T(8,128)(2,1)} all-gather(bf16[64,1024]{1,0:T(8,128)(2,1)S(1)} %bitcast.700), channel_id=1, replica_groups=mesh['dp'=2,'rb'=1,'rx'=2,'rc'=2,'sq'=1,'cs'=4] {'cs'}, dimensions={0}, use_global_device_ids=true | all-gather | bytes 655360 | tf_op jit(solution)/shard_map/all_gather | solution.py:310
  304.6 18.9 %dynamic_update_slice.367 = bf16[4,1024,1,256]{3,0,1,2:T(4,128)(2,1)S(1)} dynamic-update-slice(bf16[4,1024,1,256]{3,0,1,2:T(4,128)(2,1)S(1)} %copy-done, bf16[1,1024,1,256]{3,0,1,2:T(2,128)(2,1)} %copy.275, s32[]{:T(128)S(6)} %select_n.306, s32[]{:T(128)} %constant.617.clone.1, s32[]{:T(128)} %constant.617.clone.1, s32[]{:T(128)} %constant.617.clone.1) | dynamic-update-slice | bytes 1048580 | tf_op jit(solution)/shard_map/jit(dynamic_update_index_in_dim)/dynamic_update_slice | solution.py:235
  323.5 19.0 %dynamic_update_slice.368 = bf16[4,1024,1,256]{3,0,1,2:T(4,128)(2,1)S(1)} dynamic-update-slice(bf16[4,1024,1,256]{3,0,1,2:T(4,128)(2,1)S(1)} %dynamic_update_slice.367, bf16[1,1024,1,256]{3,0,1,2:T(2,128)(2,1)} %copy.276, s32[]{:T(128)S(6)} %select_n.307, s32[]{:T(128)} %constant.617.clone.1, s32[]{:T(128)} %constant.617.clone.1, s32[]{:T(128)} %constant.617.clone.1) | dynamic-update-slice | bytes 1048580 | tf_op jit(solution)/shard_map/jit(dynamic_update_index_in_dim)/dynamic_update_slice | solution.py:235
  345.3 18.9 %dynamic_update_slice.369 = bf16[4,1024,1,256]{3,0,1,2:T(4,128)(2,1)S(1)} dynamic-update-slice(bf16[4,1024,1,256]{3,0,1,2:T(4,128)(2,1)S(1)} %dynamic_update_slice.368, bf16[1,1024,1,256]{3,0,1,2:T(2,128)(2,1)} %copy.277, s32[]{:T(128)S(6)} %select_n.308, s32[]{:T(128)} %constant.617.clone.1, s32[]{:T(128)} %constant.617.clone.1, s32[]{:T(128)} %constant.617.clone.1) | dynamic-update-slice | bytes 1048580 | tf_op jit(solution)/shard_map/jit(dynamic_update_index_in_dim)/dynamic_update_slice | solution.py:235
  382.1 3.5 all-to-all-start.2
  386.5 3.8 collective-permute-start.25
  391.3 10.7 collective-permute-done.24
  404.6 4.9 collective-permute-start.35
  411.2 30.3 %attend_cross.1 = (f32[4,64,1024]{2,1,0:T(8,128)}, bf16[4,64,1024]{2,1,0:T(8,128)(2,1)}, f32[4,1,1024]{2,1,0:T(1,128)}) custom-call(s32[1]{0:T(128)S(6)} %copy.589.prefix_ref, bf16[4,64,1024]{2,1,0:T(8,128)(2,1)} %copy-done.46, bf16[4,128,1024]{2,1,0:T(8,128)(2,1)} %copy-done.42, bf16[4,128,1024]{2,1,0:T(8,128)(2,1)} %copy-done.42), custom_call_target="tpu_custom_call" | custom-call | flops 4294967296 | bytes 3670016 | tf_op jit(solution)/shard_map/attend_cross/pallas_call | solution.py:78
  441.6 6.9 all-to-all-start.3
  450.9 23.2 %all_gather.37 = bf16[256,1024]{1,0:T(8,128)(2,1)S(1)} all-gather(bf16[64,1024]{1,0:T(8,128)(2,1)S(1)} %bitcast.702), channel_id=1, replica_groups=mesh['dp'=2,'rb'=1,'rx'=2,'rc'=2,'sq'=1,'cs'=4] {'cs'}, dimensions={0}, use_global_device_ids=true | all-gather | bytes 655360 | tf_op jit(solution)/shard_map/all_gather | solution.py:310
  489.4 9.8 collective-permute-done.30
  507.5 8.9 collective-permute-done.32
  522.0 4.3 all-gather.10.cloned.1.call-done
  526.3 15.0 %multiply_convert_fusion = (bf16[1024,1024]{1,0:T(8,128)(2,1)}, f32[1024,1024]{1,0:T(8,128)}, f32[1024,1024]{1,0:T(8,128)}) fusion(f32[1024]{0:T(1024)S(1)} %bitcast.781, bf16[1024,1024]{1,0:T(8,128)(2,1)} %bitcast.112, bf16[1024,1024]{0,1:T(8,128)(2,1)} %all-gather.10.cloned.1.call-done), kind=kOutput, calls=%fused_computation.4 | convolution fusion | flops 2216689664 | bytes 14684160 | tf_op jit(solution)/shard_map/dot_general | solution.py:202
  541.3 31.5 %all-gather.12.cloned.1.call-done = bf16[1024,1024]{0,1:T(8,128)(2,1)} async-done(((bf16[256,1024]{0,1:T(8,128)(2,1)}), bf16[1024,1024]{0,1:T(8,128)(2,1)}) %all-gather.12.cloned.1.call-update) | async-done | bytes 2097168 | tf_op jit(solution)/shard_map/all_gather | solution.py:310
  572.9 4.6 fusion.74
  586.1 3.4 dynamic_update_slice.394
  590.1 3.4 dynamic_update_slice.395
  593.5 3.4 dynamic_update_slice.396
  596.9 3.8 dynamic_update_slice.397
  606.9 13.3 %collective-permute-done.49 = bf16[256,1024]{1,0:T(8,128)(2,1)S(1)} collective-permute-done((bf16[256,1024]{1,0:T(8,128)(2,1)S(1)}, bf16[256,1024]{1,0:T(8,128)(2,1)S(1)}, u32[]{:S(2)}, u32[]{:S(2)}) %collective-permute-start.49) | collective-permute-done | bytes 524320 | tf_op jit(solution)/shard_map/ppermute | solution.py:229
  623.1 3.7 convert_reduce_fusion
  634.0 13.7 %collective-permute-done.52 = bf16[256,1024]{1,0:T(8,128)(2,1)S(1)} collective-permute-done((bf16[256,1024]{1,0:T(8,128)(2,1)S(1)}, bf16[256,1024]{1,0:T(8,128)(2,1)S(1)}, u32[]{:S(2)}, u32[]{:S(2)}) %collective-permute-start.52) | collective-permute-done | bytes 524320 | tf_op jit(solution)/shard_map/ppermute | solution.py:229
  651.3 12.8 %collective-permute-done.54 = bf16[256,1024]{1,0:T(8,128)(2,1)S(1)} collective-permute-done((bf16[256,1024]{1,0:T(8,128)(2,1)S(1)}, bf16[256,1024]{1,0:T(8,128)(2,1)S(1)}, u32[]{:S(2)}, u32[]{:S(2)}) %collective-permute-start.54) | collective-permute-done | bytes 524320 | tf_op jit(solution)/shard_map/ppermute | solution.py:229
  669.2 5.3 convolution_convert_fusion
  676.2 5.3 convolution_convert_fusion.1
  690.1 3.1 convolution_convert_fusion.8
  693.2 3.5 all-to-all-start.4
  698.0 28.6 %all-to-all-done.4.g_ref = bf16[4,64,1024]{2,1,0:T(8,128)(2,1)S(1)} async-done(((bf16[4,64,1024]{2,1,0:T(8,128)(2,1)}), bf16[4,64,1024]{2,1,0:T(8,128)(2,1)S(1)}, u32[]{:S(2)}, u32[]{:S(2)}) %all-to-all-start.4) | async-done | bytes 524320 | tf_op jit(solution)/shard_map/all_to_all | solution.py:268
  727.3 48.2 %attend_cross_back.1 = (bf16[4,64,1024]{2,1,0:T(8,128)(2,1)}, bf16[4,64,1024]{2,1,0:T(8,128)(2,1)}, bf16[4,64,1024]{2,1,0:T(8,128)(2,1)}) custom-call(s32[1]{0:T(128)S(6)} %copy.589.prefix_ref, bf16[4,64,1024]{2,1,0:T(8,128)(2,1)} %copy-done.46, bf16[4,64,1024]{2,1,0:T(8,128)(2,1)} %copy-done.47, f32[4,64,1024]{2,1,0:T(8,128)} %get-tuple-element.32.o_ref, ...), custom_call_target="tpu_custom_call" | custom-call | flops 10737418240 | bytes 5242880 | tf_op jit(solution)/shard_map/attend_cross_back/pallas_call | solution.py:173
  779.7 5.1 all-to-all-start.5
  799.1 16.7 %collective-permute-done.64 = bf16[128,1024]{1,0:T(8,128)(2,1)} collective-permute-done((bf16[128,1024]{1,0:T(8,128)(2,1)}, bf16[128,1024]{1,0:T(8,128)(2,1)}, u32[]{:S(2)}, u32[]{:S(2)}) %collective-permute-start.64) | collective-permute-done | bytes 262176 | tf_op jit(solution)/shard_map/ppermute | solution.py:278
  866.1 9.7 collective-permute-done.57
  882.0 9.6 collective-permute-done.59
  895.1 8.4 all-to-all-start.6
  918.4 33.3 %attend_self_back.1 = (bf16[4,64,1024]{2,1,0:T(8,128)(2,1)}, bf16[4,64,1024]{2,1,0:T(8,128)(2,1)}, bf16[4,64,1024]{2,1,0:T(8,128)(2,1)}) custom-call(s32[1]{0:T(128)S(6)} %copy.589.prefix_ref, bf16[4,192,1024]{2,1,0:T(8,128)(2,1)} %all-to-all-done.q_ref.k_ref.v_ref, bf16[4,64,1024]{2,1,0:T(8,128)(2,1)} %all-to-all-done.6.g_ref, ...), custom_call_target="tpu_custom_call" | custom-call | flops 10737418240 | bytes 5242880 | tf_op jit(solution)/shard_map/attend_self_back/pallas_call | solution.py:173
  954.3 4.4 all-to-all-start.7
  961.1 3.3 collective-permute-start.79
  979.1 17.0 %all-to-all-done.7 = bf16[4,192,1024]{2,1,0:T(8,128)(2,1)} async-done(((bf16[4,192,1024]{2,1,0:T(8,128)(2,1)}), bf16[4,192,1024]{2,1,0:T(8,128)(2,1)}, u32[]{:S(2)}, u32[]{:S(2)}) %all-to-all-start.7) | async-done | bytes 1572896 | tf_op jit(solution)/shard_map/all_to_all | solution.py:268
  996.1 4.4 convolution_convert_fusion.2
  1002.7 99.3 %all-reduce.4.cloned.1.call-done = (f32[2,1024]{1,0:T(2,128)}, f32[11,1024]{1,0:T(8,128)}, f32[4,4,256]{2,1,0:T(4,128)}) async-done(((f32[2,1024]{1,0:T(2,128)}, f32[11,1024]{1,0:T(8,128)}, f32[4,4,256]{2,1,0:T(4,128)}), (f32[2,1024]{1,0:T(2,128)}, f32[11,1024]{1,0:T(8,128)}, f32[4,4,256]{2,1,0:T(4,128)})) %all-reduce.4.cloned.1.call-update) | async-done | bytes 69648 | tf_op jit(solution)/shard_map/psum | solution.py:494
  1106.8 3.3 fusion.76
  1115.0 5.4 copy.309
  1124.1 4.4 reduce-scatter.10.cloned.1.call-done
  1140.1 24.2 %reduce-scatter.8.cloned.1.call-done = bf16[192,1024]{1,0:T(8,128)(2,1)} async-done(((bf16[768,1024]{1,0:T(8,128)(2,1)}), bf16[192,1024]{1,0:T(8,128)(2,1)}) %reduce-scatter.8.cloned.1.call-update) | async-done | bytes 393232 | tf_op jit(solution)/shard_map/reduce_scatter | solution.py:283
  1168.6 3.7 collective-permute-done.69
  1177.8 7.0 collective-permute-done.71
  (734 shorter events, 320.9 us)
Async XLA Ops:
  7.2 97.9 %all-gather.6.cloned.1.call-start = ((), (), s32[]{:S(2)}) async-start(), calls=%async_computation.15 | async-start | bytes 1966080 | tf_op jit(solution)/shard_map/all_gather | solution.py:310
  17.8 31.7 %collective-permute-start.1 = (bf16[1024,256]{1,0:T(8,128)(2,1)}, bf16[1024,256]{1,0:T(8,128)(2,1)}, u32[]{:S(2)}, u32[]{:S(2)}) collective-permute-start(bf16[1024,256]{1,0:T(8,128)(2,1)} %param.20), channel_id=1, source_target_pairs={{0,8},{8,0},{1,9},{9,1},{2,10},{10,2},{3,11},{11,3},{4,12},{12,4},... | collective-permute-start | bytes 1572872 | tf_op jit(solution)/shard_map/ppermute | solution.py:229
  19.3 30.8 %collective-permute-start = (bf16[1024,256]{1,0:T(8,128)(2,1)}, bf16[1024,256]{1,0:T(8,128)(2,1)}, u32[]{:S(2)}, u32[]{:S(2)}) collective-permute-start(bf16[1024,256]{1,0:T(8,128)(2,1)} %param.20), channel_id=1, source_target_pairs={{0,4},{4,0},{1,5},{5,1},{2,6},{6,2},{3,7},{7,3},{8,12},{12,8},{9,1... | collective-permute-start | bytes 1572872 | tf_op jit(solution)/shard_map/ppermute | solution.py:227
  49.4 37.7 %collective-permute-start.2 = (bf16[1024,256]{1,0:T(8,128)(2,1)}, bf16[1024,256]{1,0:T(8,128)(2,1)}, u32[]{:S(2)}, u32[]{:S(2)}) collective-permute-start(bf16[1024,256]{1,0:T(8,128)(2,1)} %collective-permute-done.1), channel_id=1, source_target_pairs={{0,4},{4,0},{1,5},{5,1},{2,6},{6,2},{3,7},{7,3},{8,12},{12,8},{9,1... | collective-permute-start | bytes 1572872 | tf_op jit(solution)/shard_map/ppermute | solution.py:227
  110.2 42.9 %all-to-all-start = ((bf16[4,192,1024]{2,1,0:T(8,128)(2,1)}), bf16[4,192,1024]{2,1,0:T(8,128)(2,1)}, u32[]{:S(2)}, u32[]{:S(2)}) async-start(bf16[4,192,1024]{2,1,0:T(8,128)(2,1)} %bitcast.685), calls=%async_computation | async-start | bytes 3145728 | tf_op jit(solution)/shard_map/all_to_all | solution.py:268
  116.1 61.3 %collective-permute-start.6 = (bf16[64,256]{1,0:T(8,128)(2,1)}, bf16[64,256]{1,0:T(8,128)(2,1)S(1)}, u32[]{:S(2)}, u32[]{:S(2)}) collective-permute-start(bf16[64,256]{1,0:T(8,128)(2,1)} %get-tuple-element.206), channel_id=1, source_target_pairs={{0,4},{4,0},{1,5},{5,1},{2,6},{6,2},{3,7},{7,3},{8,12},{12,8},{9,1... | collective-permute-start | bytes 98312 | tf_op jit(solution)/shard_map/ppermute | solution.py:227
  116.3 61.1 %collective-permute-start.7 = (bf16[64,256]{1,0:T(8,128)(2,1)}, bf16[64,256]{1,0:T(8,128)(2,1)S(1)}, u32[]{:S(2)}, u32[]{:S(2)}) collective-permute-start(bf16[64,256]{1,0:T(8,128)(2,1)} %get-tuple-element.205), channel_id=1, source_target_pairs={{0,8},{8,0},{1,9},{9,1},{2,10},{10,2},{3,11},{11,3},{4,12},{12,4},... | collective-permute-start | bytes 98312 | tf_op jit(solution)/shard_map/ppermute | solution.py:229
  116.8 60.6 %collective-permute-start.8 = (bf16[64,256]{1,0:T(8,128)(2,1)S(1)}, bf16[64,256]{1,0:T(8,128)(2,1)S(1)}, u32[]{:S(2)}, u32[]{:S(2)}) collective-permute-start(bf16[64,256]{1,0:T(8,128)(2,1)S(1)} %get-tuple-element.204), channel_id=1, source_target_pairs={{0,12},{4,8},{8,4},{12,0},{1,13},{5,9},{9,5},{13,1},{2,14},{6,10},... | collective-permute-start | bytes 98312 | tf_op jit(solution)/shard_map/ppermute | solution.py:230
  173.8 28.1 %all-to-all-start.1 = ((bf16[4,64,1024]{2,1,0:T(8,128)(2,1)}), bf16[4,64,1024]{2,1,0:T(8,128)(2,1)S(1)}, u32[]{:S(2)}, u32[]{:S(2)}) async-start(bf16[4,64,1024]{2,1,0:T(8,128)(2,1)} %get-tuple-element.30), calls=%async_computation.1 | async-start | bytes 1048576 | tf_op jit(solution)/shard_map/all_to_all | solution.py:268
  177.3 190.0 %all-gather.8.cloned.1.call-start = ((), (), s32[]{:S(2)}) async-start(), calls=%async_computation.16 | async-start | bytes 1310720 | tf_op jit(solution)/shard_map/all_gather | solution.py:310
  208.0 47.9 %collective-permute-start.9 = (bf16[2,256,1024]{2,1,0:T(8,128)(2,1)}, bf16[2,256,1024]{2,1,0:T(8,128)(2,1)}, u32[]{:S(2)}, u32[]{:S(2)}) collective-permute-start(bf16[2,256,1024]{2,1,0:T(8,128)(2,1)} %fusion.16), channel_id=1, source_target_pairs={{0,4},{4,0},{1,5},{5,1},{2,6},{6,2},{3,7},{7,3},{8,12},{12,8},{9,1... | collective-permute-start | bytes 3145736 | tf_op jit(solution)/shard_map/ppermute | solution.py:227
  208.6 41.2 %collective-permute-start.17 = (bf16[128,256]{1,0:T(8,128)(2,1)}, bf16[128,256]{1,0:T(8,128)(2,1)}, u32[]{:S(2)}, u32[]{:S(2)}) collective-permute-start(bf16[128,256]{1,0:T(8,128)(2,1)} %get-tuple-element.186), channel_id=1, source_target_pairs={{0,4},{4,0},{1,5},{5,1},{2,6},{6,2},{3,7},{7,3},{8,12},{12,8},{9,1... | collective-permute-start | bytes 196616 | tf_op jit(solution)/shard_map/ppermute | solution.py:227
  209.2 42.2 %collective-permute-start.18 = (bf16[128,256]{1,0:T(8,128)(2,1)}, bf16[128,256]{1,0:T(8,128)(2,1)}, u32[]{:S(2)}, u32[]{:S(2)}) collective-permute-start(bf16[128,256]{1,0:T(8,128)(2,1)} %get-tuple-element.185), channel_id=1, source_target_pairs={{0,8},{8,0},{1,9},{9,1},{2,10},{10,2},{3,11},{11,3},{4,12},{12,4},... | collective-permute-start | bytes 196616 | tf_op jit(solution)/shard_map/ppermute | solution.py:229
  209.6 42.9 %collective-permute-start.19 = (bf16[128,256]{1,0:T(8,128)(2,1)}, bf16[128,256]{1,0:T(8,128)(2,1)}, u32[]{:S(2)}, u32[]{:S(2)}) collective-permute-start(bf16[128,256]{1,0:T(8,128)(2,1)} %get-tuple-element.184), channel_id=1, source_target_pairs={{0,12},{4,8},{8,4},{12,0},{1,13},{5,9},{9,5},{13,1},{2,14},{6,10},... | collective-permute-start | bytes 196616 | tf_op jit(solution)/shard_map/ppermute | solution.py:230
  210.5 88.4 %collective-permute-start.20 = (bf16[1024,256]{1,0:T(8,128)(2,1)}, bf16[1024,256]{1,0:T(8,128)(2,1)}, u32[]{:S(2)}, u32[]{:S(2)}) collective-permute-start(bf16[1024,256]{1,0:T(8,128)(2,1)} %param.21), channel_id=1, source_target_pairs={{0,4},{4,0},{1,5},{5,1},{2,6},{6,2},{3,7},{7,3},{8,12},{12,8},{9,1... | collective-permute-start | bytes 1572872 | tf_op jit(solution)/shard_map/ppermute | solution.py:227
  258.5 18.9 %collective-permute-start.10 = (bf16[256,1024]{1,0:T(8,128)(2,1)S(1)}, bf16[256,1024]{1,0:T(8,128)(2,1)S(1)}, u32[]{:S(2)}, u32[]{:S(2)}) collective-permute-start(bf16[256,1024]{1,0:T(8,128)(2,1)S(1)} %fusion.34), channel_id=1, source_target_pairs={{0,8},{8,0},{1,9},{9,1},{2,10},{10,2},{3,11},{11,3},{4,12},{12,4},... | collective-permute-start | bytes 1572872 | tf_op jit(solution)/shard_map/ppermute | solution.py:229
  265.7 182.8 %collective-permute-start.26 = (bf16[64,256]{1,0:T(8,128)(2,1)}, bf16[64,256]{1,0:T(8,128)(2,1)}, u32[]{:S(2)}, u32[]{:S(2)}) collective-permute-start(bf16[64,256]{1,0:T(8,128)(2,1)} %get-tuple-element.202), channel_id=1, source_target_pairs={{0,4},{4,0},{1,5},{5,1},{2,6},{6,2},{3,7},{7,3},{8,12},{12,8},{9,1... | collective-permute-start | bytes 98312 | tf_op jit(solution)/shard_map/ppermute | solution.py:227
  265.7 183.6 %collective-permute-start.27 = (bf16[64,256]{1,0:T(8,128)(2,1)}, bf16[64,256]{1,0:T(8,128)(2,1)}, u32[]{:S(2)}, u32[]{:S(2)}) collective-permute-start(bf16[64,256]{1,0:T(8,128)(2,1)} %get-tuple-element.201), channel_id=1, source_target_pairs={{0,8},{8,0},{1,9},{9,1},{2,10},{10,2},{3,11},{11,3},{4,12},{12,4},... | collective-permute-start | bytes 98312 | tf_op jit(solution)/shard_map/ppermute | solution.py:229
  266.2 76.3 %collective-permute-start.22 = (bf16[1024,256]{1,0:T(8,128)(2,1)}, bf16[1024,256]{1,0:T(8,128)(2,1)}, u32[]{:S(2)}, u32[]{:S(2)}) collective-permute-start(bf16[1024,256]{1,0:T(8,128)(2,1)} %collective-permute-done.21), channel_id=1, source_target_pairs={{0,4},{4,0},{1,5},{5,1},{2,6},{6,2},{3,7},{7,3},{8,12},{12,8},{9,1... | collective-permute-start | bytes 1572872 | tf_op jit(solution)/shard_map/ppermute | solution.py:227
  280.4 92.5 %collective-permute-start.15 = (bf16[256,1024]{1,0:T(8,128)(2,1)}, bf16[256,1024]{1,0:T(8,128)(2,1)}, u32[]{:S(2)}, u32[]{:S(2)}) collective-permute-start(bf16[256,1024]{1,0:T(8,128)(2,1)} %get-tuple-element.137), channel_id=1, source_target_pairs={{0,8},{8,0},{1,9},{9,1},{2,10},{10,2},{3,11},{11,3},{4,12},{12,4},... | collective-permute-start | bytes 1572872 | tf_op jit(solution)/shard_map/ppermute | solution.py:229
  298.9 151.1 %collective-permute-start.28 = (bf16[64,256]{1,0:T(8,128)(2,1)}, bf16[64,256]{1,0:T(8,128)(2,1)}, u32[]{:S(2)}, u32[]{:S(2)}) collective-permute-start(bf16[64,256]{1,0:T(8,128)(2,1)} %get-tuple-element.200), channel_id=1, source_target_pairs={{0,12},{4,8},{8,4},{12,0},{1,13},{5,9},{9,5},{13,1},{2,14},{6,10},... | collective-permute-start | bytes 98312 | tf_op jit(solution)/shard_map/ppermute | solution.py:230
  376.6 25.4 %collective-permute-start.24 = (bf16[128,1024]{1,0:T(8,128)(2,1)}, bf16[128,1024]{1,0:T(8,128)(2,1)}, u32[]{:S(2)}, u32[]{:S(2)}) collective-permute-start(bf16[128,1024]{1,0:T(8,128)(2,1)} %get-tuple-element.145), channel_id=1, source_target_pairs={{0,2},{1,3},{2,0},{3,1},{4,6},{5,7},{6,4},{7,5},{8,10},{9,11},{10,... | collective-permute-start | bytes 786440 | tf_op jit(solution)/shard_map/ppermute | solution.py:278
  382.1 27.4 %all-to-all-start.2 = ((bf16[4,64,1024]{2,1,0:T(8,128)(2,1)}), bf16[4,64,1024]{2,1,0:T(8,128)(2,1)S(1)}, u32[]{:S(2)}, u32[]{:S(2)}) async-start(bf16[4,64,1024]{2,1,0:T(8,128)(2,1)} %fusion.15), calls=%async_computation.2 | async-start | bytes 1048576 | tf_op jit(solution)/shard_map/all_to_all | solution.py:268
  386.5 18.1 %collective-permute-start.25 = (bf16[128,1024]{1,0:T(8,128)(2,1)}, bf16[128,1024]{1,0:T(8,128)(2,1)S(1)}, u32[]{:S(2)}, u32[]{:S(2)}) collective-permute-start(bf16[128,1024]{1,0:T(8,128)(2,1)} %get-tuple-element.144), channel_id=1, source_target_pairs={{0,3},{1,0},{2,1},{3,2},{4,7},{5,4},{6,5},{7,6},{8,11},{9,8},{10,9... | collective-permute-start | bytes 786440 | tf_op jit(solution)/shard_map/ppermute | solution.py:278
  402.0 76.3 %collective-permute-start.34 = (bf16[256,256]{1,0:T(8,128)(2,1)}, bf16[256,256]{1,0:T(8,128)(2,1)S(1)}, u32[]{:S(2)}, u32[]{:S(2)}) collective-permute-start(bf16[256,256]{1,0:T(8,128)(2,1)} %get-tuple-element.170), channel_id=1, source_target_pairs={{0,4},{4,0},{1,5},{5,1},{2,6},{6,2},{3,7},{7,3},{8,12},{12,8},{9,1... | collective-permute-start | bytes 393224 | tf_op jit(solution)/shard_map/ppermute | solution.py:227
  404.6 73.8 %collective-permute-start.35 = (bf16[256,256]{1,0:T(8,128)(2,1)}, bf16[256,256]{1,0:T(8,128)(2,1)S(1)}, u32[]{:S(2)}, u32[]{:S(2)}) collective-permute-start(bf16[256,256]{1,0:T(8,128)(2,1)} %get-tuple-element.169), channel_id=1, source_target_pairs={{0,8},{8,0},{1,9},{9,1},{2,10},{10,2},{3,11},{11,3},{4,12},{12,4},... | collective-permute-start | bytes 393224 | tf_op jit(solution)/shard_map/ppermute | solution.py:229
  441.6 32.4 %all-to-all-start.3 = ((bf16[4,64,1024]{2,1,0:T(8,128)(2,1)}), bf16[4,64,1024]{2,1,0:T(8,128)(2,1)S(1)}, u32[]{:S(2)}, u32[]{:S(2)}) async-start(bf16[4,64,1024]{2,1,0:T(8,128)(2,1)} %get-tuple-element.31), calls=%async_computation.3 | async-start | bytes 1048576 | tf_op jit(solution)/shard_map/all_to_all | solution.py:268
  448.4 77.9 %all-gather.10.cloned.1.call-start = ((), (), s32[]{:S(2)}) async-start(), calls=%async_computation.17 | async-start | bytes 2621440 | tf_op jit(solution)/shard_map/all_gather | solution.py:310
  448.5 30.0 %collective-permute-start.36 = (bf16[256,256]{1,0:T(8,128)(2,1)}, bf16[256,256]{1,0:T(8,128)(2,1)S(1)}, u32[]{:S(2)}, u32[]{:S(2)}) collective-permute-start(bf16[256,256]{1,0:T(8,128)(2,1)} %get-tuple-element.168), channel_id=1, source_target_pairs={{0,12},{4,8},{8,4},{12,0},{1,13},{5,9},{9,5},{13,1},{2,14},{6,10},... | collective-permute-start | bytes 393224 | tf_op jit(solution)/shard_map/ppermute | solution.py:230
  479.5 93.4 %all-gather.12.cloned.1.call-start = ((), (), s32[]{:S(2)}) async-start(), calls=%async_computation.18 | async-start | bytes 2621440 | tf_op jit(solution)/shard_map/all_gather | solution.py:310
  485.7 20.0 %collective-permute-start.37 = (bf16[256,256]{0,1:T(8,128)(2,1)}, bf16[256,256]{0,1:T(8,128)(2,1)}, u32[]{:S(2)}, u32[]{:S(2)}) collective-permute-start(bf16[256,256]{0,1:T(8,128)(2,1)} %bitcast.129), channel_id=1, source_target_pairs={{0,4},{4,0},{1,5},{5,1},{2,6},{6,2},{3,7},{7,3},{8,12},{12,8},{9,1... | collective-permute-start | bytes 393224 | tf_op jit(solution)/shard_map/ppermute | solution.py:227
  485.8 20.8 %collective-permute-start.38 = (bf16[256,256]{0,1:T(8,128)(2,1)S(1)}, bf16[256,256]{0,1:T(8,128)(2,1)}, u32[]{:S(2)}, u32[]{:S(2)}) collective-permute-start(bf16[256,256]{0,1:T(8,128)(2,1)S(1)} %bitcast.731), channel_id=1, source_target_pairs={{0,8},{8,0},{1,9},{9,1},{2,10},{10,2},{3,11},{11,3},{4,12},{12,4},... | collective-permute-start | bytes 393224 | tf_op jit(solution)/shard_map/ppermute | solution.py:229
  487.5 28.9 %collective-permute-start.39 = (bf16[256,256]{0,1:T(8,128)(2,1)S(1)}, bf16[256,256]{0,1:T(8,128)(2,1)S(1)}, u32[]{:S(2)}, u32[]{:S(2)}) collective-permute-start(bf16[256,256]{0,1:T(8,128)(2,1)S(1)} %bitcast.730), channel_id=1, source_target_pairs={{0,12},{4,8},{8,4},{12,0},{1,13},{5,9},{9,5},{13,1},{2,14},{6,10},... | collective-permute-start | bytes 393224 | tf_op jit(solution)/shard_map/ppermute | solution.py:230
  517.3 275.5 %reduce-scatter.16.cloned.1.call-start = ((), (), s32[]{:S(2)}) async-start(), calls=%async_computation.23 | async-start | bytes 655360 | tf_op jit(solution)/shard_map/reduce_scatter | solution.py:283
  583.6 18.7 %collective-permute-start.41 = (bf16[256,1024]{1,0:T(8,128)(2,1)}, bf16[256,1024]{1,0:T(8,128)(2,1)}, u32[]{:S(2)}, u32[]{:S(2)}) collective-permute-start(bf16[256,1024]{1,0:T(8,128)(2,1)} %fusion.36), channel_id=1, source_target_pairs={{0,8},{8,0},{1,9},{9,1},{2,10},{10,2},{3,11},{11,3},{4,12},{12,4},... | collective-permute-start | bytes 1572872 | tf_op jit(solution)/shard_map/ppermute | solution.py:229
  669.0 171.3 %reduce-scatter.20.cloned.1.call-start = ((), (), s32[]{:S(2)}) async-start(), calls=%async_computation.25 | async-start | bytes 2621440 | tf_op jit(solution)/shard_map/reduce_scatter | solution.py:283
  674.6 172.8 %reduce-scatter.18.cloned.1.call-start = ((), (), s32[]{:S(2)}) async-start(), calls=%async_computation.24 | async-start | bytes 2621440 | tf_op jit(solution)/shard_map/reduce_scatter | solution.py:283
  693.2 33.3 %all-to-all-start.4 = ((bf16[4,64,1024]{2,1,0:T(8,128)(2,1)}), bf16[4,64,1024]{2,1,0:T(8,128)(2,1)S(1)}, u32[]{:S(2)}, u32[]{:S(2)}) async-start(bf16[4,64,1024]{2,1,0:T(8,128)(2,1)} %bitcast.177), calls=%async_computation.4 | async-start | bytes 1048576 | tf_op jit(solution)/shard_map/all_to_all | solution.py:268
  779.7 39.4 %all-to-all-start.5 = ((bf16[4,64,1024]{2,1,0:T(8,128)(2,1)}), bf16[4,64,1024]{2,1,0:T(8,128)(2,1)}, u32[]{:S(2)}, u32[]{:S(2)}) async-start(bf16[4,64,1024]{2,1,0:T(8,128)(2,1)} %get-tuple-element.34), calls=%async_computation.5 | async-start | bytes 1048576 | tf_op jit(solution)/shard_map/all_to_all | solution.py:268
  784.8 129.0 %reduce-scatter.12.cloned.1.call-start = ((), (), s32[]{:S(2)}) async-start(), calls=%async_computation.21 | async-start | bytes 655360 | tf_op jit(solution)/shard_map/reduce_scatter | solution.py:283
  786.2 29.6 %collective-permute-start.64 = (bf16[128,1024]{1,0:T(8,128)(2,1)}, bf16[128,1024]{1,0:T(8,128)(2,1)}, u32[]{:S(2)}, u32[]{:S(2)}) collective-permute-start(bf16[128,1024]{1,0:T(8,128)(2,1)} %get-tuple-element.141), channel_id=1, source_target_pairs={{0,2},{1,3},{2,0},{3,1},{4,6},{5,7},{6,4},{7,5},{8,10},{9,11},{10,... | collective-permute-start | bytes 786440 | tf_op jit(solution)/shard_map/ppermute | solution.py:278
  789.2 28.3 %collective-permute-start.65 = (bf16[128,1024]{1,0:T(8,128)(2,1)}, bf16[128,1024]{1,0:T(8,128)(2,1)}, u32[]{:S(2)}, u32[]{:S(2)}) collective-permute-start(bf16[128,1024]{1,0:T(8,128)(2,1)} %get-tuple-element.140), channel_id=1, source_target_pairs={{0,3},{1,0},{2,1},{3,2},{4,7},{5,4},{6,5},{7,6},{8,11},{9,8},{10,9... | collective-permute-start | bytes 786440 | tf_op jit(solution)/shard_map/ppermute | solution.py:278
  795.3 35.3 %collective-permute-start.84 = (bf16[64,256]{1,0:T(8,128)(2,1)}, bf16[64,256]{1,0:T(8,128)(2,1)}, u32[]{:S(2)}, u32[]{:S(2)}) collective-permute-start(bf16[64,256]{1,0:T(8,128)(2,1)} %bitcast.634), channel_id=1, source_target_pairs={{0,4},{4,0},{1,5},{5,1},{2,6},{6,2},{3,7},{7,3},{8,12},{12,8},{9,1... | collective-permute-start | bytes 98312 | tf_op jit(solution)/shard_map/ppermute | solution.py:227
  795.9 35.5 %collective-permute-start.85 = (bf16[64,256]{1,0:T(8,128)(2,1)}, bf16[64,256]{1,0:T(8,128)(2,1)}, u32[]{:S(2)}, u32[]{:S(2)}) collective-permute-start(bf16[64,256]{1,0:T(8,128)(2,1)} %bitcast.633), channel_id=1, source_target_pairs={{0,8},{8,0},{1,9},{9,1},{2,10},{10,2},{3,11},{11,3},{4,12},{12,4},... | collective-permute-start | bytes 98312 | tf_op jit(solution)/shard_map/ppermute | solution.py:229
  796.5 35.6 %collective-permute-start.86 = (bf16[64,256]{1,0:T(8,128)(2,1)}, bf16[64,256]{1,0:T(8,128)(2,1)}, u32[]{:S(2)}, u32[]{:S(2)}) collective-permute-start(bf16[64,256]{1,0:T(8,128)(2,1)} %bitcast.632), channel_id=1, source_target_pairs={{0,12},{4,8},{8,4},{12,0},{1,13},{5,9},{9,5},{13,1},{2,14},{6,10},... | collective-permute-start | bytes 98312 | tf_op jit(solution)/shard_map/ppermute | solution.py:230
  821.7 142.7 %reduce-scatter.14.cloned.1.call-start = ((), (), s32[]{:S(2)}) async-start(), calls=%async_computation.22 | async-start | bytes 1310720 | tf_op jit(solution)/shard_map/reduce_scatter | solution.py:283
  827.4 53.1 %collective-permute-start.66 = (bf16[2,1024,256]{2,1,0:T(8,128)(2,1)S(1)}, bf16[2,1024,256]{2,1,0:T(8,128)(2,1)}, u32[]{:S(2)}, u32[]{:S(2)}) collective-permute-start(bf16[2,1024,256]{2,1,0:T(8,128)(2,1)S(1)} %fusion.22), channel_id=1, source_target_pairs={{0,4},{4,0},{1,5},{5,1},{2,6},{6,2},{3,7},{7,3},{8,12},{12,8},{9,1... | collective-permute-start | bytes 3145736 | tf_op jit(solution)/shard_map/ppermute | solution.py:227
  839.6 19.2 %collective-permute-start.56 = (bf16[2,256,1024]{2,1,0:T(8,128)(2,1)}, bf16[2,256,1024]{2,1,0:T(8,128)(2,1)}, u32[]{:S(2)}, u32[]{:S(2)}) collective-permute-start(bf16[2,256,1024]{2,1,0:T(8,128)(2,1)} %fusion.21), channel_id=1, source_target_pairs={{0,4},{4,0},{1,5},{5,1},{2,6},{6,2},{3,7},{7,3},{8,12},{12,8},{9,1... | collective-permute-start | bytes 3145736 | tf_op jit(solution)/shard_map/ppermute | solution.py:227
  858.8 20.5 %collective-permute-start.90 = (bf16[256,256]{0,1:T(8,128)(2,1)S(1)}, bf16[256,256]{0,1:T(8,128)(2,1)S(1)}, u32[]{:S(2)}, u32[]{:S(2)}) collective-permute-start(bf16[256,256]{0,1:T(8,128)(2,1)S(1)} %bitcast.717), channel_id=1, source_target_pairs={{0,12},{4,8},{8,4},{12,0},{1,13},{5,9},{9,5},{13,1},{2,14},{6,10},... | collective-permute-start | bytes 393224 | tf_op jit(solution)/shard_map/ppermute | solution.py:230
  864.2 41.9 %collective-permute-start.95 = (bf16[4,256,256]{1,2,0:T(8,128)(2,1)}, bf16[4,256,256]{1,2,0:T(8,128)(2,1)}, u32[]{:S(2)}, u32[]{:S(2)}) collective-permute-start(bf16[4,256,256]{1,2,0:T(8,128)(2,1)} %bitcast_dynamic-update-slice_fusion.26), channel_id=1, source_target_pairs={{0,16},{16,0},{1,17},{17,1},{2,18},{18,2},{3,19},{19,3},{4,20},{20... | collective-permute-start | bytes 1572872 | tf_op jit(solution)/shard_map/ppermute | solution.py:319
  879.9 28.8 %collective-permute-start.91 = (bf16[4,256,256]{1,2,0:T(8,128)(2,1)}, bf16[4,256,256]{1,2,0:T(8,128)(2,1)}, u32[]{:S(2)}, u32[]{:S(2)}) collective-permute-start(bf16[4,256,256]{1,2,0:T(8,128)(2,1)} %bitcast_dynamic-update-slice_fusion.29), channel_id=1, source_target_pairs={{0,16},{16,0},{1,17},{17,1},{2,18},{18,2},{3,19},{19,3},{4,20},{20... | collective-permute-start | bytes 1572872 | tf_op jit(solution)/shard_map/ppermute | solution.py:319
  895.1 23.3 %all-to-all-start.6 = ((bf16[4,64,1024]{2,1,0:T(8,128)(2,1)}), bf16[4,64,1024]{2,1,0:T(8,128)(2,1)}, u32[]{:S(2)}, u32[]{:S(2)}) async-start(bf16[4,64,1024]{2,1,0:T(8,128)(2,1)} %bitcast.192), calls=%async_computation.6 | async-start | bytes 1048576 | tf_op jit(solution)/shard_map/all_to_all | solution.py:268
  904.5 54.3 %collective-permute-start.67 = (bf16[1024,256]{1,0:T(8,128)(2,1)}, bf16[1024,256]{1,0:T(8,128)(2,1)}, u32[]{:S(2)}, u32[]{:S(2)}) collective-permute-start(bf16[1024,256]{1,0:T(8,128)(2,1)} %fusion.40), channel_id=1, source_target_pairs={{0,8},{8,0},{1,9},{9,1},{2,10},{10,2},{3,11},{11,3},{4,12},{12,4},... | collective-permute-start | bytes 1572872 | tf_op jit(solution)/shard_map/ppermute | solution.py:229
  915.1 45.9 %collective-permute-start.76 = (bf16[64,256]{1,0:T(8,128)(2,1)S(1)}, bf16[64,256]{1,0:T(8,128)(2,1)S(1)}, u32[]{:S(2)}, u32[]{:S(2)}) collective-permute-start(bf16[64,256]{1,0:T(8,128)(2,1)S(1)} %bitcast.758), channel_id=1, source_target_pairs={{0,4},{4,0},{1,5},{5,1},{2,6},{6,2},{3,7},{7,3},{8,12},{12,8},{9,1... | collective-permute-start | bytes 98312 | tf_op jit(solution)/shard_map/ppermute | solution.py:227
  915.2 45.8 %collective-permute-start.77 = (bf16[64,256]{1,0:T(8,128)(2,1)S(1)}, bf16[64,256]{1,0:T(8,128)(2,1)S(1)}, u32[]{:S(2)}, u32[]{:S(2)}) collective-permute-start(bf16[64,256]{1,0:T(8,128)(2,1)S(1)} %bitcast.757), channel_id=1, source_target_pairs={{0,8},{8,0},{1,9},{9,1},{2,10},{10,2},{3,11},{11,3},{4,12},{12,4},... | collective-permute-start | bytes 98312 | tf_op jit(solution)/shard_map/ppermute | solution.py:229
  915.8 45.3 %collective-permute-start.78 = (bf16[64,256]{1,0:T(8,128)(2,1)S(1)}, bf16[64,256]{1,0:T(8,128)(2,1)S(1)}, u32[]{:S(2)}, u32[]{:S(2)}) collective-permute-start(bf16[64,256]{1,0:T(8,128)(2,1)S(1)} %bitcast.756), channel_id=1, source_target_pairs={{0,12},{4,8},{8,4},{12,0},{1,13},{5,9},{9,5},{13,1},{2,14},{6,10},... | collective-permute-start | bytes 98312 | tf_op jit(solution)/shard_map/ppermute | solution.py:230
  954.3 41.8 %all-to-all-start.7 = ((bf16[4,192,1024]{2,1,0:T(8,128)(2,1)}), bf16[4,192,1024]{2,1,0:T(8,128)(2,1)}, u32[]{:S(2)}, u32[]{:S(2)}) async-start(bf16[4,192,1024]{2,1,0:T(8,128)(2,1)} %pad_maximum_fusion), calls=%async_computation.7 | async-start | bytes 3145728 | tf_op jit(solution)/shard_map/all_to_all | solution.py:268
  958.7 143.2 %all-reduce.4.cloned.1.call-start = ((), (), s32[]{:S(2)}) async-start(), calls=%async_computation.26 | async-start | bytes 180224 | tf_op jit(solution)/shard_map/psum | solution.py:494
  961.1 39.4 %collective-permute-start.79 = (bf16[4,64,256]{2,1,0:T(8,128)(2,1)S(1)}, bf16[4,64,256]{2,1,0:T(8,128)(2,1)S(1)}, u32[]{:S(2)}, u32[]{:S(2)}) collective-permute-start(bf16[4,64,256]{2,1,0:T(8,128)(2,1)S(1)} %constant_dynamic-update-slice_fusion.10), channel_id=1, source_target_pairs={{0,16},{16,0},{1,17},{17,1},{2,18},{18,2},{3,19},{19,3},{4,20},{20... | collective-permute-start | bytes 393224 | tf_op jit(solution)/shard_map/ppermute | solution.py:319
  970.4 158.1 %reduce-scatter.10.cloned.1.call-start = ((), (), s32[]{:S(2)}) async-start(), calls=%async_computation.20 | async-start | bytes 655360 | tf_op jit(solution)/shard_map/reduce_scatter | solution.py:283
  972.0 192.3 %reduce-scatter.8.cloned.1.call-start = ((), (), s32[]{:S(2)}) async-start(), calls=%async_computation.19 | async-start | bytes 1966080 | tf_op jit(solution)/shard_map/reduce_scatter | solution.py:283
  978.9 22.5 %collective-permute-start.83 = (bf16[4,128,256]{1,2,0:T(8,128)(2,1)S(1)}, bf16[4,128,256]{1,2,0:T(8,128)(2,1)S(1)}, u32[]{:S(2)}, u32[]{:S(2)}) collective-permute-start(bf16[4,128,256]{1,2,0:T(8,128)(2,1)S(1)} %constant_dynamic-update-slice_fusion.6), channel_id=1, source_target_pairs={{0,16},{16,0},{1,17},{17,1},{2,18},{18,2},{3,19},{19,3},{4,20},{20... | collective-permute-start | bytes 786440 | tf_op jit(solution)/shard_map/ppermute | solution.py:319
  1134.7 40.3 %collective-permute-start.75 = (bf16[4,64,256]{2,1,0:T(8,128)(2,1)S(1)}, bf16[4,64,256]{2,1,0:T(8,128)(2,1)S(1)}, u32[]{:S(2)}, u32[]{:S(2)}) collective-permute-start(bf16[4,64,256]{2,1,0:T(8,128)(2,1)S(1)} %constant_dynamic-update-slice_fusion.14), channel_id=1, source_target_pairs={{0,16},{16,0},{1,17},{17,1},{2,18},{18,2},{3,19},{19,3},{4,20},{20... | collective-permute-start | bytes 393224 | tf_op jit(solution)/shard_map/ppermute | solution.py:319
  1139.1 36.6 %collective-permute-start.62 = (bf16[1024,256]{1,0:T(8,128)(2,1)}, bf16[1024,256]{1,0:T(8,128)(2,1)}, u32[]{:S(2)}, u32[]{:S(2)}) collective-permute-start(bf16[1024,256]{1,0:T(8,128)(2,1)} %fusion.39), channel_id=1, source_target_pairs={{0,8},{8,0},{1,9},{9,1},{2,10},{10,2},{3,11},{11,3},{4,12},{12,4},... | collective-permute-start | bytes 1572872 | tf_op jit(solution)/shard_map/ppermute | solution.py:229
  (148 other events, 1278.5 us)
Sparse Core Ops, SparseCore 0:
  17.9 38.4 all-gather.5
  256.0 33.8 all-gather.7
  479.6 46.7 all-gather.9
  528.3 44.4 all-gather.11
  669.1 19.7 reduce-scatter.15
  691.1 50.3 reduce-scatter.19
  743.8 47.4 reduce-scatter.17
  821.8 26.4 reduce-scatter.11
  850.6 25.4 reduce-scatter.13
  970.5 131.4 all-reduce.3
  1104.8 23.5 reduce-scatter.9
  1130.6 33.6 reduce-scatter.7

commit v2 on v1

--- a/solution.py
+++ b/solution.py
@@ -233,27 +233,35 @@
         out = jnp.zeros((len(parts),) + parts[0].shape, parts[0].dtype)
         for part, spot in zip(parts, spots):
             out = lax.dynamic_update_index_in_dim(out, part, spot, 0)
-        return out
-
-    def team_gather(self, value):
+        return lax.optimization_barrier(out)
+
+    def spots(self):
         me = self.me()
+        return [me, me ^ 1, me ^ 2, me ^ 3]
+
+    def team_parts(self, value):
         core, across = self.swap(value, 1), self.swap(value, 2)
-        diagonal = self.swap(across, 1)
-        return self.place([value, core, across, diagonal], [me, me ^ 1, me ^ 2, me ^ 3])
-
-    def team_exchange(self, blocks):
-        me = self.me()
-        pick = lambda bits: lax.dynamic_index_in_dim(blocks, me ^ bits, 0, keepdims=False)
-        parts = [pick(0)] + [self.swap(pick(bits), bits) for bits in (1, 2, 3)]
-        return self.place(parts, [me, me ^ 1, me ^ 2, me ^ 3])
-
-    def team_reduce(self, blocks):
-        rx, rc = lax.axis_index("rx"), lax.axis_index("rc")
-        grid = blocks.reshape((2, 2) + blocks.shape[1:])
-        away = lax.dynamic_index_in_dim(grid, 1 - rc, 1, keepdims=False).astype(BF16)
-        home = lax.dynamic_index_in_dim(grid, rc, 1, keepdims=False) + self.swap(away, 1).astype(F32)
-        away = lax.dynamic_index_in_dim(home, 1 - rx, 0, keepdims=False).astype(BF16)
-        return lax.dynamic_index_in_dim(home, rx, 0, keepdims=False) + self.swap(away, 2).astype(F32)
+        return [value, core, across, self.swap(across, 1)]
+
+    def pick(self, blocks):
+        return [lax.dynamic_index_in_dim(blocks, spot, 0, keepdims=False) for spot in self.spots()]
+
+    def team_send(self, parts):
+        return [parts[0]] + [self.swap(parts[bits], bits) for bits in (1, 2, 3)]
+
+    def team_total(self, parts):
+        away = self.swap(jnp.stack([parts[1].astype(BF16), parts[3].astype(BF16)]), 1).astype(F32)
+        away_across = self.swap((parts[2] + away[1]).astype(BF16), 2).astype(F32)
+        return (parts[0] + away[0]) + away_across
+
+    def total(self, value):
+        for name in self.every:
+            bits = 1
+            while bits < self.sizes[name]:
+                pairs = [(i, i ^ bits) for i in range(self.sizes[name])]
+                value = value + lax.ppermute(value, name, pairs)
+                bits *= 2
+        return value
 
     def ring_index(self):
         return lax.axis_index("cs") * self.sizes["rb"] + lax.axis_index("rb")
@@ -292,32 +300,62 @@
             return value
         return lax.all_to_all(value, "rb", 1, 0, tiled=True)
 
-    def feature_blocks(self, value):
+    def feature_parts(self, value):
+        width = value.shape[1] // 4
+        return [value[:, i * width:(i + 1) * width] for i in range(4)]
+
+    def team_features(self, blocks):
+        rb, rows = self.sizes["rb"], blocks.shape[1]
+        return blocks.reshape(4, rows, rb, -1).transpose(1, 2, 0, 3).reshape(rows, -1)
+
+    def member_blocks(self, value):
+        rb, rows = self.sizes["rb"], value.shape[0]
+        return value.reshape(rows, rb, 4, -1).transpose(2, 0, 1, 3).reshape(4, rows, -1)
+
+    def widen(self, piece):
+        if self.sizes["rb"] > 1:
+            piece = lax.all_gather(piece, "rb", axis=2, tiled=True)
+        piece = piece.reshape(piece.shape[0], -1)
+        return lax.all_gather(piece[None], self.cols, axis=0, tiled=True)
+
+    def in_order(self, weight):
         rb = self.sizes["rb"]
-        parts = value.reshape(value.shape[0], rb, 4, -1).transpose(2, 0, 1, 3)
-        return parts.reshape(4, value.shape[0], -1)
-
-    def join_features(self, blocks):
+        if rb == 1:
+            return weight
+        parts = weight.reshape(weight.shape[:-1] + (4, rb, -1))
+        return jnp.swapaxes(parts, -3, -2).reshape(weight.shape)
+
+    def out_of_order(self, weight):
         rb = self.sizes["rb"]
-        count = blocks.shape[1]
-        return blocks.reshape(4, count, rb, -1).transpose(1, 2, 0, 3).reshape(count, -1)
-
-    def weight(self, blocks):
-        mine = self.team_exchange(blocks).transpose(1, 0, 2)
-        mine = mine.reshape(mine.shape[0], -1)
+        if rb == 1:
+            return weight
+        parts = weight.reshape(weight.shape[:-1] + (rb, 4, -1))
+        return jnp.swapaxes(parts, -3, -2).reshape(weight.shape)
+
+    def over_columns(self, partial):
+        total = lax.psum_scatter(partial.astype(BF16), self.cols, scatter_dimension=0, tiled=True)
+        total = total.reshape(total.shape[0], 4, -1)
         if self.sizes["rb"] > 1:
-            mine = lax.all_gather(mine, "rb", axis=1, tiled=True)
-        return lax.all_gather(mine, self.cols, axis=0, tiled=True)
-
-    def weight_grad(self, partial):
-        total = self.block_sum(partial.astype(BF16))
-        if self.sizes["rb"] > 1:
-            total = lax.psum_scatter(total, "rb", scatter_dimension=1, tiled=True)
-        blocks = total.reshape(total.shape[0], 4, -1).transpose(1, 0, 2)
-        low = self.team_exchange(blocks)
+            total = lax.psum_scatter(total, "rb", scatter_dimension=2, tiled=True)
+        return total
+
+    def weight_grads(self, relative, absolute):
+        flat = [[piece[:, i] for i in range(4)] for piece in relative]
+        flat += [self.pick(piece.transpose(1, 0, 2)) for piece in absolute]
+        sizes = [piece[0].shape[0] for piece in flat]
+        parts = self.team_send([jnp.concatenate([piece[i] for piece in flat]) for i in range(4)])
+        low = jnp.stack(parts)
         if self.sizes["dp"] == 2:
-            return low.astype(F32) + lax.ppermute(low, "dp", [(0, 1), (1, 0)]).astype(F32)
-        return lax.psum(low.astype(F32), "dp")
+            low = low.astype(F32) + lax.ppermute(low, "dp", [(0, 1), (1, 0)]).astype(F32)
+        else:
+            low = lax.psum(low.astype(F32), "dp")
+        parts = [low[i] for i in range(4)]
+        low = self.place(parts, self.spots())
+        out, at = [], 0
+        for size in sizes:
+            out.append(low[:, at:at + size])
+            at += size
+        return out
 
 
 def norm_forward(hidden, gain_row, shift_row):
@@ -357,8 +395,33 @@
 ):
     me = layout.me()
     split_rows = lambda weight: weight.reshape(4, -1, weight.shape[1])
-    qkv_w = layout.weight(column_rows(selfqkv))
-    tokens_all = layout.join_features(layout.team_gather(layout.halves(tokens)))
+
+    def by_token(rows):
+        return layout.halves(rows)
+
+    def gather_weights(relative, absolute, order=None):
+        pieces = relative + absolute
+        if order is not None:
+            pieces, _ = lax.optimization_barrier((pieces, order))
+        sizes = [piece.shape[1] for piece in pieces]
+        parts = layout.team_send(layout.pick(jnp.concatenate(pieces, axis=1)))
+        at = sum(piece.shape[1] for piece in relative)
+        groups = []
+        if relative:
+            groups.append(jnp.stack([part[:at] for part in parts], axis=1))
+        if absolute:
+            groups.append(layout.place([part[at:] for part in parts], layout.spots()).transpose(1, 0, 2))
+        wide = layout.widen(jnp.concatenate(groups))
+        out, at = [], 0
+        for index, size in enumerate(sizes):
+            weight = wide[:, at:at + size].reshape(-1, wide.shape[2])
+            out.append(weight if index < len(relative) else layout.in_order(weight))
+            at += size
+        return out
+
+    (qkv_w,) = gather_weights([column_rows(selfqkv)], [])
+    token_parts = layout.team_parts(by_token(tokens))
+    tokens_all = jnp.concatenate(token_parts, axis=1)
     width = tokens_all.shape[1]
     group = tokens_all.shape[0]
     own_rows = group // 4
@@ -380,10 +443,10 @@
     gains, shifts = by_row[3:6], by_row[6:9]
 
     def gather_tokens(own):
-        return layout.team_gather(own).reshape(group, width)
+        return jnp.concatenate(layout.team_parts(own))
 
     def reduce_tokens(partial):
-        return layout.team_reduce(partial.reshape(4, own_rows, width))
+        return layout.team_total([partial[i * own_rows:(i + 1) * own_rows] for i in range(4)])
 
     sequence_prefix = prefixes
     if layout.sizes["sq"] > 1:
@@ -397,23 +460,26 @@
     self_out, self_low, self_lse = flash_forward(sequence_prefix, self_set, 0, self_set, 1, 2, True)
     attended = layout.ring_exchange(self_low).reshape(heads * HD, group)
 
-    self_w = layout.weight(split_rows(selfproj))
-    encoder_all = layout.join_features(layout.team_gather(layout.halves(encoder)))
-    kv_w = layout.weight(column_rows(crosskv))
-    query_w = layout.weight(column_rows(crossquery[:, None]))
-    cross_w = layout.weight(split_rows(crossproj))
-    up_w = layout.weight(column_rows(upweight[:, None]))
-    down_w = layout.weight(split_rows(downweight))
+    kv_w, self_w, query_w, cross_w = gather_weights(
+        [column_rows(crosskv)],
+        [split_rows(selfproj), column_rows(crossquery[:, None]), split_rows(crossproj)],
+        tokens_all,
+    )
+    encoder_all = jnp.concatenate(layout.team_parts(by_token(encoder)), axis=1)
+    up_w, down_w = gather_weights([], [column_rows(upweight[:, None]), split_rows(downweight)], encoder_all)
     pair = contract(kv_w, encoder_all, 1, 1).reshape(heads, 2, HD, group)
     pair_bias = jnp.stack([jnp.zeros_like(head_biases[:, 3]), head_biases[:, 3]], axis=1)
     pair = (pair + pair_bias[..., None]).astype(BF16).reshape(heads, 2 * HD, group)
     cross_set = layout.ring_trickle(pair)
-    upstream = layout.join_features(
-        layout.team_exchange(layout.halves(cotangent).reshape(4, own_rows, -1))
-    ).astype(F32)
-
-    own_tokens = lax.dynamic_slice_in_dim(tokens_all, me * own_rows, own_rows, 0).astype(F32)
-    first_sum = own_tokens + (reduce_tokens(contract(attended, self_w, 0, 0)) + self_shift)
+    spots = layout.spots()
+    upstream = layout.team_send(layout.pick(by_token(cotangent).reshape(4, own_rows, -1)))
+    upstream = layout.team_features(layout.place(upstream, spots)).astype(F32)
+
+    own_tokens = lax.dynamic_slice_in_dim(tokens_all, me * own_rows, own_rows, 0)
+    own_tokens = layout.place(layout.feature_parts(own_tokens), spots)
+    own_tokens = layout.team_features(own_tokens).astype(F32)
+    self_partial = contract(attended, self_w, 0, 0).reshape(4, own_rows, width)
+    first_sum = own_tokens + (layout.team_total(layout.pick(self_partial)) + self_shift)
     first_out, first_normed, first_inverse = norm_forward(first_sum, gains[0], shifts[0])
     first_all = gather_tokens(first_out.astype(BF16))
 
@@ -431,8 +497,8 @@
     third_sum = second_out + (reduce_tokens(contract(hidden_act, down_w, 1, 0)) + down_bias)
     third_out, third_normed, third_inverse = norm_forward(third_sum, gains[2], shifts[2])
     layer_out = third_out.astype(BF16)
-    layer_out = layout.team_exchange(layout.feature_blocks(layer_out))
-    layer_out = layout.unhalves(layer_out.reshape(group, -1))
+    layer_out = layout.team_send(layout.pick(layout.member_blocks(layer_out)))
+    layer_out = layout.unhalves(layout.place(layer_out, spots).reshape(group, -1))
 
     third_grad, third_gain, third_shift = norm_backward(upstream, third_normed, third_inverse, gains[2])
     down_own = third_grad.astype(BF16)
@@ -440,14 +506,15 @@
     act_grad = contract(down_all, down_w, 1, 1)
     pre_low = jax.vjp(exact_gelu, hidden_pre)[1](act_grad)[0].astype(BF16)
     second_grad = third_grad + reduce_tokens(contract(pre_low, up_w, 1, 0))
-    downweight_grad = layout.weight_grad(contract(hidden_act, down_all, 0, 0))
-    upweight_grad = layout.weight_grad(contract(pre_low, second_all, 0, 0))
+    down_sum = layout.over_columns(layout.out_of_order(contract(hidden_act, down_all, 0, 0)))
+    up_sum = layout.over_columns(layout.out_of_order(contract(pre_low, second_all, 0, 0)))
+    upweight_grad, downweight_grad = layout.weight_grads([], [up_sum, down_sum])
     mid_grad, second_gain, second_shift = norm_backward(second_grad, second_normed, second_inverse, gains[1])
     cross_own = mid_grad.astype(BF16)
     cross_all = gather_tokens(cross_own)
     crossed_grad = contract(cross_w, cross_all, 1, 1).astype(BF16).reshape(heads, HD, group)
     crossed_grad = layout.ring_exchange(crossed_grad)
-    crossproj_grad = layout.weight_grad(contract(crossed, cross_all, 1, 0))
+    crossproj_sum = layout.over_columns(layout.out_of_order(contract(crossed, cross_all, 1, 0)))
     dquery, dkeys, dvalues = flash_backward(
         sequence_prefix, cross_query, 0, cross_set, 0, 1, crossed_grad, cross_out, cross_lse, False
     )
@@ -455,26 +522,31 @@
     dquery = layout.ring_exchange(dquery).reshape(heads * HD, group)
     first_grad = mid_grad + reduce_tokens(contract(dquery, query_w, 0, 0))
     dpair = layout.ring_trickle(jnp.concatenate([dkeys, dvalues], axis=1)).reshape(heads * 2 * HD, group)
-    crossquery_grad = layout.weight_grad(contract(dquery, first_all, 1, 0))
-    crosskv_grad = layout.weight_grad(contract(dpair, encoder_all, 1, 0))
-    encoder_grad = layout.team_reduce(layout.feature_blocks(contract(dpair, kv_w, 0, 0)))
+    crossquery_sum = layout.over_columns(layout.out_of_order(contract(dquery, first_all, 1, 0)))
+    crosskv_sum = layout.over_columns(contract(dpair, encoder_all, 1, 0))
+    crosskv_grad, crossproj_grad, crossquery_grad = layout.weight_grads(
+        [crosskv_sum], [crossproj_sum, crossquery_sum]
+    )
+    encoder_grad = layout.team_total(layout.feature_parts(contract(dpair, kv_w, 0, 0)))
     encoder_grad = layout.unhalves(encoder_grad)
     low_grad, first_gain, first_shift = norm_backward(first_grad, first_normed, first_inverse, gains[0])
     self_own = low_grad.astype(BF16)
-    self_all = gather_tokens(self_own)
+    self_all = layout.place(layout.team_parts(self_own), spots).reshape(group, width)
     attended_grad = contract(self_w, self_all, 1, 1).astype(BF16).reshape(heads, HD, group)
     attended_grad = layout.ring_exchange(attended_grad)
-    selfproj_grad = layout.weight_grad(contract(attended, self_all, 1, 0))
+    selfproj_sum = layout.over_columns(layout.out_of_order(contract(attended, self_all, 1, 0)))
     dq, dk, dv = flash_backward(
         sequence_prefix, self_set, 0, self_set, 1, 2, attended_grad, self_out, self_lse, True
     )
     self_bias_sums = (jnp.sum(dq.astype(F32), axis=(0, 2)), jnp.sum(dv.astype(F32), axis=(0, 2)))
     dqkv = layout.ring_exchange(jnp.concatenate([dq, dk, dv], axis=1)).reshape(heads * 3 * HD, group)
-    selfqkv_grad = layout.weight_grad(contract(dqkv, tokens_all, 1, 0))
+    selfqkv_sum = layout.over_columns(contract(dqkv, tokens_all, 1, 0))
+    selfqkv_grad, selfproj_grad = layout.weight_grads([selfqkv_sum], [selfproj_sum])
     tokens_part = contract(dqkv, qkv_w, 0, 0)
-    mine = lax.dynamic_slice_in_dim(tokens_part, me * own_rows, own_rows, 0) + low_grad
+    low_parts = jnp.concatenate(layout.pick(layout.member_blocks(low_grad)), axis=1)
+    mine = lax.dynamic_slice_in_dim(tokens_part, me * own_rows, own_rows, 0) + low_parts
     tokens_part = lax.dynamic_update_slice_in_dim(tokens_part, mine, me * own_rows, 0)
-    tokens_grad = layout.unhalves(layout.team_reduce(layout.feature_blocks(tokens_part)))
+    tokens_grad = layout.unhalves(layout.team_total(layout.feature_parts(tokens_part)))
 
     def at_head(sums):
         spot = (layout.ring_index() * 4 + me) * HD
@@ -490,8 +562,9 @@
         column_sum(self_own), column_sum(cross_own), column_sum(down_own),
         at_head(cross_bias_sums[0]), at_head(cross_bias_sums[1]),
     ])
-    rows, up_sums = lax.psum((rows, up_sums), layout.every)
-    late = lax.psum(jnp.stack([at_head(self_bias_sums[0]), at_head(self_bias_sums[1])]), layout.every)
+    rows = layout.total(jnp.concatenate([rows, up_sums.reshape(-1, width)]))
+    rows, up_sums = rows[:11], rows[11:].reshape(up_sums.shape)
+    late = layout.total(jnp.stack([at_head(self_bias_sums[0]), at_head(self_bias_sums[1])]))
     row_at = (lax.axis_index("rb") * 4 + me) * normgain.shape[1]
     col_at = lax.axis_index(layout.cols)
     by_row = lax.dynamic_slice_in_dim(rows[:9], row_at, normgain.shape[1], 1)

time: 1210 us -> 953 us (0.79)
  local copies, waits for them, and re-layouts: 331 us -> 110 us
  blocking collectives: 84.4 us -> 59.4 us
  waiting for transfers between devices: 399 us -> 380 us
  matrix products: 70.8 us -> 86.2 us
  starting transfers between devices: 115 us -> 102 us
    dynamic_update_slice x94 -> x41, local copies, waits for them, and re-layouts: 180 us -> 21.9 us  [place(): out = lax.dynamic_update_index_in_dim(out, part, spot, 0)]
    psum x1 -> x0, waiting for transfers between devices: 99.3 us -> none  [shards(): lax.psum(jnp.stack([at_head(self_bias_sums[0]), at_head(self_bias_sums[1]...]
    all_gather x3 -> x0, blocking collectives: 65.8 us -> none  [weight(): return lax.all_gather(mine, self.cols, axis=0, tiled=True)]
    ppermute x6, waiting for transfers between devices: 29 us -> 81 us  [ring_trickle(): lax.ppermute(pick(step), self.ring, [(i, (i + step) % size) for i in rang...]
    all_to_all x0 -> x1, blocking collectives: none -> 37.2 us  [ring_exchange(): lax.all_to_all(self.flip(blocks, 'cs', 'rb'), self.ring, 0, 0, tiled=True)]
    reshape x30 -> x11, local copies, waits for them, and re-layouts: 43.7 us -> 9.18 us  [the longest x7 8.25 us: over_columns(): total = total.reshape(total.shape[0], 4, -1)]
    ppermute x30 -> x22, waiting for transfers between devices: 105 us -> 133 us  [swap(): return lax.ppermute(value, 'rx', [(0, 1), (1, 0)])]
    all_gather x4 -> x3, waiting for transfers between devices: 35.9 us -> 10.8 us  [widen(): return lax.all_gather(piece[None], self.cols, axis=0, tiled=True)]
  transfers between devices with their start and end apart: 116 -> 95, of which waited for: 35 -> 42; matrix products, arithmetic and copies ran while one was open for 32% -> 20% of each run, Pallas kernels for 11% -> 14%
where the time goes in v2:
time: 953 us; the launch traced here: 940 us
  waiting for transfers between devices  380 us (40%)
  Pallas kernels  133 us (14%)
  local copies, waits for them, and re-layouts  110 us (12%)
  starting transfers between devices  102 us (11%)
  matrix products  86.2 us (9%)
  blocking collectives  59.4 us (6%)
  other arithmetic  52.1 us (5%)
  between operations  18.2 us (2%)
    ppermute x22, waiting for transfers between devices, swap(): return lax.ppermute(value, 'rx', [(0, 1), (1, 0)])  133 us
    all_to_all x7, waiting for transfers between devices, ring_exchange(): lax.all_to_all(self.flip(blocks, 'cs', 'rb'), self.ring, 0, 0, tiled=True)  101 us
    dot_general x21, matrix products, contract(): lax.dot_general(left, right, (((left_dim,), (right_dim,)), ((), ())), pre...  86.2 us
    pallas_call x2, Pallas kernels, flash_backward(): pl.pallas_call(functools.partial(backward_kernel, masked, bq, bk), out_sh...  81.5 us
    ppermute x6, waiting for transfers between devices, ring_trickle(): lax.ppermute(pick(step), self.ring, [(i, (i + step) % size) for i in rang...  81 us
    pallas_call x2, Pallas kernels, flash_forward(): pl.pallas_call(functools.partial(forward_kernel, masked, bq, bk), out_sha...  51 us
    all_to_all x1, blocking collectives, ring_exchange(): lax.all_to_all(self.flip(blocks, 'cs', 'rb'), self.ring, 0, 0, tiled=True)  37.2 us
    unnamed x274, local copies, waits for them, and re-layouts  36.7 us
  transfers between devices with their start and end apart: 95, of which 42 were waited for; matrix products, arithmetic and copies ran while one was open for 20% of the time, Pallas kernels for 14%

profile of v2, /device:TPU:0, one launch (start us, length us, event | category | flops | bytes accessed | tf_op | source)
XLA Modules:
  0.0 939.8 jit_solution(7544873402019962797)
XLA Ops:
  7.3 3.0 collective-permute-start.1
  15.6 13.4 %all-gather = f32[8192]{0:T(1024)S(1)} all-gather(f32[2048]{0:T(1024)S(1)} %pad_maximum_fusion.37), channel_id=2, replica_groups=mesh['dp'=2,'rb'=1,'rx'=2,'rc'=2,'sq'=1,'cs'=4] {'cs'}, dimensions={0}, use_global_device_ids=true | all-gather | bytes 40960 | tf_op jit(solution)/shard_map/all_gather | solution.py:432
  43.6 3.2 collective-permute-done.7
  60.9 10.8 %all-gather.5.cloned.1.call-done = bf16[4,192,1024]{2,1,0:T(8,128)(2,1)} async-done(((bf16[1,192,1024]{2,1,0:T(8,128)(2,1)}), bf16[4,192,1024]{2,1,0:T(8,128)(2,1)}) %all-gather.5.cloned.1.call-update) | async-done | bytes 1572880 | tf_op jit(solution)/shard_map/all_gather | solution.py:319
  71.7 4.4 multiply_convert_fusion.1
  76.1 3.6 all-to-all-start
  80.4 73.5 %all-to-all-done.q_ref.k_ref.v_ref = bf16[4,192,1024]{2,1,0:T(8,128)(2,1)S(1)} async-done(((bf16[4,192,1024]{2,1,0:T(8,128)(2,1)}), bf16[4,192,1024]{2,1,0:T(8,128)(2,1)S(1)}, u32[]{:S(2)}, u32[]{:S(2)}) %all-to-all-start) | async-done | bytes 1572896 | tf_op jit(solution)/shard_map/all_to_all | solution.py:276
  155.1 20.7 %attend_self.1 = (f32[4,64,1024]{2,1,0:T(8,128)}, bf16[4,64,1024]{2,1,0:T(8,128)(2,1)}, f32[4,1,1024]{2,1,0:T(1,128)}) custom-call(s32[1]{0:T(128)S(6)} %copy.610.prefix_ref, bf16[4,192,1024]{2,1,0:T(8,128)(2,1)} %copy-done.19, bf16[4,192,1024]{2,1,0:T(8,128)(2,1)} %copy-done.19, bf16[4,192,1024]{2,1,0:T(8,128)(2,1)} %copy-done.19), custom_call_target="tpu_custom_call" | custom-call | flops 4294967296 | bytes 3670016 | tf_op jit(solution)/shard_map/attend_self/pallas_call | solution.py:78
  175.8 3.5 all-to-all-start.1
  181.4 8.9 all_gather.22
  207.2 9.6 %collective-permute-done.10 = bf16[256,1024]{1,0:T(8,128)(2,1)S(1)} collective-permute-done((bf16[256,1024]{1,0:T(8,128)(2,1)S(1)}, bf16[256,1024]{1,0:T(8,128)(2,1)S(1)}, u32[]{:S(2)}, u32[]{:S(2)}) %collective-permute-start.10) | collective-permute-done | bytes 524320 | tf_op jit(solution)/shard_map/ppermute | solution.py:229
  223.6 3.3 collective-permute-done.27
  230.5 8.2 collective-permute-done.12
  238.7 3.1 add_convert_fusion.1
  245.3 2.7 fusion.22
  248.0 3.6 all-to-all-start.2
  251.7 2.9 collective-permute-start.18
  256.1 3.5 collective-permute-done.17
  259.5 46.3 %collective-permute-done.18 = bf16[128,1024]{1,0:T(8,128)(2,1)S(1)} collective-permute-done((bf16[128,1024]{1,0:T(8,128)(2,1)S(1)}, bf16[128,1024]{1,0:T(8,128)(2,1)S(1)}, u32[]{:S(2)}, u32[]{:S(2)}) %collective-permute-start.18) | collective-permute-done | bytes 262176 | tf_op jit(solution)/shard_map/ppermute | solution.py:286
  307.6 30.3 %attend_cross.1 = (f32[4,64,1024]{2,1,0:T(8,128)}, bf16[4,64,1024]{2,1,0:T(8,128)(2,1)}, f32[4,1,1024]{2,1,0:T(1,128)}) custom-call(s32[1]{0:T(128)S(6)} %copy.610.prefix_ref, bf16[4,64,1024]{2,1,0:T(8,128)(2,1)} %copy-done.36, bf16[4,128,1024]{2,1,0:T(8,128)(2,1)} %copy-done.20, bf16[4,128,1024]{2,1,0:T(8,128)(2,1)} %copy-done.20), custom_call_target="tpu_custom_call" | custom-call | flops 4294967296 | bytes 3670016 | tf_op jit(solution)/shard_map/attend_cross/pallas_call | solution.py:78
  338.0 37.2 %all_to_all.40 = bf16[4,64,1024]{2,1,0:T(8,128)(2,1)S(1)} all-to-all(bf16[4,64,1024]{2,1,0:T(8,128)(2,1)} %get-tuple-element.41), channel_id=1, replica_groups=mesh['dp'=2,'rb'=1,'rx'=2,'rc'=2,'sq'=1,'cs'=4] {'cs'}, dimensions={0} | all-to-all | bytes 1048576 | tf_op jit(solution)/shard_map/all_to_all | solution.py:276
  381.8 12.5 %collective-permute-done.21 = bf16[256,1024]{1,0:T(8,128)(2,1)S(1)} collective-permute-done((bf16[256,1024]{1,0:T(8,128)(2,1)S(1)}, bf16[256,1024]{1,0:T(8,128)(2,1)S(1)}, u32[]{:S(2)}, u32[]{:S(2)}) %collective-permute-start.21) | collective-permute-done | bytes 524320 | tf_op jit(solution)/shard_map/ppermute | solution.py:229
  396.7 11.7 %collective-permute-done.23 = bf16[256,1024]{1,0:T(8,128)(2,1)} collective-permute-done((bf16[256,1024]{1,0:T(8,128)(2,1)S(1)}, bf16[256,1024]{1,0:T(8,128)(2,1)}, u32[]{:S(2)}, u32[]{:S(2)}) %collective-permute-start.23) | collective-permute-done | bytes 524320 | tf_op jit(solution)/shard_map/ppermute | solution.py:229
  408.6 2.7 fusion.96
  411.3 15.6 %multiply_convert_fusion = (bf16[1024,1024]{1,0:T(8,128)(2,1)S(1)}, f32[1024,1024]{1,0:T(8,128)}, f32[1024,1024]{1,0:T(8,128)}) fusion(f32[1024]{0:T(1024)S(1)} %bitcast.690, bf16[1024,1024]{1,0:T(8,128)(2,1)S(1)} %bitcast.577, bf16[256,1024]{1,0:T(8,128)(2,1)} %collective-permute-done.24, bf16[256,1024]{1,0:T(8,128)(2,1)} %collective-permute-done.23, ...), kind=kOutput, calls=%fused_computation.4 | convolution fusion | flops 2225078272 | bytes 14684160 | tf_op jit(solution)/shard_map/dot_general | solution.py:202
  427.0 4.4 fusion.107
  437.0 3.4 collective-permute-done.34
  448.0 11.4 %collective-permute-done.29 = bf16[256,1024]{1,0:T(8,128)(2,1)S(1)} collective-permute-done((bf16[256,1024]{1,0:T(8,128)(2,1)S(1)}, bf16[256,1024]{1,0:T(8,128)(2,1)S(1)}, u32[]{:S(2)}, u32[]{:S(2)}) %collective-permute-start.29) | collective-permute-done | bytes 524320 | tf_op jit(solution)/shard_map/ppermute | solution.py:229
  465.2 11.8 %collective-permute-done.37 = bf16[256,1024]{1,0:T(8,128)(2,1)S(1)} collective-permute-done((bf16[256,1024]{1,0:T(8,128)(2,1)S(1)}, bf16[256,1024]{1,0:T(8,128)(2,1)S(1)}, u32[]{:S(2)}, u32[]{:S(2)}) %collective-permute-start.37) | collective-permute-done | bytes 524320 | tf_op jit(solution)/shard_map/ppermute | solution.py:229
  479.0 6.2 convert_reduce_fusion
  492.4 12.5 %collective-permute-done.40 = bf16[256,1024]{1,0:T(8,128)(2,1)S(1)} collective-permute-done((bf16[256,1024]{1,0:T(8,128)(2,1)S(1)}, bf16[256,1024]{1,0:T(8,128)(2,1)S(1)}, u32[]{:S(2)}, u32[]{:S(2)}) %collective-permute-start.40) | collective-permute-done | bytes 524320 | tf_op jit(solution)/shard_map/ppermute | solution.py:229
  509.6 11.6 %collective-permute-done.42 = bf16[256,1024]{1,0:T(8,128)(2,1)S(1)} collective-permute-done((bf16[256,1024]{1,0:T(8,128)(2,1)S(1)}, bf16[256,1024]{1,0:T(8,128)(2,1)S(1)}, u32[]{:S(2)}, u32[]{:S(2)}) %collective-permute-start.42) | collective-permute-done | bytes 524320 | tf_op jit(solution)/shard_map/ppermute | solution.py:229
  525.5 5.9 convolution_convert_fusion.1
  532.4 5.7 convolution_convert_fusion
  538.2 2.9 convolution_convert_fusion.8
  541.1 3.9 all-to-all-start.4
  548.3 4.5 collective-permute-done.31
  552.8 15.7 %all-to-all-done.4.g_ref = bf16[4,64,1024]{2,1,0:T(8,128)(2,1)S(1)} async-done(((bf16[4,64,1024]{2,1,0:T(8,128)(2,1)}), bf16[4,64,1024]{2,1,0:T(8,128)(2,1)S(1)}, u32[]{:S(2)}, u32[]{:S(2)}) %all-to-all-start.4) | async-done | bytes 524320 | tf_op jit(solution)/shard_map/all_to_all | solution.py:276
  569.2 48.2 %attend_cross_back.1 = (bf16[4,64,1024]{2,1,0:T(8,128)(2,1)}, bf16[4,64,1024]{2,1,0:T(8,128)(2,1)}, bf16[4,64,1024]{2,1,0:T(8,128)(2,1)}) custom-call(s32[1]{0:T(128)S(6)} %copy.610.prefix_ref, bf16[4,64,1024]{2,1,0:T(8,128)(2,1)} %copy-done.36, bf16[4,64,1024]{2,1,0:T(8,128)(2,1)} %copy-done.39, f32[4,64,1024]{2,1,0:T(8,128)} %get-tuple-element.44.o_ref, ...), custom_call_target="tpu_custom_call" | custom-call | flops 10737418240 | bytes 5242880 | tf_op jit(solution)/shard_map/attend_cross_back/pallas_call | solution.py:173
  623.3 5.1 all-to-all-start.5
  628.4 2.9 collective-permute-start.52
  634.4 3.8 collective-permute-done.51
  638.9 27.5 %collective-permute-done.52 = bf16[128,1024]{1,0:T(8,128)(2,1)S(1)} collective-permute-done((bf16[128,1024]{1,0:T(8,128)(2,1)S(1)}, bf16[128,1024]{1,0:T(8,128)(2,1)S(1)}, u32[]{:S(2)}, u32[]{:S(2)}) %collective-permute-start.52) | collective-permute-done | bytes 262176 | tf_op jit(solution)/shard_map/ppermute | solution.py:286
  667.8 4.9 fusion.110
  672.7 3.2 convolution_convert_fusion.4
  676.1 4.0 fusion.109
  682.9 3.5 convolution_convert_fusion.3
  702.6 10.7 %collective-permute-done.45 = bf16[256,1024]{1,0:T(8,128)(2,1)S(1)} collective-permute-done((bf16[256,1024]{1,0:T(8,128)(2,1)S(1)}, bf16[256,1024]{1,0:T(8,128)(2,1)S(1)}, u32[]{:S(2)}, u32[]{:S(2)}) %collective-permute-start.45) | collective-permute-done | bytes 524320 | tf_op jit(solution)/shard_map/ppermute | solution.py:229
  725.6 4.7 collective-permute-done.55
  732.8 8.2 collective-permute-done.47
  746.6 8.0 all-to-all-start.6
  757.6 12.2 %all-to-all-done.6.g_ref = bf16[4,64,1024]{2,1,0:T(8,128)(2,1)S(1)} async-done(((bf16[4,64,1024]{2,1,0:T(8,128)(2,1)}), bf16[4,64,1024]{2,1,0:T(8,128)(2,1)S(1)}, u32[]{:S(2)}, u32[]{:S(2)}) %all-to-all-start.6) | async-done | bytes 524320 | tf_op jit(solution)/shard_map/all_to_all | solution.py:276
  770.6 33.3 %attend_self_back.1 = (bf16[4,64,1024]{2,1,0:T(8,128)(2,1)}, bf16[4,64,1024]{2,1,0:T(8,128)(2,1)}, bf16[4,64,1024]{2,1,0:T(8,128)(2,1)}) custom-call(s32[1]{0:T(128)S(6)} %copy.610.prefix_ref, bf16[4,192,1024]{2,1,0:T(8,128)(2,1)} %copy-done.19, bf16[4,64,1024]{2,1,0:T(8,128)(2,1)} %copy-done.40, f32[4,64,1024]{2,1,0:T(8,128)} %get-tuple-element.47.o_ref, ...), custom_call_target="tpu_custom_call" | custom-call | flops 10737418240 | bytes 5242880 | tf_op jit(solution)/shard_map/attend_self_back/pallas_call | solution.py:173
  803.9 2.7 pad_maximum_fusion.4
  806.5 4.3 all-to-all-start.7
  824.9 2.7 collective-permute-done.66
  830.9 3.1 convolution_convert_fusion.6
  837.5 4.7 collective-permute-start.69
  843.8 15.0 %collective-permute-done.69 = f32[15,1024]{1,0:T(8,128)S(1)} collective-permute-done((f32[15,1024]{1,0:T(8,128)S(1)}, f32[15,1024]{1,0:T(8,128)S(1)}, u32[]{:S(2)}, u32[]{:S(2)}) %collective-permute-start.69) | collective-permute-done | bytes 61472 | tf_op jit(solution)/shard_map/ppermute | solution.py:262
  861.4 5.0 convolution_convert_fusion.2
  873.8 3.7 convolution_bitcast_fusion
  884.0 3.9 collective-permute-done.63
  893.1 8.4 reduce-scatter.8.cloned.1.call-done
  919.0 6.1 collective-permute-done.50
  (675 shorter events, 243.8 us)
Async XLA Ops:
  7.2 64.5 %all-gather.5.cloned.1.call-start = ((), (), s32[]{:S(2)}) async-start(), calls=%async_computation.15 | async-start | bytes 1966080 | tf_op jit(solution)/shard_map/all_gather | solution.py:319
  7.3 22.5 %collective-permute-start.1 = (bf16[1024,256]{1,0:T(8,128)(2,1)}, bf16[1024,256]{1,0:T(8,128)(2,1)}, u32[]{:S(2)}, u32[]{:S(2)}) collective-permute-start(bf16[1024,256]{1,0:T(8,128)(2,1)} %param.20), channel_id=1, source_target_pairs={{0,8},{8,0},{1,9},{9,1},{2,10},{10,2},{3,11},{11,3},{4,12},{12,4},... | collective-permute-start | bytes 1572872 | tf_op jit(solution)/shard_map/ppermute | solution.py:229
  10.3 24.0 %collective-permute-start = (bf16[1024,256]{1,0:T(8,128)(2,1)}, bf16[1024,256]{1,0:T(8,128)(2,1)}, u32[]{:S(2)}, u32[]{:S(2)}) collective-permute-start(bf16[1024,256]{1,0:T(8,128)(2,1)} %param.20), channel_id=1, source_target_pairs={{0,4},{4,0},{1,5},{5,1},{2,6},{6,2},{3,7},{7,3},{8,12},{12,8},{9,1... | collective-permute-start | bytes 1572872 | tf_op jit(solution)/shard_map/ppermute | solution.py:227
  11.6 20.3 %collective-permute-start.3 = (bf16[192,256]{1,0:T(8,128)(2,1)S(1)}, bf16[192,256]{1,0:T(8,128)(2,1)S(1)}, u32[]{:S(2)}, u32[]{:S(2)}) collective-permute-start(bf16[192,256]{1,0:T(8,128)(2,1)S(1)} %get-tuple-element.243), channel_id=1, source_target_pairs={{0,4},{4,0},{1,5},{5,1},{2,6},{6,2},{3,7},{7,3},{8,12},{12,8},{9,1... | collective-permute-start | bytes 294920 | tf_op jit(solution)/shard_map/ppermute | solution.py:227
  12.1 19.8 %collective-permute-start.4 = (bf16[192,256]{1,0:T(8,128)(2,1)S(1)}, bf16[192,256]{1,0:T(8,128)(2,1)S(1)}, u32[]{:S(2)}, u32[]{:S(2)}) collective-permute-start(bf16[192,256]{1,0:T(8,128)(2,1)S(1)} %get-tuple-element.242), channel_id=1, source_target_pairs={{0,8},{8,0},{1,9},{9,1},{2,10},{10,2},{3,11},{11,3},{4,12},{12,4},... | collective-permute-start | bytes 294920 | tf_op jit(solution)/shard_map/ppermute | solution.py:229
  12.2 19.7 %collective-permute-start.5 = (bf16[192,256]{1,0:T(8,128)(2,1)S(1)}, bf16[192,256]{1,0:T(8,128)(2,1)}, u32[]{:S(2)}, u32[]{:S(2)}) collective-permute-start(bf16[192,256]{1,0:T(8,128)(2,1)S(1)} %get-tuple-element.241), channel_id=1, source_target_pairs={{0,12},{4,8},{8,4},{12,0},{1,13},{5,9},{9,5},{13,1},{2,14},{6,10},... | collective-permute-start | bytes 294920 | tf_op jit(solution)/shard_map/ppermute | solution.py:230
  34.3 156.1 %all-gather.7.cloned.1.call-start = ((), (), s32[]{:S(2)}) async-start(), calls=%async_computation.16 | async-start | bytes 3276800 | tf_op jit(solution)/shard_map/all_gather | solution.py:319
  76.1 77.8 %all-to-all-start = ((bf16[4,192,1024]{2,1,0:T(8,128)(2,1)}), bf16[4,192,1024]{2,1,0:T(8,128)(2,1)S(1)}, u32[]{:S(2)}, u32[]{:S(2)}) async-start(bf16[4,192,1024]{2,1,0:T(8,128)(2,1)} %bitcast.20), calls=%async_computation | async-start | bytes 3145728 | tf_op jit(solution)/shard_map/all_to_all | solution.py:276
  175.8 16.6 %all-to-all-start.1 = ((bf16[4,64,1024]{2,1,0:T(8,128)(2,1)}), bf16[4,64,1024]{2,1,0:T(8,128)(2,1)S(1)}, u32[]{:S(2)}, u32[]{:S(2)}) async-start(bf16[4,64,1024]{2,1,0:T(8,128)(2,1)} %get-tuple-element.36), calls=%async_computation.1 | async-start | bytes 1048576 | tf_op jit(solution)/shard_map/all_to_all | solution.py:276
  179.2 229.3 %all-gather.9.cloned.1.call-start = ((), (), s32[]{:S(2)}) async-start(), calls=%async_computation.17 | async-start | bytes 5242880 | tf_op jit(solution)/shard_map/all_gather | solution.py:319
  179.5 15.8 %collective-permute-start.15 = (bf16[1024,256]{1,0:T(8,128)(2,1)S(1)}, bf16[1024,256]{1,0:T(8,128)(2,1)}, u32[]{:S(2)}, u32[]{:S(2)}) collective-permute-start(bf16[1024,256]{1,0:T(8,128)(2,1)S(1)} %copy-done.33), channel_id=1, source_target_pairs={{0,8},{8,0},{1,9},{9,1},{2,10},{10,2},{3,11},{11,3},{4,12},{12,4},... | collective-permute-start | bytes 1572872 | tf_op jit(solution)/shard_map/ppermute | solution.py:229
  181.1 14.5 %collective-permute-start.14 = (bf16[1024,256]{1,0:T(8,128)(2,1)S(1)}, bf16[1024,256]{1,0:T(8,128)(2,1)}, u32[]{:S(2)}, u32[]{:S(2)}) collective-permute-start(bf16[1024,256]{1,0:T(8,128)(2,1)S(1)} %copy-done.33), channel_id=1, source_target_pairs={{0,4},{4,0},{1,5},{5,1},{2,6},{6,2},{3,7},{7,3},{8,12},{12,8},{9,1... | collective-permute-start | bytes 1572872 | tf_op jit(solution)/shard_map/ppermute | solution.py:227
  201.9 14.9 %collective-permute-start.10 = (bf16[256,1024]{1,0:T(8,128)(2,1)S(1)}, bf16[256,1024]{1,0:T(8,128)(2,1)S(1)}, u32[]{:S(2)}, u32[]{:S(2)}) collective-permute-start(bf16[256,1024]{1,0:T(8,128)(2,1)S(1)} %fusion.64), channel_id=1, source_target_pairs={{0,8},{8,0},{1,9},{9,1},{2,10},{10,2},{3,11},{11,3},{4,12},{12,4},... | collective-permute-start | bytes 1572872 | tf_op jit(solution)/shard_map/ppermute | solution.py:229
  205.2 14.6 %collective-permute-start.25 = (bf16[512,256]{1,0:T(8,128)(2,1)S(1)}, bf16[512,256]{1,0:T(8,128)(2,1)}, u32[]{:S(2)}, u32[]{:S(2)}) collective-permute-start(bf16[512,256]{1,0:T(8,128)(2,1)S(1)} %get-tuple-element.215), channel_id=1, source_target_pairs={{0,4},{4,0},{1,5},{5,1},{2,6},{6,2},{3,7},{7,3},{8,12},{12,8},{9,1... | collective-permute-start | bytes 786440 | tf_op jit(solution)/shard_map/ppermute | solution.py:227
  205.4 17.1 %collective-permute-start.26 = (bf16[512,256]{1,0:T(8,128)(2,1)S(1)}, bf16[512,256]{1,0:T(8,128)(2,1)}, u32[]{:S(2)}, u32[]{:S(2)}) collective-permute-start(bf16[512,256]{1,0:T(8,128)(2,1)S(1)} %get-tuple-element.214), channel_id=1, source_target_pairs={{0,8},{8,0},{1,9},{9,1},{2,10},{10,2},{3,11},{11,3},{4,12},{12,4},... | collective-permute-start | bytes 786440 | tf_op jit(solution)/shard_map/ppermute | solution.py:229
  206.1 20.8 %collective-permute-start.27 = (bf16[512,256]{1,0:T(8,128)(2,1)S(1)}, bf16[512,256]{1,0:T(8,128)(2,1)}, u32[]{:S(2)}, u32[]{:S(2)}) collective-permute-start(bf16[512,256]{1,0:T(8,128)(2,1)S(1)} %get-tuple-element.213), channel_id=1, source_target_pairs={{0,12},{4,8},{8,4},{12,0},{1,13},{5,9},{9,5},{13,1},{2,14},{6,10},... | collective-permute-start | bytes 786440 | tf_op jit(solution)/shard_map/ppermute | solution.py:230
  218.2 20.5 %collective-permute-start.12 = (bf16[256,1024]{1,0:T(8,128)(2,1)}, bf16[256,1024]{1,0:T(8,128)(2,1)}, u32[]{:S(2)}, u32[]{:S(2)}) collective-permute-start(bf16[256,1024]{1,0:T(8,128)(2,1)} %fusion.61), channel_id=1, source_target_pairs={{0,8},{8,0},{1,9},{9,1},{2,10},{10,2},{3,11},{11,3},{4,12},{12,4},... | collective-permute-start | bytes 1572872 | tf_op jit(solution)/shard_map/ppermute | solution.py:229
  229.4 15.0 %collective-permute-start.11 = (bf16[256,1024]{1,0:T(8,128)(2,1)}, bf16[256,1024]{1,0:T(8,128)(2,1)S(1)}, u32[]{:S(2)}, u32[]{:S(2)}) collective-permute-start(bf16[256,1024]{1,0:T(8,128)(2,1)} %fusion.61), channel_id=1, source_target_pairs={{0,4},{4,0},{1,5},{5,1},{2,6},{6,2},{3,7},{7,3},{8,12},{12,8},{9,1... | collective-permute-start | bytes 1572872 | tf_op jit(solution)/shard_map/ppermute | solution.py:227
  242.7 16.8 %collective-permute-start.17 = (bf16[128,1024]{1,0:T(8,128)(2,1)}, bf16[128,1024]{1,0:T(8,128)(2,1)S(1)}, u32[]{:S(2)}, u32[]{:S(2)}) collective-permute-start(bf16[128,1024]{1,0:T(8,128)(2,1)} %get-tuple-element.211), channel_id=1, source_target_pairs={{0,1},{1,2},{2,3},{3,0},{4,5},{5,6},{6,7},{7,4},{8,9},{9,10},{10,1... | collective-permute-start | bytes 786440 | tf_op jit(solution)/shard_map/ppermute | solution.py:286
  248.0 57.9 %all-to-all-start.2 = ((bf16[4,64,1024]{2,1,0:T(8,128)(2,1)}), bf16[4,64,1024]{2,1,0:T(8,128)(2,1)S(1)}, u32[]{:S(2)}, u32[]{:S(2)}) async-start(bf16[4,64,1024]{2,1,0:T(8,128)(2,1)} %fusion.22), calls=%async_computation.2 | async-start | bytes 1048576 | tf_op jit(solution)/shard_map/all_to_all | solution.py:276
  251.7 434.8 %reduce-scatter.14.cloned.1.call-start = ((), (), s32[]{:S(2)}) async-start(), calls=%async_computation.21 | async-start | bytes 655360 | tf_op jit(solution)/shard_map/reduce_scatter | solution.py:336
  251.7 54.1 %collective-permute-start.18 = (bf16[128,1024]{1,0:T(8,128)(2,1)S(1)}, bf16[128,1024]{1,0:T(8,128)(2,1)S(1)}, u32[]{:S(2)}, u32[]{:S(2)}) collective-permute-start(bf16[128,1024]{1,0:T(8,128)(2,1)S(1)} %get-tuple-element.210), channel_id=1, source_target_pairs={{0,2},{1,3},{2,0},{3,1},{4,6},{5,7},{6,4},{7,5},{8,10},{9,11},{10,... | collective-permute-start | bytes 786440 | tf_op jit(solution)/shard_map/ppermute | solution.py:286
  254.6 51.2 %collective-permute-start.19 = (bf16[128,1024]{1,0:T(8,128)(2,1)S(1)}, bf16[128,1024]{1,0:T(8,128)(2,1)S(1)}, u32[]{:S(2)}, u32[]{:S(2)}) collective-permute-start(bf16[128,1024]{1,0:T(8,128)(2,1)S(1)} %get-tuple-element.209), channel_id=1, source_target_pairs={{0,3},{1,0},{2,1},{3,2},{4,7},{5,4},{6,5},{7,6},{8,11},{9,8},{10,9... | collective-permute-start | bytes 786440 | tf_op jit(solution)/shard_map/ppermute | solution.py:286
  380.3 14.0 %collective-permute-start.21 = (bf16[256,1024]{1,0:T(8,128)(2,1)S(1)}, bf16[256,1024]{1,0:T(8,128)(2,1)S(1)}, u32[]{:S(2)}, u32[]{:S(2)}) collective-permute-start(bf16[256,1024]{1,0:T(8,128)(2,1)S(1)} %fusion.50), channel_id=1, source_target_pairs={{0,8},{8,0},{1,9},{9,1},{2,10},{10,2},{3,11},{11,3},{4,12},{12,4},... | collective-permute-start | bytes 1572872 | tf_op jit(solution)/shard_map/ppermute | solution.py:229
  395.2 13.3 %collective-permute-start.23 = (bf16[256,1024]{1,0:T(8,128)(2,1)S(1)}, bf16[256,1024]{1,0:T(8,128)(2,1)}, u32[]{:S(2)}, u32[]{:S(2)}) collective-permute-start(bf16[256,1024]{1,0:T(8,128)(2,1)S(1)} %fusion.62), channel_id=1, source_target_pairs={{0,8},{8,0},{1,9},{9,1},{2,10},{10,2},{3,11},{11,3},{4,12},{12,4},... | collective-permute-start | bytes 1572872 | tf_op jit(solution)/shard_map/ppermute | solution.py:229
  396.7 14.6 %collective-permute-start.22 = (bf16[256,1024]{1,0:T(8,128)(2,1)S(1)}, bf16[256,1024]{1,0:T(8,128)(2,1)}, u32[]{:S(2)}, u32[]{:S(2)}) collective-permute-start(bf16[256,1024]{1,0:T(8,128)(2,1)S(1)} %fusion.62), channel_id=1, source_target_pairs={{0,4},{4,0},{1,5},{5,1},{2,6},{6,2},{3,7},{7,3},{8,12},{12,8},{9,1... | collective-permute-start | bytes 1572872 | tf_op jit(solution)/shard_map/ppermute | solution.py:227
  445.2 14.2 %collective-permute-start.29 = (bf16[256,1024]{1,0:T(8,128)(2,1)S(1)}, bf16[256,1024]{1,0:T(8,128)(2,1)S(1)}, u32[]{:S(2)}, u32[]{:S(2)}) collective-permute-start(bf16[256,1024]{1,0:T(8,128)(2,1)S(1)} %fusion.44), channel_id=1, source_target_pairs={{0,8},{8,0},{1,9},{9,1},{2,10},{10,2},{3,11},{11,3},{4,12},{12,4},... | collective-permute-start | bytes 1572872 | tf_op jit(solution)/shard_map/ppermute | solution.py:229
  463.7 13.3 %collective-permute-start.37 = (bf16[256,1024]{1,0:T(8,128)(2,1)S(1)}, bf16[256,1024]{1,0:T(8,128)(2,1)S(1)}, u32[]{:S(2)}, u32[]{:S(2)}) collective-permute-start(bf16[256,1024]{1,0:T(8,128)(2,1)S(1)} %get-tuple-element.163), channel_id=1, source_target_pairs={{0,8},{8,0},{1,9},{9,1},{2,10},{10,2},{3,11},{11,3},{4,12},{12,4},... | collective-permute-start | bytes 1572872 | tf_op jit(solution)/shard_map/ppermute | solution.py:229
  465.2 11.8 %collective-permute-start.36 = (bf16[256,1024]{1,0:T(8,128)(2,1)S(1)}, bf16[256,1024]{1,0:T(8,128)(2,1)S(1)}, u32[]{:S(2)}, u32[]{:S(2)}) collective-permute-start(bf16[256,1024]{1,0:T(8,128)(2,1)S(1)} %get-tuple-element.163), channel_id=1, source_target_pairs={{0,4},{4,0},{1,5},{5,1},{2,6},{6,2},{3,7},{7,3},{8,12},{12,8},{9,1... | collective-permute-start | bytes 1572872 | tf_op jit(solution)/shard_map/ppermute | solution.py:227
  490.9 14.0 %collective-permute-start.40 = (bf16[256,1024]{1,0:T(8,128)(2,1)S(1)}, bf16[256,1024]{1,0:T(8,128)(2,1)S(1)}, u32[]{:S(2)}, u32[]{:S(2)}) collective-permute-start(bf16[256,1024]{1,0:T(8,128)(2,1)S(1)} %fusion.39), channel_id=1, source_target_pairs={{0,8},{8,0},{1,9},{9,1},{2,10},{10,2},{3,11},{11,3},{4,12},{12,4},... | collective-permute-start | bytes 1572872 | tf_op jit(solution)/shard_map/ppermute | solution.py:229
  508.1 13.1 %collective-permute-start.42 = (bf16[256,1024]{1,0:T(8,128)(2,1)S(1)}, bf16[256,1024]{1,0:T(8,128)(2,1)S(1)}, u32[]{:S(2)}, u32[]{:S(2)}) collective-permute-start(bf16[256,1024]{1,0:T(8,128)(2,1)S(1)} %get-tuple-element.166), channel_id=1, source_target_pairs={{0,8},{8,0},{1,9},{9,1},{2,10},{10,2},{3,11},{11,3},{4,12},{12,4},... | collective-permute-start | bytes 1572872 | tf_op jit(solution)/shard_map/ppermute | solution.py:229
  509.6 11.7 %collective-permute-start.41 = (bf16[256,1024]{1,0:T(8,128)(2,1)S(1)}, bf16[256,1024]{1,0:T(8,128)(2,1)S(1)}, u32[]{:S(2)}, u32[]{:S(2)}) collective-permute-start(bf16[256,1024]{1,0:T(8,128)(2,1)S(1)} %get-tuple-element.166), channel_id=1, source_target_pairs={{0,4},{4,0},{1,5},{5,1},{2,6},{6,2},{3,7},{7,3},{8,12},{12,8},{9,1... | collective-permute-start | bytes 1572872 | tf_op jit(solution)/shard_map/ppermute | solution.py:227
  525.5 162.0 %reduce-scatter.18.cloned.1.call-start = ((), (), s32[]{:S(2)}) async-start(), calls=%async_computation.23 | async-start | bytes 2621440 | tf_op jit(solution)/shard_map/reduce_scatter | solution.py:336
  531.4 157.5 %reduce-scatter.20.cloned.1.call-start = ((), (), s32[]{:S(2)}) async-start(), calls=%async_computation.24 | async-start | bytes 2621440 | tf_op jit(solution)/shard_map/reduce_scatter | solution.py:336
  541.1 27.3 %all-to-all-start.4 = ((bf16[4,64,1024]{2,1,0:T(8,128)(2,1)}), bf16[4,64,1024]{2,1,0:T(8,128)(2,1)S(1)}, u32[]{:S(2)}, u32[]{:S(2)}) async-start(bf16[4,64,1024]{2,1,0:T(8,128)(2,1)} %bitcast.121), calls=%async_computation.4 | async-start | bytes 1048576 | tf_op jit(solution)/shard_map/all_to_all | solution.py:276
  547.9 73.7 %collective-permute-start.32 = (bf16[256,256]{1,0:T(8,128)(2,1)S(1)}, bf16[256,256]{1,0:T(8,128)(2,1)}, u32[]{:S(2)}, u32[]{:S(2)}) collective-permute-start(bf16[256,256]{1,0:T(8,128)(2,1)S(1)} %bitcast.636), channel_id=1, source_target_pairs={{0,12},{4,8},{8,4},{12,0},{1,13},{5,9},{9,5},{13,1},{2,14},{6,10},... | collective-permute-start | bytes 393224 | tf_op jit(solution)/shard_map/ppermute | solution.py:230
  621.6 16.6 %collective-permute-start.51 = (bf16[128,1024]{1,0:T(8,128)(2,1)S(1)}, bf16[128,1024]{1,0:T(8,128)(2,1)S(1)}, u32[]{:S(2)}, u32[]{:S(2)}) collective-permute-start(bf16[128,1024]{1,0:T(8,128)(2,1)S(1)} %get-tuple-element.203), channel_id=1, source_target_pairs={{0,1},{1,2},{2,3},{3,0},{4,5},{5,6},{6,7},{7,4},{8,9},{9,10},{10,1... | collective-permute-start | bytes 786440 | tf_op jit(solution)/shard_map/ppermute | solution.py:286
  623.3 49.4 %all-to-all-start.5 = ((bf16[4,64,1024]{2,1,0:T(8,128)(2,1)}), bf16[4,64,1024]{2,1,0:T(8,128)(2,1)}, u32[]{:S(2)}, u32[]{:S(2)}) async-start(bf16[4,64,1024]{2,1,0:T(8,128)(2,1)} %get-tuple-element.46), calls=%async_computation.5 | async-start | bytes 1048576 | tf_op jit(solution)/shard_map/all_to_all | solution.py:276
  628.4 93.0 %reduce-scatter.16.cloned.1.call-start = ((), (), s32[]{:S(2)}) async-start(), calls=%async_computation.22 | async-start | bytes 655360 | tf_op jit(solution)/shard_map/reduce_scatter | solution.py:336
  628.4 38.0 %collective-permute-start.52 = (bf16[128,1024]{1,0:T(8,128)(2,1)S(1)}, bf16[128,1024]{1,0:T(8,128)(2,1)S(1)}, u32[]{:S(2)}, u32[]{:S(2)}) collective-permute-start(bf16[128,1024]{1,0:T(8,128)(2,1)S(1)} %get-tuple-element.202), channel_id=1, source_target_pairs={{0,2},{1,3},{2,0},{3,1},{4,6},{5,7},{6,4},{7,5},{8,10},{9,11},{10,... | collective-permute-start | bytes 786440 | tf_op jit(solution)/shard_map/ppermute | solution.py:286
  632.6 34.5 %collective-permute-start.53 = (bf16[128,1024]{1,0:T(8,128)(2,1)S(1)}, bf16[128,1024]{1,0:T(8,128)(2,1)S(1)}, u32[]{:S(2)}, u32[]{:S(2)}) collective-permute-start(bf16[128,1024]{1,0:T(8,128)(2,1)S(1)} %get-tuple-element.201), channel_id=1, source_target_pairs={{0,3},{1,0},{2,1},{3,2},{4,7},{5,4},{6,5},{7,6},{8,11},{9,8},{10,9... | collective-permute-start | bytes 786440 | tf_op jit(solution)/shard_map/ppermute | solution.py:286
  675.9 139.8 %reduce-scatter.12.cloned.1.call-start = ((), (), s32[]{:S(2)}) async-start(), calls=%async_computation.20 | async-start | bytes 1310720 | tf_op jit(solution)/shard_map/reduce_scatter | solution.py:336
  681.3 13.1 %collective-permute-start.44 = (bf16[2,256,1024]{2,1,0:T(8,128)(2,1)}, bf16[2,256,1024]{2,1,0:T(8,128)(2,1)}, u32[]{:S(2)}, u32[]{:S(2)}) collective-permute-start(bf16[2,256,1024]{2,1,0:T(8,128)(2,1)} %pad_maximum_fusion.9), channel_id=1, source_target_pairs={{0,4},{4,0},{1,5},{5,1},{2,6},{6,2},{3,7},{7,3},{8,12},{12,8},{9,1... | collective-permute-start | bytes 3145736 | tf_op jit(solution)/shard_map/ppermute | solution.py:227
  681.5 16.4 %collective-permute-start.54 = (bf16[2,1024,256]{2,1,0:T(8,128)(2,1)S(1)}, bf16[2,1024,256]{2,1,0:T(8,128)(2,1)}, u32[]{:S(2)}, u32[]{:S(2)}) collective-permute-start(bf16[2,1024,256]{2,1,0:T(8,128)(2,1)S(1)} %pad_maximum_fusion.11), channel_id=1, source_target_pairs={{0,4},{4,0},{1,5},{5,1},{2,6},{6,2},{3,7},{7,3},{8,12},{12,8},{9,1... | collective-permute-start | bytes 3145736 | tf_op jit(solution)/shard_map/ppermute | solution.py:227
  692.7 25.4 %collective-permute-start.74 = (bf16[512,256]{1,0:T(8,128)(2,1)S(1)}, bf16[512,256]{1,0:T(8,128)(2,1)S(1)}, u32[]{:S(2)}, u32[]{:S(2)}) collective-permute-start(bf16[512,256]{1,0:T(8,128)(2,1)S(1)} %pad_maximum_fusion.28), channel_id=1, source_target_pairs={{0,4},{4,0},{1,5},{5,1},{2,6},{6,2},{3,7},{7,3},{8,12},{12,8},{9,1... | collective-permute-start | bytes 786440 | tf_op jit(solution)/shard_map/ppermute | solution.py:227
  692.8 25.3 %collective-permute-start.75 = (bf16[512,256]{1,0:T(8,128)(2,1)S(1)}, bf16[512,256]{1,0:T(8,128)(2,1)S(1)}, u32[]{:S(2)}, u32[]{:S(2)}) collective-permute-start(bf16[512,256]{1,0:T(8,128)(2,1)S(1)} %pad_maximum_fusion.29), channel_id=1, source_target_pairs={{0,8},{8,0},{1,9},{9,1},{2,10},{10,2},{3,11},{11,3},{4,12},{12,4},... | collective-permute-start | bytes 786440 | tf_op jit(solution)/shard_map/ppermute | solution.py:229
  696.1 17.2 %collective-permute-start.45 = (bf16[256,1024]{1,0:T(8,128)(2,1)S(1)}, bf16[256,1024]{1,0:T(8,128)(2,1)S(1)}, u32[]{:S(2)}, u32[]{:S(2)}) collective-permute-start(bf16[256,1024]{1,0:T(8,128)(2,1)S(1)} %fusion.34), channel_id=1, source_target_pairs={{0,8},{8,0},{1,9},{9,1},{2,10},{10,2},{3,11},{11,3},{4,12},{12,4},... | collective-permute-start | bytes 1572872 | tf_op jit(solution)/shard_map/ppermute | solution.py:229
  697.1 21.0 %collective-permute-start.76 = (bf16[512,256]{1,0:T(8,128)(2,1)S(1)}, bf16[512,256]{1,0:T(8,128)(2,1)S(1)}, u32[]{:S(2)}, u32[]{:S(2)}) collective-permute-start(bf16[512,256]{1,0:T(8,128)(2,1)S(1)} %pad_maximum_fusion.30), channel_id=1, source_target_pairs={{0,12},{4,8},{8,4},{12,0},{1,13},{5,9},{9,5},{13,1},{2,14},{6,10},... | collective-permute-start | bytes 786440 | tf_op jit(solution)/shard_map/ppermute | solution.py:230
  701.5 28.8 %collective-permute-start.55 = (bf16[1024,256]{1,0:T(8,128)(2,1)}, bf16[1024,256]{1,0:T(8,128)(2,1)}, u32[]{:S(2)}, u32[]{:S(2)}) collective-permute-start(bf16[1024,256]{1,0:T(8,128)(2,1)} %fusion.26), channel_id=1, source_target_pairs={{0,8},{8,0},{1,9},{9,1},{2,10},{10,2},{3,11},{11,3},{4,12},{12,4},... | collective-permute-start | bytes 1572872 | tf_op jit(solution)/shard_map/ppermute | solution.py:229
  716.6 24.4 %collective-permute-start.47 = (bf16[256,1024]{1,0:T(8,128)(2,1)}, bf16[256,1024]{1,0:T(8,128)(2,1)}, u32[]{:S(2)}, u32[]{:S(2)}) collective-permute-start(bf16[256,1024]{1,0:T(8,128)(2,1)} %get-tuple-element.169), channel_id=1, source_target_pairs={{0,8},{8,0},{1,9},{9,1},{2,10},{10,2},{3,11},{11,3},{4,12},{12,4},... | collective-permute-start | bytes 1572872 | tf_op jit(solution)/shard_map/ppermute | solution.py:229
  719.9 34.7 %collective-permute-start.77 = (bf16[4,512,256]{2,1,0:T(8,128)(2,1)}, bf16[4,512,256]{2,1,0:T(8,128)(2,1)}, u32[]{:S(2)}, u32[]{:S(2)}) collective-permute-start(bf16[4,512,256]{2,1,0:T(8,128)(2,1)} %pad_maximum_fusion.12), channel_id=1, source_target_pairs={{0,16},{16,0},{1,17},{17,1},{2,18},{18,2},{3,19},{19,3},{4,20},{20... | collective-permute-start | bytes 3145736 | tf_op jit(solution)/shard_map/ppermute | solution.py:349
  725.4 17.0 %collective-permute-start.46 = (bf16[256,1024]{1,0:T(8,128)(2,1)}, bf16[256,1024]{1,0:T(8,128)(2,1)S(1)}, u32[]{:S(2)}, u32[]{:S(2)}) collective-permute-start(bf16[256,1024]{1,0:T(8,128)(2,1)} %get-tuple-element.169), channel_id=1, source_target_pairs={{0,4},{4,0},{1,5},{5,1},{2,6},{6,2},{3,7},{7,3},{8,12},{12,8},{9,1... | collective-permute-start | bytes 1572872 | tf_op jit(solution)/shard_map/ppermute | solution.py:227
  746.6 23.2 %all-to-all-start.6 = ((bf16[4,64,1024]{2,1,0:T(8,128)(2,1)}), bf16[4,64,1024]{2,1,0:T(8,128)(2,1)S(1)}, u32[]{:S(2)}, u32[]{:S(2)}) async-start(bf16[4,64,1024]{2,1,0:T(8,128)(2,1)} %bitcast.135), calls=%async_computation.6 | async-start | bytes 1048576 | tf_op jit(solution)/shard_map/all_to_all | solution.py:276
  806.5 54.9 %all-to-all-start.7 = ((bf16[4,192,1024]{2,1,0:T(8,128)(2,1)}), bf16[4,192,1024]{2,1,0:T(8,128)(2,1)}, u32[]{:S(2)}, u32[]{:S(2)}) async-start(bf16[4,192,1024]{2,1,0:T(8,128)(2,1)} %pad_maximum_fusion.4), calls=%async_computation.7 | async-start | bytes 3145728 | tf_op jit(solution)/shard_map/all_to_all | solution.py:276
  810.9 77.1 %reduce-scatter.10.cloned.1.call-start = ((), (), s32[]{:S(2)}) async-start(), calls=%async_computation.19 | async-start | bytes 655360 | tf_op jit(solution)/shard_map/reduce_scatter | solution.py:336
  817.9 24.2 %collective-permute-start.70 = (bf16[256,256]{1,0:T(8,128)(2,1)}, bf16[256,256]{1,0:T(8,128)(2,1)S(1)}, u32[]{:S(2)}, u32[]{:S(2)}) collective-permute-start(bf16[256,256]{1,0:T(8,128)(2,1)} %pad_maximum_fusion.34), channel_id=1, source_target_pairs={{0,4},{4,0},{1,5},{5,1},{2,6},{6,2},{3,7},{7,3},{8,12},{12,8},{9,1... | collective-permute-start | bytes 393224 | tf_op jit(solution)/shard_map/ppermute | solution.py:227
  820.4 21.8 %collective-permute-start.71 = (bf16[256,256]{1,0:T(8,128)(2,1)}, bf16[256,256]{1,0:T(8,128)(2,1)S(1)}, u32[]{:S(2)}, u32[]{:S(2)}) collective-permute-start(bf16[256,256]{1,0:T(8,128)(2,1)} %pad_maximum_fusion.35), channel_id=1, source_target_pairs={{0,8},{8,0},{1,9},{9,1},{2,10},{10,2},{3,11},{11,3},{4,12},{12,4},... | collective-permute-start | bytes 393224 | tf_op jit(solution)/shard_map/ppermute | solution.py:229
  824.9 17.3 %collective-permute-start.72 = (bf16[256,256]{1,0:T(8,128)(2,1)}, bf16[256,256]{1,0:T(8,128)(2,1)S(1)}, u32[]{:S(2)}, u32[]{:S(2)}) collective-permute-start(bf16[256,256]{1,0:T(8,128)(2,1)} %pad_maximum_fusion.36), channel_id=1, source_target_pairs={{0,12},{4,8},{8,4},{12,0},{1,13},{5,9},{9,5},{13,1},{2,14},{6,10},... | collective-permute-start | bytes 393224 | tf_op jit(solution)/shard_map/ppermute | solution.py:230
  834.1 67.4 %reduce-scatter.8.cloned.1.call-start = ((), (), s32[]{:S(2)}) async-start(), calls=%async_computation.18 | async-start | bytes 1966080 | tf_op jit(solution)/shard_map/reduce_scatter | solution.py:336
  837.5 21.3 %collective-permute-start.69 = (f32[15,1024]{1,0:T(8,128)S(1)}, f32[15,1024]{1,0:T(8,128)S(1)}, u32[]{:S(2)}, u32[]{:S(2)}) collective-permute-start(f32[15,1024]{1,0:T(8,128)S(1)} %add.585), channel_id=1, source_target_pairs={{0,2},{1,3},{2,0},{3,1},{4,6},{5,7},{6,4},{7,5},{8,10},{9,11},{10,... | collective-permute-start | bytes 184328 | tf_op jit(solution)/shard_map/ppermute | solution.py:262
  842.3 24.2 %collective-permute-start.73 = (bf16[4,256,256]{2,1,0:T(8,128)(2,1)S(1)}, bf16[4,256,256]{2,1,0:T(8,128)(2,1)}, u32[]{:S(2)}, u32[]{:S(2)}) collective-permute-start(bf16[4,256,256]{2,1,0:T(8,128)(2,1)S(1)} %pad_maximum_fusion.15), channel_id=1, source_target_pairs={{0,16},{16,0},{1,17},{17,1},{2,18},{18,2},{3,19},{19,3},{4,20},{20... | collective-permute-start | bytes 1572872 | tf_op jit(solution)/shard_map/ppermute | solution.py:349
  887.9 30.5 %collective-permute-start.64 = (f32[2,1024]{1,0:T(2,128)S(1)}, f32[2,1024]{1,0:T(2,128)S(1)}, u32[]{:S(2)}, u32[]{:S(2)}) collective-permute-start(f32[2,1024]{1,0:T(2,128)S(1)} %add.579), channel_id=1, source_target_pairs={{0,2},{1,3},{2,0},{3,1},{4,6},{5,7},{6,4},{7,5},{8,10},{9,11},{10,... | collective-permute-start | bytes 24584 | tf_op jit(solution)/shard_map/ppermute | solution.py:262
  909.2 16.0 %collective-permute-start.50 = (bf16[1024,256]{1,0:T(8,128)(2,1)}, bf16[1024,256]{1,0:T(8,128)(2,1)}, u32[]{:S(2)}, u32[]{:S(2)}) collective-permute-start(bf16[1024,256]{1,0:T(8,128)(2,1)} %fusion.30), channel_id=1, source_target_pairs={{0,8},{8,0},{1,9},{9,1},{2,10},{10,2},{3,11},{11,3},{4,12},{12,4},... | collective-permute-start | bytes 1572872 | tf_op jit(solution)/shard_map/ppermute | solution.py:229
  914.2 14.9 %collective-permute-start.59 = (bf16[4,256,256]{2,1,0:T(8,128)(2,1)}, bf16[4,256,256]{2,1,0:T(8,128)(2,1)}, u32[]{:S(2)}, u32[]{:S(2)}) collective-permute-start(bf16[4,256,256]{2,1,0:T(8,128)(2,1)} %pad_maximum_fusion.14), channel_id=1, source_target_pairs={{0,16},{16,0},{1,17},{17,1},{2,18},{18,2},{3,19},{19,3},{4,20},{20... | collective-permute-start | bytes 1572872 | tf_op jit(solution)/shard_map/ppermute | solution.py:349
  (138 other events, 2017.5 us)
Sparse Core Ops, SparseCore 0:
  34.4 37.2 all-gather.4
  73.9 84.5 all-gather.6
  229.5 115.7 all-gather.8
  525.6 20.9 reduce-scatter.13
  548.8 43.3 reduce-scatter.17
  594.3 59.2 reduce-scatter.19
  676.0 25.9 reduce-scatter.15
  704.3 25.5 reduce-scatter.11
  834.2 22.6 reduce-scatter.9
  866.6 34.8 reduce-scatter.7

commit v3 on v2

--- a/solution.py
+++ b/solution.py
@@ -263,6 +263,16 @@
                 bits *= 2
         return value
 
+    def column_vectors(self, vector):
+        size = self.count(self.cols)
+        me = lax.axis_index(self.cols)
+        parts, spots = [vector], [me]
+        for step in range(1, size):
+            pairs = [(i, (i + step) % size) for i in range(size)]
+            parts.append(lax.ppermute(vector, self.cols, pairs))
+            spots.append((me + size - step) % size)
+        return self.place(parts, spots)
+
     def ring_index(self):
         return lax.axis_index("cs") * self.sizes["rb"] + lax.axis_index("rb")
 
@@ -401,8 +411,6 @@
 
     def gather_weights(relative, absolute, order=None):
         pieces = relative + absolute
-        if order is not None:
-            pieces, _ = lax.optimization_barrier((pieces, order))
         sizes = [piece.shape[1] for piece in pieces]
         parts = layout.team_send(layout.pick(jnp.concatenate(pieces, axis=1)))
         at = sum(piece.shape[1] for piece in relative)
@@ -411,7 +419,10 @@
             groups.append(jnp.stack([part[:at] for part in parts], axis=1))
         if absolute:
             groups.append(layout.place([part[at:] for part in parts], layout.spots()).transpose(1, 0, 2))
-        wide = layout.widen(jnp.concatenate(groups))
+        piece = jnp.concatenate(groups)
+        if order is not None:
+            piece, _ = lax.optimization_barrier((piece, order))
+        wide = layout.widen(piece)
         out, at = [], 0
         for index, size in enumerate(sizes):
             weight = wide[:, at:at + size].reshape(-1, wide.shape[2])
@@ -429,7 +440,7 @@
     heads = columns
 
     by_col = jnp.concatenate([selfbias.reshape(-1), crossbias.reshape(-1), upbias])
-    by_col = lax.all_gather(by_col, layout.cols, axis=0, tiled=False).reshape(columns, -1)
+    by_col = layout.column_vectors(by_col)
     block = selfbias.shape[1]
     head_biases = lax.dynamic_index_in_dim(
         by_col[:, : 4 * block].reshape(columns, 4, 4, HD), me, 2, keepdims=False
@@ -438,7 +449,9 @@
         by_col[:, 4 * block:].reshape(columns, 4, -1), me, 1, keepdims=False
     ).reshape(1, -1)
     by_row = jnp.concatenate([selfshift[None], crossshift[None], downbias[None], normgain, normshift])
-    by_row = lax.all_gather(by_row, ("rb", "rx", "rc"), axis=1, tiled=True)
+    if layout.sizes["rb"] > 1:
+        by_row = lax.all_gather(by_row, "rb", axis=1, tiled=True)
+    by_row = layout.team_features(layout.place(layout.team_parts(by_row), layout.spots()))
     self_shift, cross_shift, down_bias = by_row[0], by_row[1], by_row[2]
     gains, shifts = by_row[3:6], by_row[6:9]
 
@@ -451,27 +464,29 @@
     sequence_prefix = prefixes
     if layout.sizes["sq"] > 1:
         sequence_prefix = lax.dynamic_slice_in_dim(prefixes, lax.axis_index("sq"), 1, 0)
+
+    kv_w, self_w = gather_weights([column_rows(crosskv)], [split_rows(selfproj)])
+    encoder_all = jnp.concatenate(layout.team_parts(by_token(encoder)), axis=1)
+    pair = contract(kv_w, encoder_all, 1, 1).reshape(heads, 2, HD, group)
+    pair_bias = jnp.stack([jnp.zeros_like(head_biases[:, 3]), head_biases[:, 3]], axis=1)
+    pair = (pair + pair_bias[..., None]).astype(BF16).reshape(heads, 2 * HD, group)
 
     qkv = contract(qkv_w, tokens_all, 1, 1).reshape(heads, 3, HD, group)
     qkv_bias = jnp.stack([head_biases[:, 0], jnp.zeros_like(head_biases[:, 0]), head_biases[:, 1]], axis=1)
     factor = jnp.array([SCALE, 1.0, 1.0], F32)[None, :, None, None]
     qkv = ((qkv + qkv_bias[..., None]) * factor).astype(BF16).reshape(heads, 3 * HD, group)
     self_set = layout.ring_exchange(qkv)
+    self_set, pair = lax.optimization_barrier((self_set, pair))
+    cross_set = layout.ring_trickle(pair)
     self_out, self_low, self_lse = flash_forward(sequence_prefix, self_set, 0, self_set, 1, 2, True)
+    self_low, cross_set = lax.optimization_barrier((self_low, cross_set))
     attended = layout.ring_exchange(self_low).reshape(heads * HD, group)
-
-    kv_w, self_w, query_w, cross_w = gather_weights(
-        [column_rows(crosskv)],
-        [split_rows(selfproj), column_rows(crossquery[:, None]), split_rows(crossproj)],
-        tokens_all,
+    spots = layout.spots()
+    query_w, cross_w = gather_weights(
+        [], [column_rows(crossquery[:, None]), split_rows(crossproj)], attended
     )
-    encoder_all = jnp.concatenate(layout.team_parts(by_token(encoder)), axis=1)
-    up_w, down_w = gather_weights([], [column_rows(upweight[:, None]), split_rows(downweight)], encoder_all)
-    pair = contract(kv_w, encoder_all, 1, 1).reshape(heads, 2, HD, group)
-    pair_bias = jnp.stack([jnp.zeros_like(head_biases[:, 3]), head_biases[:, 3]], axis=1)
-    pair = (pair + pair_bias[..., None]).astype(BF16).reshape(heads, 2 * HD, group)
-    cross_set = layout.ring_trickle(pair)
-    spots = layout.spots()
+    up_w, down_w = gather_weights([], [column_rows(upweight[:, None]), split_rows(downweight)], query_w)
+
     upstream = layout.team_send(layout.pick(by_token(cotangent).reshape(4, own_rows, -1)))
     upstream = layout.team_features(layout.place(upstream, spots)).astype(F32)
 
@@ -508,13 +523,14 @@
     second_grad = third_grad + reduce_tokens(contract(pre_low, up_w, 1, 0))
     down_sum = layout.over_columns(layout.out_of_order(contract(hidden_act, down_all, 0, 0)))
     up_sum = layout.over_columns(layout.out_of_order(contract(pre_low, second_all, 0, 0)))
-    upweight_grad, downweight_grad = layout.weight_grads([], [up_sum, down_sum])
     mid_grad, second_gain, second_shift = norm_backward(second_grad, second_normed, second_inverse, gains[1])
     cross_own = mid_grad.astype(BF16)
     cross_all = gather_tokens(cross_own)
     crossed_grad = contract(cross_w, cross_all, 1, 1).astype(BF16).reshape(heads, HD, group)
     crossed_grad = layout.ring_exchange(crossed_grad)
-    crossproj_sum = layout.over_columns(layout.out_of_order(contract(crossed, cross_all, 1, 0)))
+    crossproj_part = contract(crossed, cross_all, 1, 0).astype(BF16)
+    crossed_grad, crossproj_part = lax.optimization_barrier((crossed_grad, crossproj_part))
+    crossproj_sum = layout.over_columns(layout.out_of_order(crossproj_part))
     dquery, dkeys, dvalues = flash_backward(
         sequence_prefix, cross_query, 0, cross_set, 0, 1, crossed_grad, cross_out, cross_lse, False
     )
@@ -524,9 +540,6 @@
     dpair = layout.ring_trickle(jnp.concatenate([dkeys, dvalues], axis=1)).reshape(heads * 2 * HD, group)
     crossquery_sum = layout.over_columns(layout.out_of_order(contract(dquery, first_all, 1, 0)))
     crosskv_sum = layout.over_columns(contract(dpair, encoder_all, 1, 0))
-    crosskv_grad, crossproj_grad, crossquery_grad = layout.weight_grads(
-        [crosskv_sum], [crossproj_sum, crossquery_sum]
-    )
     encoder_grad = layout.team_total(layout.feature_parts(contract(dpair, kv_w, 0, 0)))
     encoder_grad = layout.unhalves(encoder_grad)
     low_grad, first_gain, first_shift = norm_backward(first_grad, first_normed, first_inverse, gains[0])
@@ -534,10 +547,17 @@
     self_all = layout.place(layout.team_parts(self_own), spots).reshape(group, width)
     attended_grad = contract(self_w, self_all, 1, 1).astype(BF16).reshape(heads, HD, group)
     attended_grad = layout.ring_exchange(attended_grad)
-    selfproj_sum = layout.over_columns(layout.out_of_order(contract(attended, self_all, 1, 0)))
+    selfproj_part = contract(attended, self_all, 1, 0).astype(BF16)
+    sums = (up_sum, down_sum, crosskv_sum, crossproj_sum, crossquery_sum)
+    attended_grad, selfproj_part, sums = lax.optimization_barrier((attended_grad, selfproj_part, sums))
+    up_sum, down_sum, crosskv_sum, crossproj_sum, crossquery_sum = sums
+    early_grads = layout.weight_grads([crosskv_sum], [crossproj_sum, crossquery_sum, up_sum, down_sum])
+    selfproj_sum = layout.over_columns(layout.out_of_order(selfproj_part))
     dq, dk, dv = flash_backward(
         sequence_prefix, self_set, 0, self_set, 1, 2, attended_grad, self_out, self_lse, True
     )
+    dq, dk, dv, early_grads, selfproj_sum = lax.optimization_barrier((dq, dk, dv, early_grads, selfproj_sum))
+    crosskv_grad, crossproj_grad, crossquery_grad, upweight_grad, downweight_grad = early_grads
     self_bias_sums = (jnp.sum(dq.astype(F32), axis=(0, 2)), jnp.sum(dv.astype(F32), axis=(0, 2)))
     dqkv = layout.ring_exchange(jnp.concatenate([dq, dk, dv], axis=1)).reshape(heads * 3 * HD, group)
     selfqkv_sum = layout.over_columns(contract(dqkv, tokens_all, 1, 0))

time: 953 us -> 905 us (0.950)
  waiting for transfers between devices: 380 us -> 335 us
  blocking collectives: 59.4 us -> 78 us
  starting transfers between devices: 102 us -> 89.4 us
    ppermute x6, waiting for transfers between devices: 81 us -> 22.7 us  [ring_trickle(): lax.ppermute(pick(step), self.ring, [(i, (i + step) % size) for i in rang...]
    all_to_all x7 -> x5, waiting for transfers between devices: 101 us -> 50.8 us  [ring_exchange(): lax.all_to_all(self.flip(blocks, 'cs', 'rb'), self.ring, 0, 0, tiled=True)]
    all_gather x3 -> x4, waiting for transfers between devices: 10.8 us -> 55.4 us  [widen(): return lax.all_gather(piece[None], self.cols, axis=0, tiled=True)]
    all_to_all x1 -> x3, blocking collectives: 37.2 us -> 78 us  [ring_exchange(): lax.all_to_all(self.flip(blocks, 'cs', 'rb'), self.ring, 0, 0, tiled=True)]
    all_gather x2 -> x0, blocking collectives: 22.2 us -> none  [the longest x1 13.4 us: shards(): lax.all_gather(by_col, layout.cols, axis=0, tiled=False)]
    ppermute x22 -> x23, waiting for transfers between devices: 133 us -> 148 us  [swap(): return lax.ppermute(value, 'rx', [(0, 1), (1, 0)])]
    ppermute x10, waiting for transfers between devices: 27.6 us -> 12.5 us  [total(): value = value + lax.ppermute(value, name, pairs)]
    reduce_scatter x7, waiting for transfers between devices: 8.44 us -> 21.2 us  [over_columns(): lax.psum_scatter(partial.astype(BF16), self.cols, scatter_dimension=0, ti...]
  transfers between devices with their start and end apart: 95 -> 99, of which waited for: 42 -> 45; matrix products, arithmetic and copies ran while one was open for 20% -> 19% of each run, Pallas kernels for 14% -> 15%
where the time goes in v3:
time: 905 us; the launch traced here: 892 us
  waiting for transfers between devices  335 us (37%)
  Pallas kernels  133 us (15%)
  local copies, waits for them, and re-layouts  108 us (12%)
  starting transfers between devices  89.4 us (10%)
  matrix products  79.6 us (9%)
  blocking collectives  78 us (9%)
  other arithmetic  50.5 us (6%)
  between operations  17.3 us (2%)
    ppermute x23, waiting for transfers between devices, swap(): return lax.ppermute(value, 'rx', [(0, 1), (1, 0)])  148 us
    pallas_call x2, Pallas kernels, flash_backward(): pl.pallas_call(functools.partial(backward_kernel, masked, bq, bk), out_sh...  81.9 us
    dot_general x21, matrix products, contract(): lax.dot_general(left, right, (((left_dim,), (right_dim,)), ((), ())), pre...  79.6 us
    all_to_all x3, blocking collectives, ring_exchange(): lax.all_to_all(self.flip(blocks, 'cs', 'rb'), self.ring, 0, 0, tiled=True)  78 us
    all_gather x4, waiting for transfers between devices, widen(): return lax.all_gather(piece[None], self.cols, axis=0, tiled=True)  55.4 us
    pallas_call x2, Pallas kernels, flash_forward(): pl.pallas_call(functools.partial(forward_kernel, masked, bq, bk), out_sha...  51.1 us
    all_to_all x5, waiting for transfers between devices, ring_exchange(): lax.all_to_all(self.flip(blocks, 'cs', 'rb'), self.ring, 0, 0, tiled=True)  50.8 us
    unnamed x193, local copies, waits for them, and re-layouts  30.5 us
  transfers between devices with their start and end apart: 99, of which 45 were waited for; matrix products, arithmetic and copies ran while one was open for 19% of the time, Pallas kernels for 15%

profile of v3, /device:TPU:0, one launch (start us, length us, event | category | flops | bytes accessed | tf_op | source)
XLA Modules:
  0.0 891.7 jit_solution(9443076173345501698)
XLA Ops:
  12.6 3.1 collective-permute-start.6
  15.6 2.6 collective-permute-start.7
  34.5 7.8 collective-permute-done.10
  49.1 15.2 %all-gather.5.cloned.1.call-done = bf16[4,192,1024]{2,1,0:T(8,128)(2,1)} async-done(((bf16[1,192,1024]{2,1,0:T(8,128)(2,1)}), bf16[4,192,1024]{2,1,0:T(8,128)(2,1)}) %all-gather.5.cloned.1.call-update) | async-done | bytes 1572880 | tf_op jit(solution)/shard_map/all_gather | solution.py:329
  64.3 4.4 multiply_convert_fusion.1
  68.7 3.7 all-to-all-start
  73.9 11.3 %collective-permute-done.13 = bf16[1024,256]{1,0:T(8,128)(2,1)S(1)} collective-permute-done((bf16[1024,256]{1,0:T(8,128)(2,1)S(1)}, bf16[1024,256]{1,0:T(8,128)(2,1)S(1)}, u32[]{:S(2)}, u32[]{:S(2)}) %collective-permute-start.13) | collective-permute-done | bytes 524320 | tf_op jit(solution)/shard_map/ppermute | solution.py:229
  91.0 40.1 %all-gather.7.cloned.1.call-done = bf16[4,192,1024]{2,1,0:T(8,128)(2,1)} async-done(((bf16[1,192,1024]{2,1,0:T(8,128)(2,1)}), bf16[4,192,1024]{2,1,0:T(8,128)(2,1)}) %all-gather.7.cloned.1.call-update) | async-done | bytes 1572880 | tf_op jit(solution)/shard_map/all_gather | solution.py:329
  132.4 2.9 add_convert_fusion.1
  137.5 2.5 collective-permute-start.16
  141.4 20.7 %attend_self.1 = (f32[4,64,1024]{2,1,0:T(8,128)}, bf16[4,64,1024]{2,1,0:T(8,128)(2,1)}, f32[4,1,1024]{2,1,0:T(1,128)}) custom-call(s32[1]{0:T(128)S(6)} %copy.588.prefix_ref, bf16[4,192,1024]{2,1,0:T(8,128)(2,1)} %copy-done.20, bf16[4,192,1024]{2,1,0:T(8,128)(2,1)} %copy-done.20, bf16[4,192,1024]{2,1,0:T(8,128)(2,1)} %copy-done.20), custom_call_target="tpu_custom_call" | custom-call | flops 4294967296 | bytes 3670016 | tf_op jit(solution)/shard_map/attend_self/pallas_call | solution.py:78
  162.2 3.5 all-to-all-start.1
  167.0 13.0 %all-to-all-done.1 = bf16[4,64,1024]{2,1,0:T(8,128)(2,1)S(1)} async-done(((bf16[4,64,1024]{2,1,0:T(8,128)(2,1)}), bf16[4,64,1024]{2,1,0:T(8,128)(2,1)S(1)}, u32[]{:S(2)}, u32[]{:S(2)}) %all-to-all-start.1) | async-done | bytes 524320 | tf_op jit(solution)/shard_map/all_to_all | solution.py:286
  192.6 3.5 collective-permute-done.25
  210.3 7.7 collective-permute-done.19
  227.1 9.0 %collective-permute-done.27 = bf16[256,1024]{1,0:T(8,128)(2,1)} collective-permute-done((bf16[256,1024]{1,0:T(8,128)(2,1)S(1)}, bf16[256,1024]{1,0:T(8,128)(2,1)}, u32[]{:S(2)}, u32[]{:S(2)}) %collective-permute-start.27) | collective-permute-done | bytes 524320 | tf_op jit(solution)/shard_map/ppermute | solution.py:229
  237.5 4.2 collective-permute-done.35
  248.7 27.8 %all_to_all.40.q_ref = bf16[4,64,1024]{2,1,0:T(8,128)(2,1)} all-to-all(bf16[4,64,1024]{2,1,0:T(8,128)(2,1)S(1)} %fusion.22), channel_id=1, replica_groups=mesh['dp'=2,'rb'=1,'rx'=2,'rc'=2,'sq'=1,'cs'=4] {'cs'}, dimensions={0} | all-to-all | bytes 1048576 | tf_op jit(solution)/shard_map/all_to_all | solution.py:286
  276.5 30.4 %attend_cross.1 = (f32[4,64,1024]{2,1,0:T(8,128)}, bf16[4,64,1024]{2,1,0:T(8,128)(2,1)}, f32[4,1,1024]{2,1,0:T(1,128)}) custom-call(s32[1]{0:T(128)S(6)} %copy.588.prefix_ref, bf16[4,64,1024]{2,1,0:T(8,128)(2,1)} %all_to_all.40.q_ref, bf16[4,128,1024]{2,1,0:T(8,128)(2,1)} %copy-done.23, bf16[4,128,1024]{2,1,0:T(8,128)(2,1)} %copy-done.23), custom_call_target="tpu_custom_call" | custom-call | flops 4294967296 | bytes 3670016 | tf_op jit(solution)/shard_map/attend_cross/pallas_call | solution.py:78
  306.9 35.2 %all_to_all.41 = bf16[4,64,1024]{2,1,0:T(8,128)(2,1)S(1)} all-to-all(bf16[4,64,1024]{2,1,0:T(8,128)(2,1)} %get-tuple-element.59), channel_id=1, replica_groups=mesh['dp'=2,'rb'=1,'rx'=2,'rc'=2,'sq'=1,'cs'=4] {'cs'}, dimensions={0} | all-to-all | bytes 1048576 | tf_op jit(solution)/shard_map/all_to_all | solution.py:286
  343.4 2.4 collective-permute-done.29
  347.5 12.9 %collective-permute-done.30 = bf16[256,1024]{1,0:T(8,128)(2,1)S(1)} collective-permute-done((bf16[256,1024]{1,0:T(8,128)(2,1)S(1)}, bf16[256,1024]{1,0:T(8,128)(2,1)S(1)}, u32[]{:S(2)}, u32[]{:S(2)}) %collective-permute-start.30) | collective-permute-done | bytes 524320 | tf_op jit(solution)/shard_map/ppermute | solution.py:229
  362.4 12.0 %collective-permute-done.32 = bf16[256,1024]{1,0:T(8,128)(2,1)S(1)} collective-permute-done((bf16[256,1024]{1,0:T(8,128)(2,1)S(1)}, bf16[256,1024]{1,0:T(8,128)(2,1)S(1)}, u32[]{:S(2)}, u32[]{:S(2)}) %collective-permute-start.32) | collective-permute-done | bytes 524320 | tf_op jit(solution)/shard_map/ppermute | solution.py:229
  374.5 2.9 fusion.124
  377.5 13.3 %multiply_convert_fusion = (bf16[1024,1024]{1,0:T(8,128)(2,1)S(1)}, f32[1024,1024]{1,0:T(8,128)S(1)}, f32[1024,1024]{1,0:T(8,128)S(1)}) fusion(f32[1024]{0:T(1024)S(1)} %bitcast.698, bf16[1024,1024]{1,0:T(8,128)(2,1)S(1)} %bitcast.602, bf16[256,1024]{1,0:T(8,128)(2,1)} %collective-permute-done.33, bf16[256,1024]{1,0:T(8,128)(2,1)S(1)} %collective-permute-done.32, ...), kind=kOutput, calls=%fused_computation.4 | convolution fusion | flops 2225078272 | bytes 14684160 | tf_op jit(solution)/shard_map/dot_general | solution.py:202
  396.2 4.8 collective-permute-done.43
  405.1 12.1 %collective-permute-done.38 = bf16[256,1024]{1,0:T(8,128)(2,1)S(1)} collective-permute-done((bf16[256,1024]{1,0:T(8,128)(2,1)S(1)}, bf16[256,1024]{1,0:T(8,128)(2,1)S(1)}, u32[]{:S(2)}, u32[]{:S(2)}) %collective-permute-start.38) | collective-permute-done | bytes 524320 | tf_op jit(solution)/shard_map/ppermute | solution.py:229
  420.6 12.5 %collective-permute-done.46 = bf16[256,1024]{1,0:T(8,128)(2,1)S(1)} collective-permute-done((bf16[256,1024]{1,0:T(8,128)(2,1)S(1)}, bf16[256,1024]{1,0:T(8,128)(2,1)S(1)}, u32[]{:S(2)}, u32[]{:S(2)}) %collective-permute-start.46) | collective-permute-done | bytes 524320 | tf_op jit(solution)/shard_map/ppermute | solution.py:229
  435.0 6.6 convert_reduce_fusion
  441.6 4.9 fusion.134
  446.5 3.8 convolution_convert_fusion
  452.0 2.5 collective-permute-done.48
  456.2 12.8 %collective-permute-done.49 = bf16[256,1024]{1,0:T(8,128)(2,1)S(1)} collective-permute-done((bf16[256,1024]{1,0:T(8,128)(2,1)S(1)}, bf16[256,1024]{1,0:T(8,128)(2,1)S(1)}, u32[]{:S(2)}, u32[]{:S(2)}) %collective-permute-start.49) | collective-permute-done | bytes 524320 | tf_op jit(solution)/shard_map/ppermute | solution.py:229
  473.3 12.0 %collective-permute-done.51 = bf16[256,1024]{1,0:T(8,128)(2,1)S(1)} collective-permute-done((bf16[256,1024]{1,0:T(8,128)(2,1)S(1)}, bf16[256,1024]{1,0:T(8,128)(2,1)S(1)}, u32[]{:S(2)}, u32[]{:S(2)}) %collective-permute-start.51) | collective-permute-done | bytes 524320 | tf_op jit(solution)/shard_map/ppermute | solution.py:229
  485.4 5.1 convolution_convert_fusion.1
  490.6 3.0 convolution_convert_fusion.8
  493.5 3.5 all-to-all-start.4
  497.0 2.9 convolution_convert_fusion.7
  499.9 24.6 %all-to-all-done.4.g_ref = bf16[4,64,1024]{2,1,0:T(8,128)(2,1)S(1)} async-done(((bf16[4,64,1024]{2,1,0:T(8,128)(2,1)}), bf16[4,64,1024]{2,1,0:T(8,128)(2,1)S(1)}, u32[]{:S(2)}, u32[]{:S(2)}) %all-to-all-start.4) | async-done | bytes 524320 | tf_op jit(solution)/shard_map/all_to_all | solution.py:286
  525.4 48.7 %attend_cross_back.1 = (bf16[4,64,1024]{2,1,0:T(8,128)(2,1)}, bf16[4,64,1024]{2,1,0:T(8,128)(2,1)}, bf16[4,64,1024]{2,1,0:T(8,128)(2,1)}) custom-call(s32[1]{0:T(128)S(6)} %copy.588.prefix_ref, bf16[4,64,1024]{2,1,0:T(8,128)(2,1)} %all_to_all.40.q_ref, bf16[4,64,1024]{2,1,0:T(8,128)(2,1)} %copy-done.35, f32[4,64,1024]{2,1,0:T(8,128)} %get-tuple-element.61.o_ref, ...), custom_call_target="tpu_custom_call" | custom-call | flops 10737418240 | bytes 5242880 | tf_op jit(solution)/shard_map/attend_cross_back/pallas_call | solution.py:173
  574.0 15.0 %all_to_all.42 = bf16[4,64,1024]{2,1,0:T(8,128)(2,1)S(1)} all-to-all(bf16[4,64,1024]{2,1,0:T(8,128)(2,1)} %get-tuple-element.63), channel_id=1, replica_groups=mesh['dp'=2,'rb'=1,'rx'=2,'rc'=2,'sq'=1,'cs'=4] {'cs'}, dimensions={0} | all-to-all | bytes 1048576 | tf_op jit(solution)/shard_map/all_to_all | solution.py:286
  589.1 2.8 fusion.135
  599.0 7.2 collective-permute-done.58
  606.9 15.5 %collective-permute-done.59 = bf16[128,1024]{1,0:T(8,128)(2,1)S(1)} collective-permute-done((bf16[128,1024]{1,0:T(8,128)(2,1)S(1)}, bf16[128,1024]{1,0:T(8,128)(2,1)S(1)}, u32[]{:S(2)}, u32[]{:S(2)}) %collective-permute-start.59) | collective-permute-done | bytes 262176 | tf_op jit(solution)/shard_map/ppermute | solution.py:296
  628.8 2.9 convolution_convert_fusion.4
  631.7 6.3 collective-permute-done.54
  638.0 2.9 multiply_reduce_fusion.2
  644.0 4.1 convolution_convert_fusion.3
  648.2 4.8 collective-permute-done.56
  657.2 9.5 %all-to-all-start.6 = ((bf16[4,64,1024]{2,1,0:T(8,128)(2,1)}), bf16[4,64,1024]{2,1,0:T(8,128)(2,1)}, u32[]{:S(2)}, u32[]{:S(2)}) async-start(bf16[4,64,1024]{2,1,0:T(8,128)(2,1)} %bitcast.630), calls=%async_computation.6 | async-start | bytes 1048576 | tf_op jit(solution)/shard_map/all_to_all | solution.py:286
  674.0 20.4 %reduce-scatter.12.cloned.1.call-done = bf16[128,1024]{1,0:T(8,128)(2,1)} async-done(((bf16[512,1024]{1,0:T(8,128)(2,1)}), bf16[128,1024]{1,0:T(8,128)(2,1)}) %reduce-scatter.12.cloned.1.call-update) | async-done | bytes 262160 | tf_op jit(solution)/shard_map/reduce_scatter | solution.py:346
  695.5 2.5 convolution_convert_fusion.5
  703.4 10.2 %collective-permute-done.62 = bf16[768,256]{1,0:T(8,128)(2,1)S(1)} collective-permute-done((bf16[768,256]{1,0:T(8,128)(2,1)S(1)}, bf16[768,256]{1,0:T(8,128)(2,1)S(1)}, u32[]{:S(2)}, u32[]{:S(2)}) %collective-permute-start.62) | collective-permute-done | bytes 393248 | tf_op jit(solution)/shard_map/ppermute | solution.py:229
  713.6 7.3 collective-permute-done.63
  723.8 33.3 %attend_self_back.1 = (bf16[4,64,1024]{2,1,0:T(8,128)(2,1)}, bf16[4,64,1024]{2,1,0:T(8,128)(2,1)}, bf16[4,64,1024]{2,1,0:T(8,128)(2,1)}) custom-call(s32[1]{0:T(128)S(6)} %copy.588.prefix_ref, bf16[4,192,1024]{2,1,0:T(8,128)(2,1)} %copy-done.20, bf16[4,64,1024]{2,1,0:T(8,128)(2,1)} %all-to-all-done.6.g_ref, f32[4,64,1024]{2,1,0:T(8,128)} %get-tuple-element.68.o_ref, ...), custom_call_target="tpu_custom_call" | custom-call | flops 10737418240 | bytes 5242880 | tf_op jit(solution)/shard_map/attend_self_back/pallas_call | solution.py:173
  766.1 4.4 all-to-all-start.7
  772.0 4.5 fusion.136
  794.4 13.2 %all-to-all-done.7 = bf16[4,192,1024]{2,1,0:T(8,128)(2,1)} async-done(((bf16[4,192,1024]{2,1,0:T(8,128)(2,1)}), bf16[4,192,1024]{2,1,0:T(8,128)(2,1)}, u32[]{:S(2)}, u32[]{:S(2)}) %all-to-all-start.7) | async-done | bytes 1572896 | tf_op jit(solution)/shard_map/all_to_all | solution.py:286
  807.6 5.0 convolution_convert_fusion.2
  814.3 2.5 fusion.28
  821.4 7.0 collective-permute-done.82
  828.4 3.3 convolution_bitcast_fusion
  861.7 2.8 collective-permute-done.70
  876.6 2.5 fusion.32
  (607 shorter events, 232.7 us)
Async XLA Ops:
  7.2 57.1 %all-gather.5.cloned.1.call-start = ((), (), s32[]{:S(2)}) async-start(), calls=%async_computation.15 | async-start | bytes 1966080 | tf_op jit(solution)/shard_map/all_gather | solution.py:329
  12.6 16.8 %collective-permute-start.6 = (f32[2048]{0:T(1024)}, f32[2048]{0:T(1024)S(1)}, u32[]{:S(2)}, u32[]{:S(2)}) collective-permute-start(f32[2048]{0:T(1024)} %constant_dynamic-update-slice_fusion.24), channel_id=1, source_target_pairs={{0,1},{1,2},{2,3},{3,0},{4,5},{5,6},{6,7},{7,4},{8,9},{9,10},{10,1... | collective-permute-start | bytes 24584 | tf_op jit(solution)/shard_map/ppermute | solution.py:272
  15.6 14.4 %collective-permute-start.7 = (f32[2048]{0:T(1024)}, f32[2048]{0:T(1024)S(1)}, u32[]{:S(2)}, u32[]{:S(2)}) collective-permute-start(f32[2048]{0:T(1024)} %constant_dynamic-update-slice_fusion.24), channel_id=1, source_target_pairs={{0,2},{1,3},{2,0},{3,1},{4,6},{5,7},{6,4},{7,5},{8,10},{9,11},{10,... | collective-permute-start | bytes 24584 | tf_op jit(solution)/shard_map/ppermute | solution.py:272
  25.4 18.2 %collective-permute-start.1 = (bf16[1024,256]{1,0:T(8,128)(2,1)S(1)}, bf16[1024,256]{1,0:T(8,128)(2,1)S(1)}, u32[]{:S(2)}, u32[]{:S(2)}) collective-permute-start(bf16[1024,256]{1,0:T(8,128)(2,1)S(1)} %copy-done.28), channel_id=1, source_target_pairs={{0,8},{8,0},{1,9},{9,1},{2,10},{10,2},{3,11},{11,3},{4,12},{12,4},... | collective-permute-start | bytes 1572872 | tf_op jit(solution)/shard_map/ppermute | solution.py:229
  26.9 19.9 %collective-permute-start = (bf16[1024,256]{1,0:T(8,128)(2,1)S(1)}, bf16[1024,256]{1,0:T(8,128)(2,1)}, u32[]{:S(2)}, u32[]{:S(2)}) collective-permute-start(bf16[1024,256]{1,0:T(8,128)(2,1)S(1)} %copy-done.28), channel_id=1, source_target_pairs={{0,4},{4,0},{1,5},{5,1},{2,6},{6,2},{3,7},{7,3},{8,12},{12,8},{9,1... | collective-permute-start | bytes 1572872 | tf_op jit(solution)/shard_map/ppermute | solution.py:227
  28.3 102.8 %all-gather.7.cloned.1.call-start = ((), (), s32[]{:S(2)}) async-start(), calls=%async_computation.16 | async-start | bytes 1966080 | tf_op jit(solution)/shard_map/all_gather | solution.py:329
  30.0 12.2 %collective-permute-start.10 = (bf16[192,256]{1,0:T(8,128)(2,1)}, bf16[192,256]{1,0:T(8,128)(2,1)S(1)}, u32[]{:S(2)}, u32[]{:S(2)}) collective-permute-start(bf16[192,256]{1,0:T(8,128)(2,1)} %get-tuple-element.272), channel_id=1, source_target_pairs={{0,8},{8,0},{1,9},{9,1},{2,10},{10,2},{3,11},{11,3},{4,12},{12,4},... | collective-permute-start | bytes 294920 | tf_op jit(solution)/shard_map/ppermute | solution.py:229
  31.1 11.8 %collective-permute-start.11 = (bf16[192,256]{1,0:T(8,128)(2,1)}, bf16[192,256]{1,0:T(8,128)(2,1)S(1)}, u32[]{:S(2)}, u32[]{:S(2)}) collective-permute-start(bf16[192,256]{1,0:T(8,128)(2,1)} %get-tuple-element.269), channel_id=1, source_target_pairs={{0,12},{4,8},{8,4},{12,0},{1,13},{5,9},{9,5},{13,1},{2,14},{6,10},... | collective-permute-start | bytes 294920 | tf_op jit(solution)/shard_map/ppermute | solution.py:230
  68.7 66.6 %all-to-all-start = ((bf16[4,192,1024]{2,1,0:T(8,128)(2,1)}), bf16[4,192,1024]{2,1,0:T(8,128)(2,1)S(1)}, u32[]{:S(2)}, u32[]{:S(2)}) async-start(bf16[4,192,1024]{2,1,0:T(8,128)(2,1)} %bitcast.24), calls=%async_computation | async-start | bytes 3145728 | tf_op jit(solution)/shard_map/all_to_all | solution.py:286
  72.4 12.8 %collective-permute-start.13 = (bf16[1024,256]{1,0:T(8,128)(2,1)S(1)}, bf16[1024,256]{1,0:T(8,128)(2,1)S(1)}, u32[]{:S(2)}, u32[]{:S(2)}) collective-permute-start(bf16[1024,256]{1,0:T(8,128)(2,1)S(1)} %copy-done.29), channel_id=1, source_target_pairs={{0,8},{8,0},{1,9},{9,1},{2,10},{10,2},{3,11},{11,3},{4,12},{12,4},... | collective-permute-start | bytes 1572872 | tf_op jit(solution)/shard_map/ppermute | solution.py:229
  73.9 13.4 %collective-permute-start.12 = (bf16[1024,256]{1,0:T(8,128)(2,1)S(1)}, bf16[1024,256]{1,0:T(8,128)(2,1)}, u32[]{:S(2)}, u32[]{:S(2)}) collective-permute-start(bf16[1024,256]{1,0:T(8,128)(2,1)S(1)} %copy-done.29), channel_id=1, source_target_pairs={{0,4},{4,0},{1,5},{5,1},{2,6},{6,2},{3,7},{7,3},{8,12},{12,8},{9,1... | collective-permute-start | bytes 1572872 | tf_op jit(solution)/shard_map/ppermute | solution.py:227
  137.5 24.5 %collective-permute-start.15 = (bf16[128,1024]{1,0:T(8,128)(2,1)}, bf16[128,1024]{1,0:T(8,128)(2,1)S(1)}, u32[]{:S(2)}, u32[]{:S(2)}) collective-permute-start(bf16[128,1024]{1,0:T(8,128)(2,1)} %get-tuple-element.243), channel_id=1, source_target_pairs={{0,1},{1,2},{2,3},{3,0},{4,5},{5,6},{6,7},{7,4},{8,9},{9,10},{10,1... | collective-permute-start | bytes 786440 | tf_op jit(solution)/shard_map/ppermute | solution.py:296
  137.5 24.6 %collective-permute-start.16 = (bf16[128,1024]{1,0:T(8,128)(2,1)}, bf16[128,1024]{1,0:T(8,128)(2,1)S(1)}, u32[]{:S(2)}, u32[]{:S(2)}) collective-permute-start(bf16[128,1024]{1,0:T(8,128)(2,1)} %get-tuple-element.242), channel_id=1, source_target_pairs={{0,2},{1,3},{2,0},{3,1},{4,6},{5,7},{6,4},{7,5},{8,10},{9,11},{10,... | collective-permute-start | bytes 786440 | tf_op jit(solution)/shard_map/ppermute | solution.py:296
  140.1 22.0 %collective-permute-start.17 = (bf16[128,1024]{1,0:T(8,128)(2,1)}, bf16[128,1024]{1,0:T(8,128)(2,1)S(1)}, u32[]{:S(2)}, u32[]{:S(2)}) collective-permute-start(bf16[128,1024]{1,0:T(8,128)(2,1)} %get-tuple-element.241), channel_id=1, source_target_pairs={{0,3},{1,0},{2,1},{3,2},{4,7},{5,4},{6,5},{7,6},{8,11},{9,8},{10,9... | collective-permute-start | bytes 786440 | tf_op jit(solution)/shard_map/ppermute | solution.py:296
  162.2 17.8 %all-to-all-start.1 = ((bf16[4,64,1024]{2,1,0:T(8,128)(2,1)}), bf16[4,64,1024]{2,1,0:T(8,128)(2,1)S(1)}, u32[]{:S(2)}, u32[]{:S(2)}) async-start(bf16[4,64,1024]{2,1,0:T(8,128)(2,1)} %get-tuple-element.56), calls=%async_computation.1 | async-start | bytes 1048576 | tf_op jit(solution)/shard_map/all_to_all | solution.py:286
  165.7 80.8 %all-gather.9.cloned.1.call-start = ((), (), s32[]{:S(2)}) async-start(), calls=%async_computation.17 | async-start | bytes 1310720 | tf_op jit(solution)/shard_map/all_gather | solution.py:329
  183.3 19.1 %collective-permute-start.18 = (bf16[2,256,1024]{2,1,0:T(8,128)(2,1)S(1)}, bf16[2,256,1024]{2,1,0:T(8,128)(2,1)S(1)}, u32[]{:S(2)}, u32[]{:S(2)}) collective-permute-start(bf16[2,256,1024]{2,1,0:T(8,128)(2,1)S(1)} %pad_maximum_fusion.6), channel_id=1, source_target_pairs={{0,4},{4,0},{1,5},{5,1},{2,6},{6,2},{3,7},{7,3},{8,12},{12,8},{9,1... | collective-permute-start | bytes 3145736 | tf_op jit(solution)/shard_map/ppermute | solution.py:227
  204.0 14.0 %collective-permute-start.19 = (bf16[256,1024]{1,0:T(8,128)(2,1)S(1)}, bf16[256,1024]{1,0:T(8,128)(2,1)S(1)}, u32[]{:S(2)}, u32[]{:S(2)}) collective-permute-start(bf16[256,1024]{1,0:T(8,128)(2,1)S(1)} %fusion.64), channel_id=1, source_target_pairs={{0,8},{8,0},{1,9},{9,1},{2,10},{10,2},{3,11},{11,3},{4,12},{12,4},... | collective-permute-start | bytes 1572872 | tf_op jit(solution)/shard_map/ppermute | solution.py:229
  210.2 164.3 %all-gather.11.cloned.1.call-start = ((), (), s32[]{:S(2)}) async-start(), calls=%async_computation.18 | async-start | bytes 5242880 | tf_op jit(solution)/shard_map/all_gather | solution.py:329
  221.1 15.0 %collective-permute-start.27 = (bf16[256,1024]{1,0:T(8,128)(2,1)S(1)}, bf16[256,1024]{1,0:T(8,128)(2,1)}, u32[]{:S(2)}, u32[]{:S(2)}) collective-permute-start(bf16[256,1024]{1,0:T(8,128)(2,1)S(1)} %fusion.61), channel_id=1, source_target_pairs={{0,8},{8,0},{1,9},{9,1},{2,10},{10,2},{3,11},{11,3},{4,12},{12,4},... | collective-permute-start | bytes 1572872 | tf_op jit(solution)/shard_map/ppermute | solution.py:229
  224.9 11.4 %collective-permute-start.34 = (bf16[512,256]{1,0:T(8,128)(2,1)}, bf16[512,256]{1,0:T(8,128)(2,1)}, u32[]{:S(2)}, u32[]{:S(2)}) collective-permute-start(bf16[512,256]{1,0:T(8,128)(2,1)} %get-tuple-element.247), channel_id=1, source_target_pairs={{0,4},{4,0},{1,5},{5,1},{2,6},{6,2},{3,7},{7,3},{8,12},{12,8},{9,1... | collective-permute-start | bytes 786440 | tf_op jit(solution)/shard_map/ppermute | solution.py:227
  224.9 16.8 %collective-permute-start.35 = (bf16[512,256]{1,0:T(8,128)(2,1)S(1)}, bf16[512,256]{1,0:T(8,128)(2,1)}, u32[]{:S(2)}, u32[]{:S(2)}) collective-permute-start(bf16[512,256]{1,0:T(8,128)(2,1)S(1)} %get-tuple-element.248), channel_id=1, source_target_pairs={{0,8},{8,0},{1,9},{9,1},{2,10},{10,2},{3,11},{11,3},{4,12},{12,4},... | collective-permute-start | bytes 786440 | tf_op jit(solution)/shard_map/ppermute | solution.py:229
  226.3 17.5 %collective-permute-start.36 = (bf16[512,256]{1,0:T(8,128)(2,1)S(1)}, bf16[512,256]{1,0:T(8,128)(2,1)}, u32[]{:S(2)}, u32[]{:S(2)}) collective-permute-start(bf16[512,256]{1,0:T(8,128)(2,1)S(1)} %get-tuple-element.245), channel_id=1, source_target_pairs={{0,12},{4,8},{8,4},{12,0},{1,13},{5,9},{9,5},{13,1},{2,14},{6,10},... | collective-permute-start | bytes 786440 | tf_op jit(solution)/shard_map/ppermute | solution.py:230
  226.8 19.7 %collective-permute-start.26 = (bf16[256,1024]{1,0:T(8,128)(2,1)S(1)}, bf16[256,1024]{1,0:T(8,128)(2,1)}, u32[]{:S(2)}, u32[]{:S(2)}) collective-permute-start(bf16[256,1024]{1,0:T(8,128)(2,1)S(1)} %fusion.61), channel_id=1, source_target_pairs={{0,4},{4,0},{1,5},{5,1},{2,6},{6,2},{3,7},{7,3},{8,12},{12,8},{9,1... | collective-permute-start | bytes 1572872 | tf_op jit(solution)/shard_map/ppermute | solution.py:227
  236.1 10.4 %collective-permute-start.28 = (bf16[256,1024]{1,0:T(8,128)(2,1)}, bf16[256,1024]{1,0:T(8,128)(2,1)}, u32[]{:S(2)}, u32[]{:S(2)}) collective-permute-start(bf16[256,1024]{1,0:T(8,128)(2,1)} %collective-permute-done.27), channel_id=1, source_target_pairs={{0,4},{4,0},{1,5},{5,1},{2,6},{6,2},{3,7},{7,3},{8,12},{12,8},{9,1... | collective-permute-start | bytes 1572872 | tf_op jit(solution)/shard_map/ppermute | solution.py:227
  246.4 420.5 %reduce-scatter.10.cloned.1.call-start = ((), (), s32[]{:S(2)}) async-start(), calls=%async_computation.20 | async-start | bytes 2621440 | tf_op jit(solution)/shard_map/reduce_scatter | solution.py:346
  346.2 14.1 %collective-permute-start.30 = (bf16[256,1024]{1,0:T(8,128)(2,1)S(1)}, bf16[256,1024]{1,0:T(8,128)(2,1)S(1)}, u32[]{:S(2)}, u32[]{:S(2)}) collective-permute-start(bf16[256,1024]{1,0:T(8,128)(2,1)S(1)} %fusion.50), channel_id=1, source_target_pairs={{0,8},{8,0},{1,9},{9,1},{2,10},{10,2},{3,11},{11,3},{4,12},{12,4},... | collective-permute-start | bytes 1572872 | tf_op jit(solution)/shard_map/ppermute | solution.py:229
  361.2 13.3 %collective-permute-start.32 = (bf16[256,1024]{1,0:T(8,128)(2,1)S(1)}, bf16[256,1024]{1,0:T(8,128)(2,1)S(1)}, u32[]{:S(2)}, u32[]{:S(2)}) collective-permute-start(bf16[256,1024]{1,0:T(8,128)(2,1)S(1)} %fusion.62), channel_id=1, source_target_pairs={{0,8},{8,0},{1,9},{9,1},{2,10},{10,2},{3,11},{11,3},{4,12},{12,4},... | collective-permute-start | bytes 1572872 | tf_op jit(solution)/shard_map/ppermute | solution.py:229
  362.4 15.0 %collective-permute-start.31 = (bf16[256,1024]{1,0:T(8,128)(2,1)S(1)}, bf16[256,1024]{1,0:T(8,128)(2,1)}, u32[]{:S(2)}, u32[]{:S(2)}) collective-permute-start(bf16[256,1024]{1,0:T(8,128)(2,1)S(1)} %fusion.62), channel_id=1, source_target_pairs={{0,4},{4,0},{1,5},{5,1},{2,6},{6,2},{3,7},{7,3},{8,12},{12,8},{9,1... | collective-permute-start | bytes 1572872 | tf_op jit(solution)/shard_map/ppermute | solution.py:227
  402.6 14.6 %collective-permute-start.38 = (bf16[256,1024]{1,0:T(8,128)(2,1)S(1)}, bf16[256,1024]{1,0:T(8,128)(2,1)S(1)}, u32[]{:S(2)}, u32[]{:S(2)}) collective-permute-start(bf16[256,1024]{1,0:T(8,128)(2,1)S(1)} %fusion.44), channel_id=1, source_target_pairs={{0,8},{8,0},{1,9},{9,1},{2,10},{10,2},{3,11},{11,3},{4,12},{12,4},... | collective-permute-start | bytes 1572872 | tf_op jit(solution)/shard_map/ppermute | solution.py:229
  419.4 13.6 %collective-permute-start.46 = (bf16[256,1024]{1,0:T(8,128)(2,1)S(1)}, bf16[256,1024]{1,0:T(8,128)(2,1)S(1)}, u32[]{:S(2)}, u32[]{:S(2)}) collective-permute-start(bf16[256,1024]{1,0:T(8,128)(2,1)S(1)} %get-tuple-element.197), channel_id=1, source_target_pairs={{0,8},{8,0},{1,9},{9,1},{2,10},{10,2},{3,11},{11,3},{4,12},{12,4},... | collective-permute-start | bytes 1572872 | tf_op jit(solution)/shard_map/ppermute | solution.py:229
  420.6 12.5 %collective-permute-start.45 = (bf16[256,1024]{1,0:T(8,128)(2,1)S(1)}, bf16[256,1024]{1,0:T(8,128)(2,1)S(1)}, u32[]{:S(2)}, u32[]{:S(2)}) collective-permute-start(bf16[256,1024]{1,0:T(8,128)(2,1)S(1)} %get-tuple-element.197), channel_id=1, source_target_pairs={{0,4},{4,0},{1,5},{5,1},{2,6},{6,2},{3,7},{7,3},{8,12},{12,8},{9,1... | collective-permute-start | bytes 1572872 | tf_op jit(solution)/shard_map/ppermute | solution.py:227
  450.3 218.7 %reduce-scatter.8.cloned.1.call-start = ((), (), s32[]{:S(2)}) async-start(), calls=%async_computation.19 | async-start | bytes 2621440 | tf_op jit(solution)/shard_map/reduce_scatter | solution.py:346
  454.9 14.0 %collective-permute-start.49 = (bf16[256,1024]{1,0:T(8,128)(2,1)S(1)}, bf16[256,1024]{1,0:T(8,128)(2,1)S(1)}, u32[]{:S(2)}, u32[]{:S(2)}) collective-permute-start(bf16[256,1024]{1,0:T(8,128)(2,1)S(1)} %fusion.39), channel_id=1, source_target_pairs={{0,8},{8,0},{1,9},{9,1},{2,10},{10,2},{3,11},{11,3},{4,12},{12,4},... | collective-permute-start | bytes 1572872 | tf_op jit(solution)/shard_map/ppermute | solution.py:229
  472.1 13.2 %collective-permute-start.51 = (bf16[256,1024]{1,0:T(8,128)(2,1)S(1)}, bf16[256,1024]{1,0:T(8,128)(2,1)S(1)}, u32[]{:S(2)}, u32[]{:S(2)}) collective-permute-start(bf16[256,1024]{1,0:T(8,128)(2,1)S(1)} %get-tuple-element.200), channel_id=1, source_target_pairs={{0,8},{8,0},{1,9},{9,1},{2,10},{10,2},{3,11},{11,3},{4,12},{12,4},... | collective-permute-start | bytes 1572872 | tf_op jit(solution)/shard_map/ppermute | solution.py:229
  473.3 17.2 %collective-permute-start.50 = (bf16[256,1024]{1,0:T(8,128)(2,1)S(1)}, bf16[256,1024]{1,0:T(8,128)(2,1)}, u32[]{:S(2)}, u32[]{:S(2)}) collective-permute-start(bf16[256,1024]{1,0:T(8,128)(2,1)S(1)} %get-tuple-element.200), channel_id=1, source_target_pairs={{0,4},{4,0},{1,5},{5,1},{2,6},{6,2},{3,7},{7,3},{8,12},{12,8},{9,1... | collective-permute-start | bytes 1572872 | tf_op jit(solution)/shard_map/ppermute | solution.py:227
  493.5 31.0 %all-to-all-start.4 = ((bf16[4,64,1024]{2,1,0:T(8,128)(2,1)}), bf16[4,64,1024]{2,1,0:T(8,128)(2,1)S(1)}, u32[]{:S(2)}, u32[]{:S(2)}) async-start(bf16[4,64,1024]{2,1,0:T(8,128)(2,1)} %bitcast.131), calls=%async_computation.4 | async-start | bytes 1048576 | tf_op jit(solution)/shard_map/all_to_all | solution.py:286
  497.0 174.3 %reduce-scatter.14.cloned.1.call-start = ((), (), s32[]{:S(2)}) async-start(), calls=%async_computation.22 | async-start | bytes 655360 | tf_op jit(solution)/shard_map/reduce_scatter | solution.py:346
  592.0 31.1 %collective-permute-start.53 = (bf16[2,256,1024]{2,1,0:T(8,128)(2,1)S(1)}, bf16[2,256,1024]{2,1,0:T(8,128)(2,1)}, u32[]{:S(2)}, u32[]{:S(2)}) collective-permute-start(bf16[2,256,1024]{2,1,0:T(8,128)(2,1)S(1)} %pad_maximum_fusion.10), channel_id=1, source_target_pairs={{0,4},{4,0},{1,5},{5,1},{2,6},{6,2},{3,7},{7,3},{8,12},{12,8},{9,1... | collective-permute-start | bytes 3145736 | tf_op jit(solution)/shard_map/ppermute | solution.py:227
  595.1 11.1 %collective-permute-start.58 = (bf16[128,1024]{1,0:T(8,128)(2,1)S(1)}, bf16[128,1024]{1,0:T(8,128)(2,1)S(1)}, u32[]{:S(2)}, u32[]{:S(2)}) collective-permute-start(bf16[128,1024]{1,0:T(8,128)(2,1)S(1)} %get-tuple-element.239), channel_id=1, source_target_pairs={{0,1},{1,2},{2,3},{3,0},{4,5},{5,6},{6,7},{7,4},{8,9},{9,10},{10,1... | collective-permute-start | bytes 786440 | tf_op jit(solution)/shard_map/ppermute | solution.py:296
  595.3 27.1 %collective-permute-start.59 = (bf16[128,1024]{1,0:T(8,128)(2,1)S(1)}, bf16[128,1024]{1,0:T(8,128)(2,1)S(1)}, u32[]{:S(2)}, u32[]{:S(2)}) collective-permute-start(bf16[128,1024]{1,0:T(8,128)(2,1)S(1)} %get-tuple-element.238), channel_id=1, source_target_pairs={{0,2},{1,3},{2,0},{3,1},{4,6},{5,7},{6,4},{7,5},{8,10},{9,11},{10,... | collective-permute-start | bytes 786440 | tf_op jit(solution)/shard_map/ppermute | solution.py:296
  597.1 31.0 %collective-permute-start.60 = (bf16[128,1024]{1,0:T(8,128)(2,1)}, bf16[128,1024]{1,0:T(8,128)(2,1)S(1)}, u32[]{:S(2)}, u32[]{:S(2)}) collective-permute-start(bf16[128,1024]{1,0:T(8,128)(2,1)} %get-tuple-element.237), channel_id=1, source_target_pairs={{0,3},{1,0},{2,1},{3,2},{4,7},{5,4},{6,5},{7,6},{8,11},{9,8},{10,9... | collective-permute-start | bytes 786440 | tf_op jit(solution)/shard_map/ppermute | solution.py:296
  598.9 73.4 %reduce-scatter.16.cloned.1.call-start = ((), (), s32[]{:S(2)}) async-start(), calls=%async_computation.23 | async-start | bytes 655360 | tf_op jit(solution)/shard_map/reduce_scatter | solution.py:346
  626.8 11.2 %collective-permute-start.54 = (bf16[256,1024]{1,0:T(8,128)(2,1)}, bf16[256,1024]{1,0:T(8,128)(2,1)}, u32[]{:S(2)}, u32[]{:S(2)}) collective-permute-start(bf16[256,1024]{1,0:T(8,128)(2,1)} %fusion.34), channel_id=1, source_target_pairs={{0,8},{8,0},{1,9},{9,1},{2,10},{10,2},{3,11},{11,3},{4,12},{12,4},... | collective-permute-start | bytes 1572872 | tf_op jit(solution)/shard_map/ppermute | solution.py:229
  631.7 62.7 %reduce-scatter.12.cloned.1.call-start = ((), (), s32[]{:S(2)}) async-start(), calls=%async_computation.21 | async-start | bytes 1310720 | tf_op jit(solution)/shard_map/reduce_scatter | solution.py:346
  642.7 10.4 %collective-permute-start.56 = (bf16[256,1024]{1,0:T(8,128)(2,1)}, bf16[256,1024]{1,0:T(8,128)(2,1)}, u32[]{:S(2)}, u32[]{:S(2)}) collective-permute-start(bf16[256,1024]{1,0:T(8,128)(2,1)} %get-tuple-element.203), channel_id=1, source_target_pairs={{0,8},{8,0},{1,9},{9,1},{2,10},{10,2},{3,11},{11,3},{4,12},{12,4},... | collective-permute-start | bytes 1572872 | tf_op jit(solution)/shard_map/ppermute | solution.py:229
  657.2 40.9 %all-to-all-start.6 = ((bf16[4,64,1024]{2,1,0:T(8,128)(2,1)}), bf16[4,64,1024]{2,1,0:T(8,128)(2,1)}, u32[]{:S(2)}, u32[]{:S(2)}) async-start(bf16[4,64,1024]{2,1,0:T(8,128)(2,1)} %bitcast.630), calls=%async_computation.6 | async-start | bytes 1048576 | tf_op jit(solution)/shard_map/all_to_all | solution.py:286
  666.6 90.4 %reduce-scatter.18.cloned.1.call-start = ((), (), s32[]{:S(2)}) async-start(), calls=%async_computation.24 | async-start | bytes 655360 | tf_op jit(solution)/shard_map/reduce_scatter | solution.py:346
  701.5 12.1 %collective-permute-start.62 = (bf16[768,256]{1,0:T(8,128)(2,1)S(1)}, bf16[768,256]{1,0:T(8,128)(2,1)S(1)}, u32[]{:S(2)}, u32[]{:S(2)}) collective-permute-start(bf16[768,256]{1,0:T(8,128)(2,1)S(1)} %get-tuple-element.251), channel_id=1, source_target_pairs={{0,8},{8,0},{1,9},{9,1},{2,10},{10,2},{3,11},{11,3},{4,12},{12,4},... | collective-permute-start | bytes 1179656 | tf_op jit(solution)/shard_map/ppermute | solution.py:229
  703.1 17.8 %collective-permute-start.63 = (bf16[768,256]{1,0:T(8,128)(2,1)S(1)}, bf16[768,256]{1,0:T(8,128)(2,1)S(1)}, u32[]{:S(2)}, u32[]{:S(2)}) collective-permute-start(bf16[768,256]{1,0:T(8,128)(2,1)S(1)} %get-tuple-element.250), channel_id=1, source_target_pairs={{0,12},{4,8},{8,4},{12,0},{1,13},{5,9},{9,5},{13,1},{2,14},{6,10},... | collective-permute-start | bytes 1179656 | tf_op jit(solution)/shard_map/ppermute | solution.py:230
  722.3 37.0 %collective-permute-start.64 = (bf16[4,768,256]{2,1,0:T(8,128)(2,1)}, bf16[4,768,256]{2,1,0:T(8,128)(2,1)}, u32[]{:S(2)}, u32[]{:S(2)}) collective-permute-start(bf16[4,768,256]{2,1,0:T(8,128)(2,1)} %pad_maximum_fusion.4), channel_id=1, source_target_pairs={{0,16},{16,0},{1,17},{17,1},{2,18},{18,2},{3,19},{19,3},{4,20},{20... | collective-permute-start | bytes 4718600 | tf_op jit(solution)/shard_map/ppermute | solution.py:359
  766.1 41.5 %all-to-all-start.7 = ((bf16[4,192,1024]{2,1,0:T(8,128)(2,1)}), bf16[4,192,1024]{2,1,0:T(8,128)(2,1)}, u32[]{:S(2)}, u32[]{:S(2)}) async-start(bf16[4,192,1024]{2,1,0:T(8,128)(2,1)} %pad_maximum_fusion.5), calls=%async_computation.13 | async-start | bytes 3145728 | tf_op jit(solution)/shard_map/all_to_all | solution.py:286
  770.5 78.4 %reduce-scatter.20.cloned.1.call-start = ((), (), s32[]{:S(2)}) async-start(), calls=%async_computation.25 | async-start | bytes 1966080 | tf_op jit(solution)/shard_map/reduce_scatter | solution.py:346
  777.7 10.8 %collective-permute-start.67 = (bf16[2,1024,256]{2,1,0:T(8,128)(2,1)}, bf16[2,1024,256]{2,1,0:T(8,128)(2,1)}, u32[]{:S(2)}, u32[]{:S(2)}) collective-permute-start(bf16[2,1024,256]{2,1,0:T(8,128)(2,1)} %pad_maximum_fusion.12), channel_id=1, source_target_pairs={{0,4},{4,0},{1,5},{5,1},{2,6},{6,2},{3,7},{7,3},{8,12},{12,8},{9,1... | collective-permute-start | bytes 3145736 | tf_op jit(solution)/shard_map/ppermute | solution.py:227
  781.7 30.9 %collective-permute-start.41 = (bf16[256,256]{1,0:T(8,128)(2,1)S(1)}, bf16[256,256]{1,0:T(8,128)(2,1)}, u32[]{:S(2)}, u32[]{:S(2)}) collective-permute-start(bf16[256,256]{1,0:T(8,128)(2,1)S(1)} %bitcast.648), channel_id=1, source_target_pairs={{0,12},{4,8},{8,4},{12,0},{1,13},{5,9},{9,5},{13,1},{2,14},{6,10},... | collective-permute-start | bytes 393224 | tf_op jit(solution)/shard_map/ppermute | solution.py:230
  793.7 20.6 %collective-permute-start.68 = (bf16[1024,256]{1,0:T(8,128)(2,1)}, bf16[1024,256]{1,0:T(8,128)(2,1)}, u32[]{:S(2)}, u32[]{:S(2)}) collective-permute-start(bf16[1024,256]{1,0:T(8,128)(2,1)} %fusion.26), channel_id=1, source_target_pairs={{0,8},{8,0},{1,9},{9,1},{2,10},{10,2},{3,11},{11,3},{4,12},{12,4},... | collective-permute-start | bytes 1572872 | tf_op jit(solution)/shard_map/ppermute | solution.py:229
  794.3 19.9 %collective-permute-start.80 = (f32[15,1024]{1,0:T(8,128)S(1)}, f32[15,1024]{1,0:T(8,128)S(1)}, u32[]{:S(2)}, u32[]{:S(2)}) collective-permute-start(f32[15,1024]{1,0:T(8,128)S(1)} %add.598), channel_id=1, source_target_pairs={{0,4},{4,0},{1,5},{5,1},{2,6},{6,2},{3,7},{7,3},{8,12},{12,8},{9,1... | collective-permute-start | bytes 184328 | tf_op jit(solution)/shard_map/ppermute | solution.py:262
  834.1 10.3 %collective-permute-start.65 = (bf16[2,1024,256]{2,1,0:T(8,128)(2,1)S(1)}, bf16[2,1024,256]{2,1,0:T(8,128)(2,1)S(1)}, u32[]{:S(2)}, u32[]{:S(2)}) collective-permute-start(bf16[2,1024,256]{2,1,0:T(8,128)(2,1)S(1)} %pad_maximum_fusion.11), channel_id=1, source_target_pairs={{0,4},{4,0},{1,5},{5,1},{2,6},{6,2},{3,7},{7,3},{8,12},{12,8},{9,1... | collective-permute-start | bytes 3145736 | tf_op jit(solution)/shard_map/ppermute | solution.py:227
  844.4 13.0 %collective-permute-start.76 = (f32[2,1024]{1,0:T(2,128)S(1)}, f32[2,1024]{1,0:T(2,128)}, u32[]{:S(2)}, u32[]{:S(2)}) collective-permute-start(f32[2,1024]{1,0:T(2,128)S(1)} %add.593), channel_id=1, source_target_pairs={{0,1},{1,0},{2,3},{3,2},{4,5},{5,4},{6,7},{7,6},{8,9},{9,8},{10,11... | collective-permute-start | bytes 24584 | tf_op jit(solution)/shard_map/ppermute | solution.py:262
  846.7 29.9 %collective-permute-start.66 = (bf16[1024,256]{1,0:T(8,128)(2,1)}, bf16[1024,256]{1,0:T(8,128)(2,1)}, u32[]{:S(2)}, u32[]{:S(2)}) collective-permute-start(bf16[1024,256]{1,0:T(8,128)(2,1)} %fusion.30), channel_id=1, source_target_pairs={{0,8},{8,0},{1,9},{9,1},{2,10},{10,2},{3,11},{11,3},{4,12},{12,4},... | collective-permute-start | bytes 1572872 | tf_op jit(solution)/shard_map/ppermute | solution.py:229
  852.4 12.1 %collective-permute-start.70 = (bf16[256,256]{1,0:T(8,128)(2,1)S(1)}, bf16[256,256]{1,0:T(8,128)(2,1)S(1)}, u32[]{:S(2)}, u32[]{:S(2)}) collective-permute-start(bf16[256,256]{1,0:T(8,128)(2,1)S(1)} %pad_maximum_fusion.27), channel_id=1, source_target_pairs={{0,8},{8,0},{1,9},{9,1},{2,10},{10,2},{3,11},{11,3},{4,12},{12,4},... | collective-permute-start | bytes 393224 | tf_op jit(solution)/shard_map/ppermute | solution.py:229
  854.8 10.9 %collective-permute-start.71 = (bf16[256,256]{1,0:T(8,128)(2,1)S(1)}, bf16[256,256]{1,0:T(8,128)(2,1)S(1)}, u32[]{:S(2)}, u32[]{:S(2)}) collective-permute-start(bf16[256,256]{1,0:T(8,128)(2,1)S(1)} %pad_maximum_fusion.28), channel_id=1, source_target_pairs={{0,12},{4,8},{8,4},{12,0},{1,13},{5,9},{9,5},{13,1},{2,14},{6,10},... | collective-permute-start | bytes 393224 | tf_op jit(solution)/shard_map/ppermute | solution.py:230
  858.7 16.6 %collective-permute-start.77 = (f32[2,1024]{1,0:T(2,128)}, f32[2,1024]{1,0:T(2,128)S(1)}, u32[]{:S(2)}, u32[]{:S(2)}) collective-permute-start(f32[2,1024]{1,0:T(2,128)} %add.594), channel_id=1, source_target_pairs={{0,2},{1,3},{2,0},{3,1},{4,6},{5,7},{6,4},{7,5},{8,10},{9,11},{10,... | collective-permute-start | bytes 24584 | tf_op jit(solution)/shard_map/ppermute | solution.py:262
  866.6 14.8 %collective-permute-start.72 = (bf16[4,256,256]{2,1,0:T(8,128)(2,1)}, bf16[4,256,256]{2,1,0:T(8,128)(2,1)}, u32[]{:S(2)}, u32[]{:S(2)}) collective-permute-start(bf16[4,256,256]{2,1,0:T(8,128)(2,1)} %pad_maximum_fusion.13), channel_id=1, source_target_pairs={{0,16},{16,0},{1,17},{17,1},{2,18},{18,2},{3,19},{19,3},{4,20},{20... | collective-permute-start | bytes 1572872 | tf_op jit(solution)/shard_map/ppermute | solution.py:359
  (108 other events, 855.5 us)
Sparse Core Ops, SparseCore 0:
  28.4 35.8 all-gather.4
  66.4 64.6 all-gather.6
  210.4 27.1 all-gather.8
  246.5 100.3 all-gather.10
  450.5 41.4 reduce-scatter.9
  494.1 50.0 reduce-scatter.7
  599.0 27.9 reduce-scatter.13
  631.8 25.6 reduce-scatter.15
  660.4 33.9 reduce-scatter.11
  723.9 21.3 reduce-scatter.17
  812.7 36.1 reduce-scatter.19

commit v4 on v3

--- a/solution.py
+++ b/solution.py
@@ -465,7 +465,10 @@
     if layout.sizes["sq"] > 1:
         sequence_prefix = lax.dynamic_slice_in_dim(prefixes, lax.axis_index("sq"), 1, 0)
 
-    kv_w, self_w = gather_weights([column_rows(crosskv)], [split_rows(selfproj)])
+    kv_w, self_w, query_w, cross_w = gather_weights(
+        [column_rows(crosskv)],
+        [split_rows(selfproj), column_rows(crossquery[:, None]), split_rows(crossproj)],
+    )
     encoder_all = jnp.concatenate(layout.team_parts(by_token(encoder)), axis=1)
     pair = contract(kv_w, encoder_all, 1, 1).reshape(heads, 2, HD, group)
     pair_bias = jnp.stack([jnp.zeros_like(head_biases[:, 3]), head_biases[:, 3]], axis=1)
@@ -482,10 +485,7 @@
     self_low, cross_set = lax.optimization_barrier((self_low, cross_set))
     attended = layout.ring_exchange(self_low).reshape(heads * HD, group)
     spots = layout.spots()
-    query_w, cross_w = gather_weights(
-        [], [column_rows(crossquery[:, None]), split_rows(crossproj)], attended
-    )
-    up_w, down_w = gather_weights([], [column_rows(upweight[:, None]), split_rows(downweight)], query_w)
+    up_w, down_w = gather_weights([], [column_rows(upweight[:, None]), split_rows(downweight)], self_low)
 
     upstream = layout.team_send(layout.pick(by_token(cotangent).reshape(4, own_rows, -1)))
     upstream = layout.team_features(layout.place(upstream, spots)).astype(F32)
@@ -548,20 +548,22 @@
     attended_grad = contract(self_w, self_all, 1, 1).astype(BF16).reshape(heads, HD, group)
     attended_grad = layout.ring_exchange(attended_grad)
     selfproj_part = contract(attended, self_all, 1, 0).astype(BF16)
-    sums = (up_sum, down_sum, crosskv_sum, crossproj_sum, crossquery_sum)
+    sums = (up_sum, down_sum, crossproj_sum)
     attended_grad, selfproj_part, sums = lax.optimization_barrier((attended_grad, selfproj_part, sums))
-    up_sum, down_sum, crosskv_sum, crossproj_sum, crossquery_sum = sums
-    early_grads = layout.weight_grads([crosskv_sum], [crossproj_sum, crossquery_sum, up_sum, down_sum])
+    early_grads = layout.weight_grads([], list(sums))
     selfproj_sum = layout.over_columns(layout.out_of_order(selfproj_part))
     dq, dk, dv = flash_backward(
         sequence_prefix, self_set, 0, self_set, 1, 2, attended_grad, self_out, self_lse, True
     )
     dq, dk, dv, early_grads, selfproj_sum = lax.optimization_barrier((dq, dk, dv, early_grads, selfproj_sum))
-    crosskv_grad, crossproj_grad, crossquery_grad, upweight_grad, downweight_grad = early_grads
+    upweight_grad, downweight_grad, crossproj_grad = early_grads
+    crosskv_grad, selfproj_grad, crossquery_grad = layout.weight_grads(
+        [crosskv_sum], [selfproj_sum, crossquery_sum]
+    )
     self_bias_sums = (jnp.sum(dq.astype(F32), axis=(0, 2)), jnp.sum(dv.astype(F32), axis=(0, 2)))
     dqkv = layout.ring_exchange(jnp.concatenate([dq, dk, dv], axis=1)).reshape(heads * 3 * HD, group)
     selfqkv_sum = layout.over_columns(contract(dqkv, tokens_all, 1, 0))
-    selfqkv_grad, selfproj_grad = layout.weight_grads([selfqkv_sum], [selfproj_sum])
+    (selfqkv_grad,) = layout.weight_grads([selfqkv_sum], [])
     tokens_part = contract(dqkv, qkv_w, 0, 0)
     low_parts = jnp.concatenate(layout.pick(layout.member_blocks(low_grad)), axis=1)
     mine = lax.dynamic_slice_in_dim(tokens_part, me * own_rows, own_rows, 0) + low_parts

time: 905 us -> 875 us (0.967)
  blocking collectives: 78 us -> 63.2 us
  local copies, waits for them, and re-layouts: 108 us -> 93.9 us
    all_to_all x3 -> x2, blocking collectives: 78 us -> 63.2 us  [ring_exchange(): lax.all_to_all(self.flip(blocks, 'cs', 'rb'), self.ring, 0, 0, tiled=True)]
    ppermute x6, waiting for transfers between devices: 22.7 us -> 8.73 us  [ring_trickle(): lax.ppermute(pick(step), self.ring, [(i, (i + step) % size) for i in rang...]
    all_gather x4 -> x3, waiting for transfers between devices: 55.4 us -> 68.6 us  [widen(): return lax.all_gather(piece[None], self.cols, axis=0, tiled=True)]
    ppermute x10, waiting for transfers between devices: 12.5 us -> 25.6 us  [total(): value = value + lax.ppermute(value, name, pairs)]
    unnamed x193 -> x175, local copies, waits for them, and re-layouts: 30.5 us -> 23.2 us
    all_to_all x5 -> x6, waiting for transfers between devices: 50.8 us -> 44.4 us  [ring_exchange(): lax.all_to_all(self.flip(blocks, 'cs', 'rb'), self.ring, 0, 0, tiled=True)]
    all_to_all x5 -> x6, starting transfers between devices: 24.5 us -> 23.3 us  [ring_exchange(): lax.all_to_all(self.flip(blocks, 'cs', 'rb'), self.ring, 0, 0, tiled=True)]
  transfers between devices with their start and end apart: 99 -> 100, of which waited for: 45 -> 51; matrix products, arithmetic and copies ran while one was open for 19% -> 19% of each run, Pallas kernels for 15% -> 16%
where the time goes in v4:
time: 875 us; the launch traced here: 864 us
  waiting for transfers between devices  337 us (39%)
  Pallas kernels  137 us (16%)
  local copies, waits for them, and re-layouts  93.9 us (11%)
  starting transfers between devices  92.1 us (11%)
  matrix products  79.7 us (9%)
  blocking collectives  63.2 us (7%)
  other arithmetic  43.1 us (5%)
  between operations  17.8 us (2%)
    ppermute x23, waiting for transfers between devices, swap(): return lax.ppermute(value, 'rx', [(0, 1), (1, 0)])  140 us
    pallas_call x2, Pallas kernels, flash_backward(): pl.pallas_call(functools.partial(backward_kernel, masked, bq, bk), out_sh...  84.2 us
    dot_general x21, matrix products, contract(): lax.dot_general(left, right, (((left_dim,), (right_dim,)), ((), ())), pre...  79.7 us
    all_gather x3, waiting for transfers between devices, widen(): return lax.all_gather(piece[None], self.cols, axis=0, tiled=True)  68.6 us
    all_to_all x2, blocking collectives, ring_exchange(): lax.all_to_all(self.flip(blocks, 'cs', 'rb'), self.ring, 0, 0, tiled=True)  63.2 us
    pallas_call x2, Pallas kernels, flash_forward(): pl.pallas_call(functools.partial(forward_kernel, masked, bq, bk), out_sha...  52.7 us
    all_to_all x6, waiting for transfers between devices, ring_exchange(): lax.all_to_all(self.flip(blocks, 'cs', 'rb'), self.ring, 0, 0, tiled=True)  44.4 us
    ppermute x23, starting transfers between devices, swap(): return lax.ppermute(value, 'rx', [(0, 1), (1, 0)])  28.4 us
  transfers between devices with their start and end apart: 100, of which 51 were waited for; matrix products, arithmetic and copies ran while one was open for 19% of the time, Pallas kernels for 16%

profile of v4, /device:TPU:0, one launch (start us, length us, event | category | flops | bytes accessed | tf_op | source)
XLA Modules:
  0.0 864.0 jit_solution(16875260848539043793)
XLA Ops:
  9.1 2.6 collective-permute-start.4
  11.7 3.6 collective-permute-done.4
  22.6 2.5 dynamic_update_slice.197
  26.3 2.6 collective-permute-done.11
  29.0 2.5 dynamic_update_slice.198
  31.6 2.5 dynamic_update_slice.199
  34.1 2.5 dynamic_update_slice.200
  40.4 2.6 collective-permute-start.7
  49.7 7.8 all-gather.4.cloned.1.call-done
  57.5 4.5 multiply_convert_fusion.1
  62.0 3.7 all-to-all-start
  67.2 11.9 %collective-permute-done.13 = bf16[1024,256]{1,0:T(8,128)(2,1)S(1)} collective-permute-done((bf16[1024,256]{1,0:T(8,128)(2,1)S(1)}, bf16[1024,256]{1,0:T(8,128)(2,1)S(1)}, u32[]{:S(2)}, u32[]{:S(2)}) %collective-permute-start.13) | collective-permute-done | bytes 524320 | tf_op jit(solution)/shard_map/ppermute | solution.py:229
  84.2 60.8 %all-gather.6.cloned.1.call-done = bf16[4,320,1024]{2,1,0:T(8,128)(2,1)} async-done(((bf16[1,320,1024]{2,1,0:T(8,128)(2,1)}), bf16[4,320,1024]{2,1,0:T(8,128)(2,1)}) %all-gather.6.cloned.1.call-update) | async-done | bytes 2621456 | tf_op jit(solution)/shard_map/all_gather | solution.py:329
  146.3 2.9 add_convert_fusion.1
  155.7 22.4 %attend_self.1 = (f32[4,64,1024]{2,1,0:T(8,128)}, bf16[4,64,1024]{2,1,0:T(8,128)(2,1)}, f32[4,1,1024]{2,1,0:T(1,128)}) custom-call(s32[1]{0:T(128)S(6)} %copy.597.prefix_ref, bf16[4,192,1024]{2,1,0:T(8,128)(2,1)} %copy-done.21, bf16[4,192,1024]{2,1,0:T(8,128)(2,1)} %copy-done.21, bf16[4,192,1024]{2,1,0:T(8,128)(2,1)} %copy-done.21), custom_call_target="tpu_custom_call" | custom-call | flops 4294967296 | bytes 3670016 | tf_op jit(solution)/shard_map/attend_self/pallas_call | solution.py:78
  178.2 3.5 all-to-all-start.1
  183.9 12.2 %all-to-all-done.1 = bf16[4,64,1024]{2,1,0:T(8,128)(2,1)S(1)} async-done(((bf16[4,64,1024]{2,1,0:T(8,128)(2,1)}), bf16[4,64,1024]{2,1,0:T(8,128)(2,1)S(1)}, u32[]{:S(2)}, u32[]{:S(2)}) %all-to-all-start.1) | async-done | bytes 524320 | tf_op jit(solution)/shard_map/all_to_all | solution.py:286
  212.9 8.8 %collective-permute-done.19 = bf16[256,1024]{1,0:T(8,128)(2,1)S(1)} collective-permute-done((bf16[256,1024]{1,0:T(8,128)(2,1)S(1)}, bf16[256,1024]{1,0:T(8,128)(2,1)S(1)}, u32[]{:S(2)}, u32[]{:S(2)}) %collective-permute-start.19) | collective-permute-done | bytes 524320 | tf_op jit(solution)/shard_map/ppermute | solution.py:229
  228.3 10.3 %collective-permute-done.24 = bf16[256,1024]{1,0:T(8,128)(2,1)} collective-permute-done((bf16[256,1024]{1,0:T(8,128)(2,1)S(1)}, bf16[256,1024]{1,0:T(8,128)(2,1)}, u32[]{:S(2)}, u32[]{:S(2)}) %collective-permute-start.24) | collective-permute-done | bytes 524320 | tf_op jit(solution)/shard_map/ppermute | solution.py:229
  240.0 4.2 collective-permute-done.32
  252.0 32.0 %all_to_all.40.q_ref = bf16[4,64,1024]{2,1,0:T(8,128)(2,1)} all-to-all(bf16[4,64,1024]{2,1,0:T(8,128)(2,1)S(1)} %fusion.22), channel_id=1, replica_groups=mesh['dp'=2,'rb'=1,'rx'=2,'rc'=2,'sq'=1,'cs'=4] {'cs'}, dimensions={0} | all-to-all | bytes 1048576 | tf_op jit(solution)/shard_map/all_to_all | solution.py:286
  283.9 30.3 %attend_cross.1 = (f32[4,64,1024]{2,1,0:T(8,128)}, bf16[4,64,1024]{2,1,0:T(8,128)(2,1)}, f32[4,1,1024]{2,1,0:T(1,128)}) custom-call(s32[1]{0:T(128)S(6)} %copy.597.prefix_ref, bf16[4,64,1024]{2,1,0:T(8,128)(2,1)} %all_to_all.40.q_ref, bf16[4,128,1024]{2,1,0:T(8,128)(2,1)} %copy-done.24, bf16[4,128,1024]{2,1,0:T(8,128)(2,1)} %copy-done.24), custom_call_target="tpu_custom_call" | custom-call | flops 4294967296 | bytes 3670016 | tf_op jit(solution)/shard_map/attend_cross/pallas_call | solution.py:78
  314.2 31.2 %all_to_all.41 = bf16[4,64,1024]{2,1,0:T(8,128)(2,1)S(1)} all-to-all(bf16[4,64,1024]{2,1,0:T(8,128)(2,1)} %get-tuple-element.54), channel_id=1, replica_groups=mesh['dp'=2,'rb'=1,'rx'=2,'rc'=2,'sq'=1,'cs'=4] {'cs'}, dimensions={0} | all-to-all | bytes 1048576 | tf_op jit(solution)/shard_map/all_to_all | solution.py:286
  351.8 13.1 %collective-permute-done.27 = bf16[256,1024]{1,0:T(8,128)(2,1)S(1)} collective-permute-done((bf16[256,1024]{1,0:T(8,128)(2,1)S(1)}, bf16[256,1024]{1,0:T(8,128)(2,1)S(1)}, u32[]{:S(2)}, u32[]{:S(2)}) %collective-permute-start.27) | collective-permute-done | bytes 524320 | tf_op jit(solution)/shard_map/ppermute | solution.py:229
  366.8 12.3 %collective-permute-done.29 = bf16[256,1024]{1,0:T(8,128)(2,1)S(1)} collective-permute-done((bf16[256,1024]{1,0:T(8,128)(2,1)S(1)}, bf16[256,1024]{1,0:T(8,128)(2,1)S(1)}, u32[]{:S(2)}, u32[]{:S(2)}) %collective-permute-start.29) | collective-permute-done | bytes 524320 | tf_op jit(solution)/shard_map/ppermute | solution.py:229
  379.1 2.9 fusion.103
  382.0 13.3 %multiply_convert_fusion = (bf16[1024,1024]{1,0:T(8,128)(2,1)S(1)}, f32[1024,1024]{1,0:T(8,128)S(1)}, f32[1024,1024]{1,0:T(8,128)S(1)}) fusion(f32[1024]{0:T(1024)S(1)} %bitcast.686, bf16[1024,1024]{1,0:T(8,128)(2,1)S(1)} %bitcast.586, bf16[256,1024]{1,0:T(8,128)(2,1)} %collective-permute-done.30, bf16[256,1024]{1,0:T(8,128)(2,1)S(1)} %collective-permute-done.29, ...), kind=kOutput, calls=%fused_computation.4 | convolution fusion | flops 2225078272 | bytes 14684160 | tf_op jit(solution)/shard_map/dot_general | solution.py:202
  400.8 4.8 collective-permute-done.40
  409.4 12.3 %collective-permute-done.35 = bf16[256,1024]{1,0:T(8,128)(2,1)S(1)} collective-permute-done((bf16[256,1024]{1,0:T(8,128)(2,1)S(1)}, bf16[256,1024]{1,0:T(8,128)(2,1)S(1)}, u32[]{:S(2)}, u32[]{:S(2)}) %collective-permute-start.35) | collective-permute-done | bytes 524320 | tf_op jit(solution)/shard_map/ppermute | solution.py:229
  425.0 12.7 %collective-permute-done.43 = bf16[256,1024]{1,0:T(8,128)(2,1)S(1)} collective-permute-done((bf16[256,1024]{1,0:T(8,128)(2,1)S(1)}, bf16[256,1024]{1,0:T(8,128)(2,1)S(1)}, u32[]{:S(2)}, u32[]{:S(2)}) %collective-permute-start.43) | collective-permute-done | bytes 524320 | tf_op jit(solution)/shard_map/ppermute | solution.py:229
  439.6 6.4 convert_reduce_fusion
  454.8 3.8 convolution_convert_fusion
  458.6 9.6 %collective-permute-done.46 = bf16[256,1024]{1,0:T(8,128)(2,1)} collective-permute-done((bf16[256,1024]{1,0:T(8,128)(2,1)}, bf16[256,1024]{1,0:T(8,128)(2,1)}, u32[]{:S(2)}, u32[]{:S(2)}) %collective-permute-start.46) | collective-permute-done | bytes 524320 | tf_op jit(solution)/shard_map/ppermute | solution.py:229
  471.9 12.2 %collective-permute-done.48 = bf16[256,1024]{1,0:T(8,128)(2,1)S(1)} collective-permute-done((bf16[256,1024]{1,0:T(8,128)(2,1)S(1)}, bf16[256,1024]{1,0:T(8,128)(2,1)S(1)}, u32[]{:S(2)}, u32[]{:S(2)}) %collective-permute-start.48) | collective-permute-done | bytes 524320 | tf_op jit(solution)/shard_map/ppermute | solution.py:229
  487.6 3.5 all-to-all-start.4
  491.1 3.1 convolution_convert_fusion.7
  494.1 16.1 %all-to-all-done.4.g_ref = bf16[4,64,1024]{2,1,0:T(8,128)(2,1)S(1)} async-done(((bf16[4,64,1024]{2,1,0:T(8,128)(2,1)}), bf16[4,64,1024]{2,1,0:T(8,128)(2,1)S(1)}, u32[]{:S(2)}, u32[]{:S(2)}) %all-to-all-start.4) | async-done | bytes 524320 | tf_op jit(solution)/shard_map/all_to_all | solution.py:286
  511.1 48.3 %attend_cross_back.1 = (bf16[4,64,1024]{2,1,0:T(8,128)(2,1)}, bf16[4,64,1024]{2,1,0:T(8,128)(2,1)}, bf16[4,64,1024]{2,1,0:T(8,128)(2,1)}) custom-call(s32[1]{0:T(128)S(6)} %copy.597.prefix_ref, bf16[4,64,1024]{2,1,0:T(8,128)(2,1)} %all_to_all.40.q_ref, bf16[4,64,1024]{2,1,0:T(8,128)(2,1)} %copy-done.37, f32[4,64,1024]{2,1,0:T(8,128)} %get-tuple-element.57.o_ref, ...), custom_call_target="tpu_custom_call" | custom-call | flops 10737418240 | bytes 5242880 | tf_op jit(solution)/shard_map/attend_cross_back/pallas_call | solution.py:173
  559.3 3.5 all-to-all-start.5
  563.0 5.7 convolution_convert_fusion.1
  568.9 9.0 %all-to-all-done.5 = bf16[4,64,1024]{2,1,0:T(8,128)(2,1)S(1)} async-done(((bf16[4,64,1024]{2,1,0:T(8,128)(2,1)}), bf16[4,64,1024]{2,1,0:T(8,128)(2,1)S(1)}, u32[]{:S(2)}, u32[]{:S(2)}) %all-to-all-start.5) | async-done | bytes 524320 | tf_op jit(solution)/shard_map/all_to_all | solution.py:286
  577.8 4.0 fusion.116
  593.7 12.0 %collective-permute-done.51 = bf16[256,1024]{1,0:T(8,128)(2,1)S(1)} collective-permute-done((bf16[256,1024]{1,0:T(8,128)(2,1)S(1)}, bf16[256,1024]{1,0:T(8,128)(2,1)S(1)}, u32[]{:S(2)}, u32[]{:S(2)}) %collective-permute-start.51) | collective-permute-done | bytes 524320 | tf_op jit(solution)/shard_map/ppermute | solution.py:229
  616.8 4.2 collective-permute-done.53
  627.6 3.6 all-to-all-start.6
  632.3 8.7 %collective-permute-done.62 = bf16[128,1024]{1,0:T(8,128)(2,1)} collective-permute-done((bf16[128,1024]{1,0:T(8,128)(2,1)}, bf16[128,1024]{1,0:T(8,128)(2,1)}, u32[]{:S(2)}, u32[]{:S(2)}) %collective-permute-start.62) | collective-permute-done | bytes 262176 | tf_op jit(solution)/shard_map/ppermute | solution.py:296
  649.1 3.1 convolution_convert_fusion.5
  652.3 7.1 all-to-all-done.6.g_ref
  659.4 4.6 fusion.117
  665.6 3.0 convolution_convert_fusion.4
  677.7 3.8 convolution_convert_fusion.3
  685.6 4.7 collective-permute-done.57
  696.8 36.0 %attend_self_back.1 = (bf16[4,64,1024]{2,1,0:T(8,128)(2,1)}, bf16[4,64,1024]{2,1,0:T(8,128)(2,1)}, bf16[4,64,1024]{2,1,0:T(8,128)(2,1)}) custom-call(s32[1]{0:T(128)S(6)} %copy.597.prefix_ref, bf16[4,192,1024]{2,1,0:T(8,128)(2,1)} %copy-done.21, bf16[4,64,1024]{2,1,0:T(8,128)(2,1)} %copy-done.36, f32[4,64,1024]{2,1,0:T(8,128)} %get-tuple-element.62.o_ref, ...), custom_call_target="tpu_custom_call" | custom-call | flops 10737418240 | bytes 5242880 | tf_op jit(solution)/shard_map/attend_self_back/pallas_call | solution.py:173
  740.2 5.5 all-to-all-start.7
  759.6 3.1 collective-permute-start.82
  762.8 10.3 %collective-permute-done.82 = f32[15,1024]{1,0:T(8,128)S(1)} collective-permute-done((f32[15,1024]{1,0:T(8,128)S(1)}, f32[15,1024]{1,0:T(8,128)S(1)}, u32[]{:S(2)}, u32[]{:S(2)}) %collective-permute-start.82) | collective-permute-done | bytes 61472 | tf_op jit(solution)/shard_map/ppermute | solution.py:262
  773.1 4.7 collective-permute-start.83
  777.8 8.2 collective-permute-done.83
  793.4 5.0 convolution_convert_fusion.2
  806.5 3.7 convolution_bitcast_fusion
  812.1 6.9 collective-permute-done.78
  822.5 10.5 %reduce-scatter.16.cloned.1.call-done = bf16[192,1024]{1,0:T(8,128)(2,1)} async-done(((bf16[768,1024]{1,0:T(8,128)(2,1)}), bf16[192,1024]{1,0:T(8,128)(2,1)}) %reduce-scatter.16.cloned.1.call-update) | async-done | bytes 393232 | tf_op jit(solution)/shard_map/reduce_scatter | solution.py:346
  837.0 3.7 collective-permute-done.67
  849.3 5.0 collective-permute-done.69
  (597 shorter events, 224.4 us)
Async XLA Ops:
  7.2 50.3 %all-gather.4.cloned.1.call-start = ((), (), s32[]{:S(2)}) async-start(), calls=%async_computation.15 | async-start | bytes 1966080 | tf_op jit(solution)/shard_map/all_gather | solution.py:329
  18.4 126.6 %all-gather.6.cloned.1.call-start = ((), (), s32[]{:S(2)}) async-start(), calls=%async_computation.16 | async-start | bytes 3276800 | tf_op jit(solution)/shard_map/all_gather | solution.py:329
  19.0 7.1 collective-permute-start.10
  20.8 8.1 collective-permute-start.11
  20.8 26.8 %collective-permute-start.1 = (bf16[1024,256]{1,0:T(8,128)(2,1)S(1)}, bf16[1024,256]{1,0:T(8,128)(2,1)S(1)}, u32[]{:S(2)}, u32[]{:S(2)}) collective-permute-start(bf16[1024,256]{1,0:T(8,128)(2,1)S(1)} %copy-done.28), channel_id=1, source_target_pairs={{0,8},{8,0},{1,9},{9,1},{2,10},{10,2},{3,11},{11,3},{4,12},{12,4},... | collective-permute-start | bytes 1572872 | tf_op jit(solution)/shard_map/ppermute | solution.py:229
  62.0 87.2 %all-to-all-start = ((bf16[4,192,1024]{2,1,0:T(8,128)(2,1)}), bf16[4,192,1024]{2,1,0:T(8,128)(2,1)S(1)}, u32[]{:S(2)}, u32[]{:S(2)}) async-start(bf16[4,192,1024]{2,1,0:T(8,128)(2,1)} %bitcast.24), calls=%async_computation | async-start | bytes 3145728 | tf_op jit(solution)/shard_map/all_to_all | solution.py:286
  65.7 13.4 %collective-permute-start.13 = (bf16[1024,256]{1,0:T(8,128)(2,1)S(1)}, bf16[1024,256]{1,0:T(8,128)(2,1)S(1)}, u32[]{:S(2)}, u32[]{:S(2)}) collective-permute-start(bf16[1024,256]{1,0:T(8,128)(2,1)S(1)} %copy-done.29), channel_id=1, source_target_pairs={{0,8},{8,0},{1,9},{9,1},{2,10},{10,2},{3,11},{11,3},{4,12},{12,4},... | collective-permute-start | bytes 1572872 | tf_op jit(solution)/shard_map/ppermute | solution.py:229
  67.2 13.4 %collective-permute-start.12 = (bf16[1024,256]{1,0:T(8,128)(2,1)S(1)}, bf16[1024,256]{1,0:T(8,128)(2,1)}, u32[]{:S(2)}, u32[]{:S(2)}) collective-permute-start(bf16[1024,256]{1,0:T(8,128)(2,1)S(1)} %copy-done.29), channel_id=1, source_target_pairs={{0,4},{4,0},{1,5},{5,1},{2,6},{6,2},{3,7},{7,3},{8,12},{12,8},{9,1... | collective-permute-start | bytes 1572872 | tf_op jit(solution)/shard_map/ppermute | solution.py:227
  151.4 26.7 %collective-permute-start.15 = (bf16[128,1024]{1,0:T(8,128)(2,1)}, bf16[128,1024]{1,0:T(8,128)(2,1)S(1)}, u32[]{:S(2)}, u32[]{:S(2)}) collective-permute-start(bf16[128,1024]{1,0:T(8,128)(2,1)} %get-tuple-element.237), channel_id=1, source_target_pairs={{0,1},{1,2},{2,3},{3,0},{4,5},{5,6},{6,7},{7,4},{8,9},{9,10},{10,1... | collective-permute-start | bytes 786440 | tf_op jit(solution)/shard_map/ppermute | solution.py:296
  151.4 26.7 %collective-permute-start.16 = (bf16[128,1024]{1,0:T(8,128)(2,1)}, bf16[128,1024]{1,0:T(8,128)(2,1)S(1)}, u32[]{:S(2)}, u32[]{:S(2)}) collective-permute-start(bf16[128,1024]{1,0:T(8,128)(2,1)} %get-tuple-element.236), channel_id=1, source_target_pairs={{0,2},{1,3},{2,0},{3,1},{4,6},{5,7},{6,4},{7,5},{8,10},{9,11},{10,... | collective-permute-start | bytes 786440 | tf_op jit(solution)/shard_map/ppermute | solution.py:296
  153.4 24.8 %collective-permute-start.17 = (bf16[128,1024]{1,0:T(8,128)(2,1)}, bf16[128,1024]{1,0:T(8,128)(2,1)S(1)}, u32[]{:S(2)}, u32[]{:S(2)}) collective-permute-start(bf16[128,1024]{1,0:T(8,128)(2,1)} %get-tuple-element.235), channel_id=1, source_target_pairs={{0,3},{1,0},{2,1},{3,2},{4,7},{5,4},{6,5},{7,6},{8,11},{9,8},{10,9... | collective-permute-start | bytes 786440 | tf_op jit(solution)/shard_map/ppermute | solution.py:296
  178.2 17.8 %all-to-all-start.1 = ((bf16[4,64,1024]{2,1,0:T(8,128)(2,1)}), bf16[4,64,1024]{2,1,0:T(8,128)(2,1)S(1)}, u32[]{:S(2)}, u32[]{:S(2)}) async-start(bf16[4,64,1024]{2,1,0:T(8,128)(2,1)} %get-tuple-element.52), calls=%async_computation.1 | async-start | bytes 1048576 | tf_op jit(solution)/shard_map/all_to_all | solution.py:286
  181.7 197.4 %all-gather.8.cloned.1.call-start = ((), (), s32[]{:S(2)}) async-start(), calls=%async_computation.17 | async-start | bytes 5242880 | tf_op jit(solution)/shard_map/all_gather | solution.py:329
  207.6 14.1 %collective-permute-start.19 = (bf16[256,1024]{1,0:T(8,128)(2,1)S(1)}, bf16[256,1024]{1,0:T(8,128)(2,1)S(1)}, u32[]{:S(2)}, u32[]{:S(2)}) collective-permute-start(bf16[256,1024]{1,0:T(8,128)(2,1)S(1)} %fusion.64), channel_id=1, source_target_pairs={{0,8},{8,0},{1,9},{9,1},{2,10},{10,2},{3,11},{11,3},{4,12},{12,4},... | collective-permute-start | bytes 1572872 | tf_op jit(solution)/shard_map/ppermute | solution.py:229
  223.6 15.0 %collective-permute-start.24 = (bf16[256,1024]{1,0:T(8,128)(2,1)S(1)}, bf16[256,1024]{1,0:T(8,128)(2,1)}, u32[]{:S(2)}, u32[]{:S(2)}) collective-permute-start(bf16[256,1024]{1,0:T(8,128)(2,1)S(1)} %fusion.61), channel_id=1, source_target_pairs={{0,8},{8,0},{1,9},{9,1},{2,10},{10,2},{3,11},{11,3},{4,12},{12,4},... | collective-permute-start | bytes 1572872 | tf_op jit(solution)/shard_map/ppermute | solution.py:229
  226.2 12.7 %collective-permute-start.31 = (bf16[512,256]{1,0:T(8,128)(2,1)}, bf16[512,256]{1,0:T(8,128)(2,1)}, u32[]{:S(2)}, u32[]{:S(2)}) collective-permute-start(bf16[512,256]{1,0:T(8,128)(2,1)} %get-tuple-element.241), channel_id=1, source_target_pairs={{0,4},{4,0},{1,5},{5,1},{2,6},{6,2},{3,7},{7,3},{8,12},{12,8},{9,1... | collective-permute-start | bytes 786440 | tf_op jit(solution)/shard_map/ppermute | solution.py:227
  226.2 18.0 %collective-permute-start.32 = (bf16[512,256]{1,0:T(8,128)(2,1)S(1)}, bf16[512,256]{1,0:T(8,128)(2,1)}, u32[]{:S(2)}, u32[]{:S(2)}) collective-permute-start(bf16[512,256]{1,0:T(8,128)(2,1)S(1)} %get-tuple-element.242), channel_id=1, source_target_pairs={{0,8},{8,0},{1,9},{9,1},{2,10},{10,2},{3,11},{11,3},{4,12},{12,4},... | collective-permute-start | bytes 786440 | tf_op jit(solution)/shard_map/ppermute | solution.py:229
  226.7 20.3 %collective-permute-start.33 = (bf16[512,256]{1,0:T(8,128)(2,1)S(1)}, bf16[512,256]{1,0:T(8,128)(2,1)}, u32[]{:S(2)}, u32[]{:S(2)}) collective-permute-start(bf16[512,256]{1,0:T(8,128)(2,1)S(1)} %get-tuple-element.239), channel_id=1, source_target_pairs={{0,12},{4,8},{8,4},{12,0},{1,13},{5,9},{9,5},{13,1},{2,14},{6,10},... | collective-permute-start | bytes 786440 | tf_op jit(solution)/shard_map/ppermute | solution.py:230
  228.0 21.6 %collective-permute-start.23 = (bf16[256,1024]{1,0:T(8,128)(2,1)S(1)}, bf16[256,1024]{1,0:T(8,128)(2,1)}, u32[]{:S(2)}, u32[]{:S(2)}) collective-permute-start(bf16[256,1024]{1,0:T(8,128)(2,1)S(1)} %fusion.61), channel_id=1, source_target_pairs={{0,4},{4,0},{1,5},{5,1},{2,6},{6,2},{3,7},{7,3},{8,12},{12,8},{9,1... | collective-permute-start | bytes 1572872 | tf_op jit(solution)/shard_map/ppermute | solution.py:227
  238.6 11.1 %collective-permute-start.25 = (bf16[256,1024]{1,0:T(8,128)(2,1)}, bf16[256,1024]{1,0:T(8,128)(2,1)}, u32[]{:S(2)}, u32[]{:S(2)}) collective-permute-start(bf16[256,1024]{1,0:T(8,128)(2,1)} %collective-permute-done.24), channel_id=1, source_target_pairs={{0,4},{4,0},{1,5},{5,1},{2,6},{6,2},{3,7},{7,3},{8,12},{12,8},{9,1... | collective-permute-start | bytes 1572872 | tf_op jit(solution)/shard_map/ppermute | solution.py:227
  249.6 392.4 %reduce-scatter.10.cloned.1.call-start = ((), (), s32[]{:S(2)}) async-start(), calls=%async_computation.19 | async-start | bytes 2621440 | tf_op jit(solution)/shard_map/reduce_scatter | solution.py:346
  350.8 14.1 %collective-permute-start.27 = (bf16[256,1024]{1,0:T(8,128)(2,1)S(1)}, bf16[256,1024]{1,0:T(8,128)(2,1)S(1)}, u32[]{:S(2)}, u32[]{:S(2)}) collective-permute-start(bf16[256,1024]{1,0:T(8,128)(2,1)S(1)} %fusion.50), channel_id=1, source_target_pairs={{0,8},{8,0},{1,9},{9,1},{2,10},{10,2},{3,11},{11,3},{4,12},{12,4},... | collective-permute-start | bytes 1572872 | tf_op jit(solution)/shard_map/ppermute | solution.py:229
  365.8 13.3 %collective-permute-start.29 = (bf16[256,1024]{1,0:T(8,128)(2,1)S(1)}, bf16[256,1024]{1,0:T(8,128)(2,1)S(1)}, u32[]{:S(2)}, u32[]{:S(2)}) collective-permute-start(bf16[256,1024]{1,0:T(8,128)(2,1)S(1)} %fusion.62), channel_id=1, source_target_pairs={{0,8},{8,0},{1,9},{9,1},{2,10},{10,2},{3,11},{11,3},{4,12},{12,4},... | collective-permute-start | bytes 1572872 | tf_op jit(solution)/shard_map/ppermute | solution.py:229
  366.8 15.2 %collective-permute-start.28 = (bf16[256,1024]{1,0:T(8,128)(2,1)S(1)}, bf16[256,1024]{1,0:T(8,128)(2,1)}, u32[]{:S(2)}, u32[]{:S(2)}) collective-permute-start(bf16[256,1024]{1,0:T(8,128)(2,1)S(1)} %fusion.62), channel_id=1, source_target_pairs={{0,4},{4,0},{1,5},{5,1},{2,6},{6,2},{3,7},{7,3},{8,12},{12,8},{9,1... | collective-permute-start | bytes 1572872 | tf_op jit(solution)/shard_map/ppermute | solution.py:227
  397.9 8.8 %collective-permute-start.34 = (bf16[2,256,1024]{2,1,0:T(8,128)(2,1)S(1)}, bf16[2,256,1024]{2,1,0:T(8,128)(2,1)S(1)}, u32[]{:S(2)}, u32[]{:S(2)}) collective-permute-start(bf16[2,256,1024]{2,1,0:T(8,128)(2,1)S(1)} %pad_maximum_fusion.8), channel_id=1, source_target_pairs={{0,4},{4,0},{1,5},{5,1},{2,6},{6,2},{3,7},{7,3},{8,12},{12,8},{9,1... | collective-permute-start | bytes 3145736 | tf_op jit(solution)/shard_map/ppermute | solution.py:227
  407.2 14.6 %collective-permute-start.35 = (bf16[256,1024]{1,0:T(8,128)(2,1)S(1)}, bf16[256,1024]{1,0:T(8,128)(2,1)S(1)}, u32[]{:S(2)}, u32[]{:S(2)}) collective-permute-start(bf16[256,1024]{1,0:T(8,128)(2,1)S(1)} %fusion.44), channel_id=1, source_target_pairs={{0,8},{8,0},{1,9},{9,1},{2,10},{10,2},{3,11},{11,3},{4,12},{12,4},... | collective-permute-start | bytes 1572872 | tf_op jit(solution)/shard_map/ppermute | solution.py:229
  424.0 13.6 %collective-permute-start.43 = (bf16[256,1024]{1,0:T(8,128)(2,1)S(1)}, bf16[256,1024]{1,0:T(8,128)(2,1)S(1)}, u32[]{:S(2)}, u32[]{:S(2)}) collective-permute-start(bf16[256,1024]{1,0:T(8,128)(2,1)S(1)} %get-tuple-element.189), channel_id=1, source_target_pairs={{0,8},{8,0},{1,9},{9,1},{2,10},{10,2},{3,11},{11,3},{4,12},{12,4},... | collective-permute-start | bytes 1572872 | tf_op jit(solution)/shard_map/ppermute | solution.py:229
  425.0 12.7 %collective-permute-start.42 = (bf16[256,1024]{1,0:T(8,128)(2,1)S(1)}, bf16[256,1024]{1,0:T(8,128)(2,1)S(1)}, u32[]{:S(2)}, u32[]{:S(2)}) collective-permute-start(bf16[256,1024]{1,0:T(8,128)(2,1)S(1)} %get-tuple-element.189), channel_id=1, source_target_pairs={{0,4},{4,0},{1,5},{5,1},{2,6},{6,2},{3,7},{7,3},{8,12},{12,8},{9,1... | collective-permute-start | bytes 1572872 | tf_op jit(solution)/shard_map/ppermute | solution.py:227
  453.9 14.3 %collective-permute-start.46 = (bf16[256,1024]{1,0:T(8,128)(2,1)}, bf16[256,1024]{1,0:T(8,128)(2,1)}, u32[]{:S(2)}, u32[]{:S(2)}) collective-permute-start(bf16[256,1024]{1,0:T(8,128)(2,1)} %fusion.39), channel_id=1, source_target_pairs={{0,8},{8,0},{1,9},{9,1},{2,10},{10,2},{3,11},{11,3},{4,12},{12,4},... | collective-permute-start | bytes 1572872 | tf_op jit(solution)/shard_map/ppermute | solution.py:229
  470.9 13.2 %collective-permute-start.48 = (bf16[256,1024]{1,0:T(8,128)(2,1)S(1)}, bf16[256,1024]{1,0:T(8,128)(2,1)S(1)}, u32[]{:S(2)}, u32[]{:S(2)}) collective-permute-start(bf16[256,1024]{1,0:T(8,128)(2,1)S(1)} %get-tuple-element.192), channel_id=1, source_target_pairs={{0,8},{8,0},{1,9},{9,1},{2,10},{10,2},{3,11},{11,3},{4,12},{12,4},... | collective-permute-start | bytes 1572872 | tf_op jit(solution)/shard_map/ppermute | solution.py:229
  471.9 12.2 %collective-permute-start.47 = (bf16[256,1024]{1,0:T(8,128)(2,1)S(1)}, bf16[256,1024]{1,0:T(8,128)(2,1)S(1)}, u32[]{:S(2)}, u32[]{:S(2)}) collective-permute-start(bf16[256,1024]{1,0:T(8,128)(2,1)S(1)} %get-tuple-element.192), channel_id=1, source_target_pairs={{0,4},{4,0},{1,5},{5,1},{2,6},{6,2},{3,7},{7,3},{8,12},{12,8},{9,1... | collective-permute-start | bytes 1572872 | tf_op jit(solution)/shard_map/ppermute | solution.py:227
  487.6 22.7 %all-to-all-start.4 = ((bf16[4,64,1024]{2,1,0:T(8,128)(2,1)}), bf16[4,64,1024]{2,1,0:T(8,128)(2,1)S(1)}, u32[]{:S(2)}, u32[]{:S(2)}) async-start(bf16[4,64,1024]{2,1,0:T(8,128)(2,1)} %bitcast.605), calls=%async_computation.4 | async-start | bytes 1048576 | tf_op jit(solution)/shard_map/all_to_all | solution.py:286
  559.3 18.5 %all-to-all-start.5 = ((bf16[4,64,1024]{2,1,0:T(8,128)(2,1)}), bf16[4,64,1024]{2,1,0:T(8,128)(2,1)S(1)}, u32[]{:S(2)}, u32[]{:S(2)}) async-start(bf16[4,64,1024]{2,1,0:T(8,128)(2,1)} %get-tuple-element.59), calls=%async_computation.5 | async-start | bytes 1048576 | tf_op jit(solution)/shard_map/all_to_all | solution.py:286
  562.8 81.4 %reduce-scatter.8.cloned.1.call-start = ((), (), s32[]{:S(2)}) async-start(), calls=%async_computation.18 | async-start | bytes 2621440 | tf_op jit(solution)/shard_map/reduce_scatter | solution.py:346
  568.8 79.3 %reduce-scatter.12.cloned.1.call-start = ((), (), s32[]{:S(2)}) async-start(), calls=%async_computation.20 | async-start | bytes 655360 | tf_op jit(solution)/shard_map/reduce_scatter | solution.py:346
  586.2 6.8 collective-permute-start.37
  587.7 21.3 %collective-permute-start.38 = (bf16[256,256]{1,0:T(8,128)(2,1)S(1)}, bf16[256,256]{1,0:T(8,128)(2,1)S(1)}, u32[]{:S(2)}, u32[]{:S(2)}) collective-permute-start(bf16[256,256]{1,0:T(8,128)(2,1)S(1)} %bitcast.630), channel_id=1, source_target_pairs={{0,12},{4,8},{8,4},{12,0},{1,13},{5,9},{9,5},{13,1},{2,14},{6,10},... | collective-permute-start | bytes 393224 | tf_op jit(solution)/shard_map/ppermute | solution.py:230
  589.4 16.3 %collective-permute-start.51 = (bf16[256,1024]{1,0:T(8,128)(2,1)S(1)}, bf16[256,1024]{1,0:T(8,128)(2,1)S(1)}, u32[]{:S(2)}, u32[]{:S(2)}) collective-permute-start(bf16[256,1024]{1,0:T(8,128)(2,1)S(1)} %fusion.34), channel_id=1, source_target_pairs={{0,8},{8,0},{1,9},{9,1},{2,10},{10,2},{3,11},{11,3},{4,12},{12,4},... | collective-permute-start | bytes 1572872 | tf_op jit(solution)/shard_map/ppermute | solution.py:229
  607.6 13.4 %collective-permute-start.53 = (bf16[256,1024]{1,0:T(8,128)(2,1)}, bf16[256,1024]{1,0:T(8,128)(2,1)}, u32[]{:S(2)}, u32[]{:S(2)}) collective-permute-start(bf16[256,1024]{1,0:T(8,128)(2,1)} %get-tuple-element.195), channel_id=1, source_target_pairs={{0,8},{8,0},{1,9},{9,1},{2,10},{10,2},{3,11},{11,3},{4,12},{12,4},... | collective-permute-start | bytes 1572872 | tf_op jit(solution)/shard_map/ppermute | solution.py:229
  609.7 12.7 %collective-permute-start.52 = (bf16[256,1024]{1,0:T(8,128)(2,1)}, bf16[256,1024]{1,0:T(8,128)(2,1)}, u32[]{:S(2)}, u32[]{:S(2)}) collective-permute-start(bf16[256,1024]{1,0:T(8,128)(2,1)} %get-tuple-element.195), channel_id=1, source_target_pairs={{0,4},{4,0},{1,5},{5,1},{2,6},{6,2},{3,7},{7,3},{8,12},{12,8},{9,1... | collective-permute-start | bytes 1572872 | tf_op jit(solution)/shard_map/ppermute | solution.py:227
  613.0 18.3 %collective-permute-start.61 = (bf16[128,1024]{1,0:T(8,128)(2,1)}, bf16[128,1024]{1,0:T(8,128)(2,1)}, u32[]{:S(2)}, u32[]{:S(2)}) collective-permute-start(bf16[128,1024]{1,0:T(8,128)(2,1)} %get-tuple-element.229), channel_id=1, source_target_pairs={{0,1},{1,2},{2,3},{3,0},{4,5},{5,6},{6,7},{7,4},{8,9},{9,10},{10,1... | collective-permute-start | bytes 786440 | tf_op jit(solution)/shard_map/ppermute | solution.py:296
  613.0 28.0 %collective-permute-start.62 = (bf16[128,1024]{1,0:T(8,128)(2,1)}, bf16[128,1024]{1,0:T(8,128)(2,1)}, u32[]{:S(2)}, u32[]{:S(2)}) collective-permute-start(bf16[128,1024]{1,0:T(8,128)(2,1)} %get-tuple-element.228), channel_id=1, source_target_pairs={{0,2},{1,3},{2,0},{3,1},{4,6},{5,7},{6,4},{7,5},{8,10},{9,11},{10,... | collective-permute-start | bytes 786440 | tf_op jit(solution)/shard_map/ppermute | solution.py:296
  615.1 26.9 %collective-permute-start.63 = (bf16[128,1024]{1,0:T(8,128)(2,1)}, bf16[128,1024]{1,0:T(8,128)(2,1)S(1)}, u32[]{:S(2)}, u32[]{:S(2)}) collective-permute-start(bf16[128,1024]{1,0:T(8,128)(2,1)} %get-tuple-element.227), channel_id=1, source_target_pairs={{0,3},{1,0},{2,1},{3,2},{4,7},{5,4},{6,5},{7,6},{8,11},{9,8},{10,9... | collective-permute-start | bytes 786440 | tf_op jit(solution)/shard_map/ppermute | solution.py:296
  627.6 31.8 %all-to-all-start.6 = ((bf16[4,64,1024]{2,1,0:T(8,128)(2,1)}), bf16[4,64,1024]{2,1,0:T(8,128)(2,1)S(1)}, u32[]{:S(2)}, u32[]{:S(2)}) async-start(bf16[4,64,1024]{2,1,0:T(8,128)(2,1)} %bitcast.604), calls=%async_computation.6 | async-start | bytes 1048576 | tf_op jit(solution)/shard_map/all_to_all | solution.py:286
  631.2 101.6 %reduce-scatter.14.cloned.1.call-start = ((), (), s32[]{:S(2)}) async-start(), calls=%async_computation.21 | async-start | bytes 655360 | tf_op jit(solution)/shard_map/reduce_scatter | solution.py:346
  659.4 89.1 %reduce-scatter.20.cloned.1.call-start = ((), (), s32[]{:S(2)}) async-start(), calls=%async_computation.24 | async-start | bytes 655360 | tf_op jit(solution)/shard_map/reduce_scatter | solution.py:346
  665.2 16.3 %collective-permute-start.64 = (bf16[2,1024,256]{2,1,0:T(8,128)(2,1)}, bf16[2,1024,256]{2,1,0:T(8,128)(2,1)}, u32[]{:S(2)}, u32[]{:S(2)}) collective-permute-start(bf16[2,1024,256]{2,1,0:T(8,128)(2,1)} %pad_maximum_fusion.12), channel_id=1, source_target_pairs={{0,4},{4,0},{1,5},{5,1},{2,6},{6,2},{3,7},{7,3},{8,12},{12,8},{9,1... | collective-permute-start | bytes 3145736 | tf_op jit(solution)/shard_map/ppermute | solution.py:227
  668.6 83.1 %reduce-scatter.18.cloned.1.call-start = ((), (), s32[]{:S(2)}) async-start(), calls=%async_computation.23 | async-start | bytes 1310720 | tf_op jit(solution)/shard_map/reduce_scatter | solution.py:346
  674.3 9.6 %collective-permute-start.55 = (bf16[576,256]{1,0:T(8,128)(2,1)}, bf16[576,256]{1,0:T(8,128)(2,1)}, u32[]{:S(2)}, u32[]{:S(2)}) collective-permute-start(bf16[576,256]{1,0:T(8,128)(2,1)} %pad_maximum_fusion.28), channel_id=1, source_target_pairs={{0,4},{4,0},{1,5},{5,1},{2,6},{6,2},{3,7},{7,3},{8,12},{12,8},{9,1... | collective-permute-start | bytes 884744 | tf_op jit(solution)/shard_map/ppermute | solution.py:227
  675.4 10.2 %collective-permute-start.56 = (bf16[576,256]{1,0:T(8,128)(2,1)}, bf16[576,256]{1,0:T(8,128)(2,1)}, u32[]{:S(2)}, u32[]{:S(2)}) collective-permute-start(bf16[576,256]{1,0:T(8,128)(2,1)} %pad_maximum_fusion.29), channel_id=1, source_target_pairs={{0,8},{8,0},{1,9},{9,1},{2,10},{10,2},{3,11},{11,3},{4,12},{12,4},... | collective-permute-start | bytes 884744 | tf_op jit(solution)/shard_map/ppermute | solution.py:229
  676.7 13.7 %collective-permute-start.57 = (bf16[576,256]{1,0:T(8,128)(2,1)}, bf16[576,256]{1,0:T(8,128)(2,1)}, u32[]{:S(2)}, u32[]{:S(2)}) collective-permute-start(bf16[576,256]{1,0:T(8,128)(2,1)} %pad_maximum_fusion.30), channel_id=1, source_target_pairs={{0,12},{4,8},{8,4},{12,0},{1,13},{5,9},{9,5},{13,1},{2,14},{6,10},... | collective-permute-start | bytes 884744 | tf_op jit(solution)/shard_map/ppermute | solution.py:230
  692.6 41.8 %collective-permute-start.58 = (bf16[4,576,256]{2,1,0:T(8,128)(2,1)}, bf16[4,576,256]{2,1,0:T(8,128)(2,1)}, u32[]{:S(2)}, u32[]{:S(2)}) collective-permute-start(bf16[4,576,256]{2,1,0:T(8,128)(2,1)} %pad_maximum_fusion.5), channel_id=1, source_target_pairs={{0,16},{16,0},{1,17},{17,1},{2,18},{18,2},{3,19},{19,3},{4,20},{20... | collective-permute-start | bytes 3538952 | tf_op jit(solution)/shard_map/ppermute | solution.py:359
  696.3 49.7 %collective-permute-start.65 = (bf16[1024,256]{1,0:T(8,128)(2,1)}, bf16[1024,256]{1,0:T(8,128)(2,1)}, u32[]{:S(2)}, u32[]{:S(2)}) collective-permute-start(bf16[1024,256]{1,0:T(8,128)(2,1)} %fusion.26), channel_id=1, source_target_pairs={{0,8},{8,0},{1,9},{9,1},{2,10},{10,2},{3,11},{11,3},{4,12},{12,4},... | collective-permute-start | bytes 1572872 | tf_op jit(solution)/shard_map/ppermute | solution.py:229
  740.2 53.2 %all-to-all-start.7 = ((bf16[4,192,1024]{2,1,0:T(8,128)(2,1)}), bf16[4,192,1024]{2,1,0:T(8,128)(2,1)}, u32[]{:S(2)}, u32[]{:S(2)}) async-start(bf16[4,192,1024]{2,1,0:T(8,128)(2,1)} %pad_maximum_fusion.4), calls=%async_computation.11 | async-start | bytes 3145728 | tf_op jit(solution)/shard_map/all_to_all | solution.py:286
  745.7 87.2 %reduce-scatter.16.cloned.1.call-start = ((), (), s32[]{:S(2)}) async-start(), calls=%async_computation.22 | async-start | bytes 1966080 | tf_op jit(solution)/shard_map/reduce_scatter | solution.py:346
  759.6 13.5 %collective-permute-start.82 = (f32[15,1024]{1,0:T(8,128)S(1)}, f32[15,1024]{1,0:T(8,128)S(1)}, u32[]{:S(2)}, u32[]{:S(2)}) collective-permute-start(f32[15,1024]{1,0:T(8,128)S(1)} %add.598), channel_id=1, source_target_pairs={{0,1},{1,0},{2,3},{3,2},{4,5},{5,4},{6,7},{7,6},{8,9},{9,8},{10,11... | collective-permute-start | bytes 184328 | tf_op jit(solution)/shard_map/ppermute | solution.py:262
  773.1 12.9 %collective-permute-start.83 = (f32[15,1024]{1,0:T(8,128)S(1)}, f32[15,1024]{1,0:T(8,128)S(1)}, u32[]{:S(2)}, u32[]{:S(2)}) collective-permute-start(f32[15,1024]{1,0:T(8,128)S(1)} %add.599), channel_id=1, source_target_pairs={{0,2},{1,3},{2,0},{3,1},{4,6},{5,7},{6,4},{7,5},{8,10},{9,11},{10,... | collective-permute-start | bytes 184328 | tf_op jit(solution)/shard_map/ppermute | solution.py:262
  787.5 18.4 %collective-permute-start.75 = (bf16[256,256]{1,0:T(8,128)(2,1)S(1)}, bf16[256,256]{1,0:T(8,128)(2,1)S(1)}, u32[]{:S(2)}, u32[]{:S(2)}) collective-permute-start(bf16[256,256]{1,0:T(8,128)(2,1)S(1)} %pad_maximum_fusion.32), channel_id=1, source_target_pairs={{0,4},{4,0},{1,5},{5,1},{2,6},{6,2},{3,7},{7,3},{8,12},{12,8},{9,1... | collective-permute-start | bytes 393224 | tf_op jit(solution)/shard_map/ppermute | solution.py:227
  788.9 16.9 %collective-permute-start.76 = (bf16[256,256]{1,0:T(8,128)(2,1)S(1)}, bf16[256,256]{1,0:T(8,128)(2,1)S(1)}, u32[]{:S(2)}, u32[]{:S(2)}) collective-permute-start(bf16[256,256]{1,0:T(8,128)(2,1)S(1)} %pad_maximum_fusion.33), channel_id=1, source_target_pairs={{0,8},{8,0},{1,9},{9,1},{2,10},{10,2},{3,11},{11,3},{4,12},{12,4},... | collective-permute-start | bytes 393224 | tf_op jit(solution)/shard_map/ppermute | solution.py:229
  798.5 7.3 collective-permute-start.77
  805.9 13.1 %collective-permute-start.78 = (bf16[4,256,256]{2,1,0:T(8,128)(2,1)S(1)}, bf16[4,256,256]{2,1,0:T(8,128)(2,1)S(1)}, u32[]{:S(2)}, u32[]{:S(2)}) collective-permute-start(bf16[4,256,256]{2,1,0:T(8,128)(2,1)S(1)} %pad_maximum_fusion.15), channel_id=1, source_target_pairs={{0,16},{16,0},{1,17},{17,1},{2,18},{18,2},{3,19},{19,3},{4,20},{20... | collective-permute-start | bytes 1572872 | tf_op jit(solution)/shard_map/ppermute | solution.py:359
  810.9 9.4 %collective-permute-start.59 = (bf16[2,1024,256]{2,1,0:T(8,128)(2,1)S(1)}, bf16[2,1024,256]{2,1,0:T(8,128)(2,1)S(1)}, u32[]{:S(2)}, u32[]{:S(2)}) collective-permute-start(bf16[2,1024,256]{2,1,0:T(8,128)(2,1)S(1)} %pad_maximum_fusion.11), channel_id=1, source_target_pairs={{0,4},{4,0},{1,5},{5,1},{2,6},{6,2},{3,7},{7,3},{8,12},{12,8},{9,1... | collective-permute-start | bytes 3145736 | tf_op jit(solution)/shard_map/ppermute | solution.py:227
  821.4 25.3 %collective-permute-start.60 = (bf16[1024,256]{1,0:T(8,128)(2,1)}, bf16[1024,256]{1,0:T(8,128)(2,1)}, u32[]{:S(2)}, u32[]{:S(2)}) collective-permute-start(bf16[1024,256]{1,0:T(8,128)(2,1)} %fusion.30), channel_id=1, source_target_pairs={{0,8},{8,0},{1,9},{9,1},{2,10},{10,2},{3,11},{11,3},{4,12},{12,4},... | collective-permute-start | bytes 1572872 | tf_op jit(solution)/shard_map/ppermute | solution.py:229
  842.6 11.6 %collective-permute-start.69 = (bf16[4,192,256]{2,1,0:T(8,128)(2,1)}, bf16[4,192,256]{2,1,0:T(8,128)(2,1)}, u32[]{:S(2)}, u32[]{:S(2)}) collective-permute-start(bf16[4,192,256]{2,1,0:T(8,128)(2,1)} %pad_maximum_fusion.17), channel_id=1, source_target_pairs={{0,16},{16,0},{1,17},{17,1},{2,18},{18,2},{3,19},{19,3},{4,20},{20... | collective-permute-start | bytes 1179656 | tf_op jit(solution)/shard_map/ppermute | solution.py:359
  (98 other events, 685.8 us)
Sparse Core Ops, SparseCore 0:
  18.5 38.9 all-gather.3
  59.6 85.3 all-gather.5
  249.7 100.5 all-gather.7
  458.7 44.7 reduce-scatter.9
  568.9 44.9 reduce-scatter.7
  616.9 31.1 reduce-scatter.11
  659.5 22.7 reduce-scatter.13
  684.6 20.0 reduce-scatter.19
  707.6 25.5 reduce-scatter.17
  798.6 34.2 reduce-scatter.15
